TPU v7x, 128 devices: a whole 4x4x4 slice. The times are simulated.
128 devices in a mesh: row: 4 (over z), col: 8 (over y, core), seq: 4 (over x).
Axes of the slice: x: 4, y: 4, z: 4, core: 2. Of those that a mesh axis runs over, the one named last changes fastest.
Arguments:
- motion_ids: int32 [1536], P('col'), may hold values from 0 to 511
- audio_ids: int32 [1536], P('col'), may hold values from 0 to 1023
- segment_ids: int32 [1536], replicated, may hold values from 0 to 3, never falling along the last dimension, each value on 1 to 768 neighbouring positions
- motion_table: bfloat16 [512, 8192], P(None, ('row', 'seq')), may hold values from -40 to 40
- audio_table: bfloat16 [1024, 8192], P(None, ('row', 'seq')), may hold values from -40 to 40
- norm_gain: float32 [8192], P(('row', 'seq')), may hold values from 0.5 to 1.5
- w_query: bfloat16 [8192, 8192], P(('row', 'seq'), 'col'), may hold values from -0.1875 to 0.1875
- w_key: bfloat16 [8192, 1024], P(('row', 'seq'), 'col'), may hold values from -0.0625 to 0.0625
- w_value: bfloat16 [8192, 1024], P(('row', 'seq'), 'col'), may hold values from -0.0625 to 0.0625
- w_out: bfloat16 [8192, 8192], P('col', ('row', 'seq')), may hold values from -0.0625 to 0.0625
- out_grad: bfloat16 [1536, 8192], P('col', ('row', 'seq')), may hold values from -6 to 6
Outputs:
- layer_out: bfloat16 [1536, 8192], P('col', ('row', 'seq'))
- grad_input: bfloat16 [1536, 8192], P('col', ('row', 'seq'))
- grad_gain: float32 [8192], P(('row', 'seq'))
- grad_wq: float32 [8192, 8192], P(('row', 'seq'), 'col')
- grad_wk: float32 [8192, 1024], P(('row', 'seq'), 'col')
- grad_wv: float32 [8192, 1024], P(('row', 'seq'), 'col')
- grad_wo: float32 [8192, 8192], P('col', ('row', 'seq'))
Inputs may be any that keep to these rules, and one draw needn't show every extreme that they name: `segment_ids`: document ids never fall along the sequence; no document is longer than 768 positions, and one is exactly that long.
All inputs are finite; a program needn't handle non-finite values.
Results may differ from a plain program's by a relative error of at most 0.023.
Values may be sent and summed in bfloat16 or wider, within the bound.
No kernel may reach another device: no remote copies, remote signals or barrier semaphores. Data moves between devices by JAX's collectives and lax.ppermute only.
A program may use at most 128 MiB of HBM per device.

v0:
```python
import jax
import jax.numpy as jnp
from jax import lax
from jax.sharding import PartitionSpec as P

D = 8192
H = 64
KV = 8
HD = 128


epsilon = 1e-05
softcap = 20.0
rope_base = 500000.0


def rotary_tables(positions, head_size):
    half_size = head_size // 2
    frequency = rope_base ** (-(jnp.arange(half_size, dtype=jnp.float32) * 2.0) / head_size)
    angles = positions.astype(jnp.float32)[:, None] * frequency[None, :]
    return (jnp.cos(angles), jnp.sin(angles))


def rotate_pairs(values, cosines, sines):
    half_size = values.shape[-1] // 2
    first_half = values[..., :half_size]
    second_half = values[..., half_size:]
    cos_part = cosines[:, None, :]
    sin_part = sines[:, None, :]
    return jnp.concatenate(
        [
            first_half * cos_part - second_half * sin_part,
            second_half * cos_part + first_half * sin_part,
        ],
        axis=-1,
    )


def rotate_back(values, cosines, sines):
    half_size = values.shape[-1] // 2
    first_half = values[..., :half_size]
    second_half = values[..., half_size:]
    cos_part = cosines[:, None, :]
    sin_part = sines[:, None, :]
    return jnp.concatenate(
        [
            first_half * cos_part + second_half * sin_part,
            second_half * cos_part - first_half * sin_part,
        ],
        axis=-1,
    )


def rope_round(values, positions):
    cosines, sines = rotary_tables(positions, HD)
    row_total = values.shape[0]
    return (
        rotate_pairs(values.reshape(row_total, -1, HD), cosines, sines)
        .reshape(row_total, -1)
        .astype(jnp.bfloat16)
    )


def plain_round(values, positions):
    return values.astype(jnp.bfloat16)


def per_device(
    motion_ids,
    audio_ids,
    segment_ids,
    motion_table,
    audio_table,
    norm_gain,
    w_query,
    w_key,
    w_value,
    w_out,
    out_grad,
):
    seq_len = segment_ids.shape[0]
    row_devices = lax.axis_size("row")
    seq_devices = lax.axis_size("seq")
    row_index = lax.axis_index("row")
    seq_index = lax.axis_index("seq")
    col_index = lax.axis_index("col")
    block_len = seq_len // (row_devices * seq_devices)
    quarter_len = seq_len // row_devices
    query_width = w_query.shape[1]
    kv_width = w_key.shape[1]
    heads_col = query_width // HD
    kv_col = kv_width // HD
    group_size = H // KV
    score_scale = HD ** (-0.5)
    block_pos = (row_index * seq_devices + seq_index) * block_len + jnp.arange(
        block_len, dtype=jnp.int32
    )
    embedded = (
        jnp.take(motion_table, motion_ids, axis=0).astype(jnp.float32)
        + jnp.take(audio_table, audio_ids, axis=0).astype(jnp.float32)
    ).astype(jnp.bfloat16)
    residual = embedded.astype(jnp.float32)
    squares = lax.psum(jnp.sum(residual * residual, axis=1), ("row", "seq"))
    inverse = lax.rsqrt(squares / D + epsilon)
    normed = (residual * inverse[:, None] * norm_gain[None, :]).astype(jnp.bfloat16)
    normed_all = lax.all_gather(normed, "col", axis=0, tiled=True)
    query_pos = row_index * quarter_len + jnp.arange(quarter_len, dtype=jnp.int32)
    head_first = col_index * heads_col + seq_index * (heads_col // seq_devices)
    head_count = heads_col // seq_devices

    def to_heads(term, finish):
        own_share = lax.psum_scatter(
            term(jnp.int32(0), block_len * lax.axis_size(("row", "seq"))),
            ("row", "seq"),
            scatter_dimension=0,
            tiled=True,
        )
        return lax.all_to_all(
            finish(own_share, block_pos), "seq", split_axis=1, concat_axis=0, tiled=True
        )

    def to_rows(heads_part):
        own_share = lax.all_to_all(heads_part, "seq", split_axis=0, concat_axis=1, tiled=True)
        return lax.all_gather(own_share, ("row", "seq"), axis=0, tiled=True)

    def query_term(first_row, row_count):
        return jnp.dot(normed_all, w_query, preferred_element_type=jnp.float32)

    queries = to_heads(query_term, rope_round)
    picked = normed_all
    kv_sum = lax.psum_scatter(
        jnp.concatenate(
            [
                jnp.dot(picked, w_key, preferred_element_type=jnp.float32),
                jnp.dot(picked, w_value, preferred_element_type=jnp.float32),
            ],
            axis=1,
        ),
        ("row", "seq"),
        scatter_dimension=0,
        tiled=True,
    )
    kv_block = jnp.concatenate(
        [rope_round(kv_sum[:, :kv_width], block_pos), kv_sum[:, kv_width:].astype(jnp.bfloat16)],
        axis=1,
    )
    kv_all = lax.all_gather(kv_block, ("row", "seq"), axis=0, tiled=True)
    query_len = queries.shape[0]
    kv_slot = (
        head_first + jnp.arange(head_count, dtype=jnp.int32)
    ) // group_size - col_index * kv_col
    key_sel = jnp.take(kv_all[:, :kv_width].reshape(seq_len, kv_col, HD), kv_slot, axis=1)
    value_sel = jnp.take(kv_all[:, kv_width:].reshape(seq_len, kv_col, HD), kv_slot, axis=1)
    key_pos = jnp.arange(seq_len, dtype=jnp.int32)
    allowed = (key_pos[None, :] <= query_pos[:, None]) & (
        segment_ids[None, :] == jnp.take(segment_ids, query_pos)[:, None]
    )
    query_heads = queries.reshape(query_len, head_count, HD)
    raw_scores = (
        jnp.einsum("qhd,khd->hqk", query_heads, key_sel, preferred_element_type=jnp.float32)
        * score_scale
    )
    capped = softcap * jnp.tanh(raw_scores / softcap)
    weights = jnp.where(allowed[None], jnp.exp(capped), 0.0)
    totals = jnp.sum(weights, axis=2)
    attended = jnp.einsum(
        "hqk,khd->qhd", weights.astype(jnp.bfloat16), value_sel, preferred_element_type=jnp.float32
    )
    attn_out = (
        (attended / totals.T[:, :, None]).astype(jnp.bfloat16).reshape(query_len, head_count * HD)
    )
    out_all = to_rows(attn_out)
    picked = out_all
    branch_sum = lax.psum_scatter(
        jnp.dot(picked, w_out, preferred_element_type=jnp.float32).astype(jnp.bfloat16),
        "col",
        scatter_dimension=0,
        tiled=True,
    ).astype(jnp.float32)
    layer_out = (residual + branch_sum).astype(jnp.bfloat16)
    grad_all = lax.all_gather(out_grad, "col", axis=0, tiled=True)
    grad_wo = jnp.einsum("ln,ld->nd", out_all, grad_all, preferred_element_type=jnp.float32)

    def dout_term(first_row, row_count):
        return jnp.einsum("ld,nd->ln", grad_all, w_out, preferred_element_type=jnp.float32)

    out_heads = to_heads(dout_term, plain_round).reshape(query_len, head_count, HD)
    attn_probs = weights / totals[:, :, None]
    prob_grads = jnp.einsum(
        "qhd,khd->hqk", out_heads, value_sel, preferred_element_type=jnp.float32
    )
    row_dots = jnp.sum(attn_probs * prob_grads, axis=2, keepdims=True)
    grad_scores = (
        attn_probs * (prob_grads - row_dots) * (1.0 - (capped / softcap) ** 2) * score_scale
    ).astype(jnp.bfloat16)
    grad_query = jnp.einsum(
        "hqk,khd->qhd", grad_scores, key_sel, preferred_element_type=jnp.float32
    )
    grad_key_heads = jnp.einsum(
        "hqk,qhd->khd", grad_scores, query_heads, preferred_element_type=jnp.float32
    )
    grad_value_heads = jnp.einsum(
        "hqk,qhd->khd",
        attn_probs.astype(jnp.bfloat16),
        out_heads,
        preferred_element_type=jnp.float32,
    )
    slot_mask = (kv_slot[:, None] == jnp.arange(kv_col, dtype=jnp.int32)[None, :]).astype(
        jnp.float32
    )
    grad_key_part = jnp.sum(
        grad_key_heads[:, :, None, :] * slot_mask[None, :, :, None], axis=1
    ).reshape(seq_len, kv_width)
    grad_value_part = jnp.sum(
        grad_value_heads[:, :, None, :] * slot_mask[None, :, :, None], axis=1
    ).reshape(seq_len, kv_width)
    kv_grad_sum = lax.psum_scatter(
        jnp.concatenate([grad_key_part, grad_value_part], axis=1).astype(jnp.bfloat16),
        ("row", "seq"),
        scatter_dimension=0,
        tiled=True,
    ).astype(jnp.float32)
    cos_block, sin_block = rotary_tables(block_pos, HD)
    grad_key_block = (
        rotate_back(kv_grad_sum[:, :kv_width].reshape(block_len, kv_col, HD), cos_block, sin_block)
        .reshape(block_len, kv_width)
        .astype(jnp.bfloat16)
    )
    kv_grad_block = jnp.concatenate(
        [grad_key_block, kv_grad_sum[:, kv_width:].astype(jnp.bfloat16)], axis=1
    )
    kv_grad_all = lax.all_gather(kv_grad_block, ("row", "seq"), axis=0, tiled=True)
    cos_query, sin_query = rotary_tables(query_pos, HD)
    grad_query_round = (
        rotate_back(grad_query, cos_query, sin_query)
        .reshape(query_len, head_count * HD)
        .astype(jnp.bfloat16)
    )
    grad_query_all = to_rows(grad_query_round)
    grad_wq = jnp.einsum(
        "ld,ln->dn", normed_all, grad_query_all, preferred_element_type=jnp.float32
    )
    grad_wk = jnp.einsum(
        "ld,ln->dn", normed_all, kv_grad_all[:, :kv_width], preferred_element_type=jnp.float32
    )
    grad_wv = jnp.einsum(
        "ld,ln->dn", normed_all, kv_grad_all[:, kv_width:], preferred_element_type=jnp.float32
    )
    total_term = jnp.einsum(
        "ln,dn->ld", grad_query_all, w_query, preferred_element_type=jnp.float32
    )
    total_term = total_term + jnp.einsum(
        "ln,dn->ld", kv_grad_all[:, :kv_width], w_key, preferred_element_type=jnp.float32
    )
    grad_normed = lax.psum_scatter(
        (
            total_term
            + jnp.einsum(
                "ln,dn->ld", kv_grad_all[:, kv_width:], w_value, preferred_element_type=jnp.float32
            )
        ).astype(jnp.bfloat16),
        "col",
        scatter_dimension=0,
        tiled=True,
    ).astype(jnp.float32)
    scaled_grad = grad_normed * norm_gain[None, :]
    total_dot = lax.psum(jnp.sum(scaled_grad * residual, axis=1), ("row", "seq"))
    grad_input = (
        out_grad.astype(jnp.float32)
        + inverse[:, None] * scaled_grad
        - residual * (inverse**3 * total_dot / D)[:, None]
    ).astype(jnp.bfloat16)
    grad_gain = lax.psum(jnp.sum(grad_normed * residual * inverse[:, None], axis=0), "col")
    return (layer_out, grad_input, grad_gain, grad_wq, grad_wk, grad_wv, grad_wo)


def solution(mesh):
    placed = (
        P("col"),
        P("col"),
        P(),
        P(None, ("row", "seq")),
        P(None, ("row", "seq")),
        P(("row", "seq")),
        P(("row", "seq"), "col"),
        P(("row", "seq"), "col"),
        P(("row", "seq"), "col"),
        P("col", ("row", "seq")),
        P("col", ("row", "seq")),
    )
    return jax.shard_map(
        per_device,
        mesh=mesh,
        in_specs=placed,
        out_specs=(
            P("col", ("row", "seq")),
            P("col", ("row", "seq")),
            P(("row", "seq")),
            P(("row", "seq"), "col"),
            P(("row", "seq"), "col"),
            P(("row", "seq"), "col"),
            P("col", ("row", "seq")),
        ),
        check_vma=False,
    )
```

profile of v0, /device:TPU:0, one launch (start us, length us, event | category | flops | bytes accessed | tf_op | source)
XLA Modules:
  0.0 664.8 jit_solution(8972401229715174517)
XLA Ops:
  7.2 0.8 compare_select_fusion.3
  8.0 0.7 compare_and_fusion.1
  9.4 2.2 gather_fusion
  11.6 2.4 gather_fusion.1
  14.3 41.8 %psum.21 = f32[192]{0:T(256)S(1)} all-reduce(f32[192]{0:T(256)S(1)} %get-tuple-element.10), channel_id=1, replica_groups=mesh['row'=4,'col'=8,'seq'=4] {'row','seq'}, use_global_device_ids=true, to_apply=%region_1.2 | all-reduce | flops 192 | bytes 1536 | tf_op jit(solution)/shard_map/psum | solution.py:103
  56.1 1.5 fusion.53
  58.4 20.1 %all-gather.5.cloned.1.call-done = bf16[1536,512]{1,0:T(8,128)(2,1)} async-done(((bf16[192,512]{1,0:T(8,128)(2,1)}), bf16[1536,512]{1,0:T(8,128)(2,1)}) %all-gather.5.cloned.1.call-update) | async-done | bytes 1572880 | tf_op jit(solution)/shard_map/all_gather | solution.py:106
  78.5 2.1 fusion.110
  80.5 2.2 fusion.111
  82.7 1.3 pad_maximum_fusion
  84.0 3.0 copy.65
  87.1 4.4 fusion.112
  91.6 13.0 %all-gather.9.cloned.1.call-done = bf16[1536,512]{1,0:T(8,128)(2,1)} async-done(((bf16[192,512]{1,0:T(8,128)(2,1)}), bf16[1536,512]{1,0:T(8,128)(2,1)}) %all-gather.9.cloned.1.call-update) | async-done | bytes 1572880 | tf_op jit(solution)/shard_map/all_gather | solution.py:181
  104.7 6.2 fusion.113
  111.5 2.5 gather_fusion.2
  115.4 1.4 fusion.8
  116.8 66.5 %reduce-scatter.19.cloned.1.call-done = f32[96,256]{1,0:T(8,128)} async-done(((f32[1536,256]{1,0:T(8,128)}), f32[96,256]{1,0:T(8,128)}) %reduce-scatter.19.cloned.1.call-update) | async-done | bytes 98320
  183.4 0.8 slice.75
  184.3 0.8 slice.78
  185.5 0.7 copy.48
  186.2 81.5 %reduce-scatter.11.cloned.1.call-done = f32[96,1024]{1,0:T(8,128)} async-done(((f32[1536,1024]{1,0:T(8,128)}), f32[96,1024]{1,0:T(8,128)}) %reduce-scatter.11.cloned.1.call-update) | async-done | bytes 393232 | tf_op jit(solution)/shard_map/reduce_scatter | solution.py:112
  267.7 1.1 copy.76
  270.0 4.0 all-to-all-start
  274.0 25.8 %all_gather.19 = bf16[1536,256]{1,0:T(8,128)(2,1)S(1)} all-gather(bf16[96,256]{1,0:T(8,128)(2,1)} %copy.48), channel_id=1, replica_groups=mesh['row'=4,'col'=8,'seq'=4] {'row','seq'}, dimensions={0}, use_global_device_ids=true | all-gather | bytes 835584 | tf_op jit(solution)/shard_map/all_gather | solution.py:147
  299.8 53.3 %reduce-scatter.15.cloned.1.call-done = f32[96,1024]{1,0:T(8,128)} async-done(((f32[1536,1024]{1,0:T(8,128)}), f32[96,1024]{1,0:T(8,128)}) %reduce-scatter.15.cloned.1.call-update) | async-done | bytes 393232 | tf_op jit(solution)/shard_map/reduce_scatter | solution.py:112
  353.1 1.0 convert_element_type.112
  354.8 4.0 all-to-all-start.2
  359.0 0.9 fusion.108
  359.9 1.9 copy.50
  361.9 1.0 reshape.357
  362.9 0.8 copy.60
  363.7 1.5 all-to-all-done.2
  365.2 1.0 reshape.359
  366.4 4.1 fusion.30
  370.5 2.6 fusion.20
  373.8 1.6 copy-done.19
  375.3 2.8 fusion.14
  378.1 12.9 %fusion.17 = bf16[128,1536]{1,0:T(8,128)(2,1)} fusion(bf16[384,2,128]{0,2,1:T(8,128)(2,1)} %copy.60, f32[2,384,1536]{2,1,0:T(8,128)} %fusion.30, f32[2,384,1536]{2,1,0:T(8,128)} %copy-done.19, f32[2]{0:T(128)} %compare_convert_fusion, f32[2,384]{1,0:T(2,128)} %copy-done.18, pred[384,1536]{1,0:T(8,128)(4,1)S(1)} %copy-done.7), kind=kOutput, calls=%fused_computation.24 | convolution fusion | flops 321456384 | bytes 10619912 | tf_op jit(solution)/shard_map/hqk,qhd->khd/dot_general | solution.py:199
  391.0 1.2 pad_maximum_fusion.1
  392.2 1.2 copy.67
  393.6 1.1 multiply_cosine_fusion
  394.7 10.8 %fusion.21 = f32[384,2,128]{0,2,1:T(8,128)S(1)} fusion(f32[2,384,1536]{2,1,0:T(8,128)} %fusion.30, f32[2,384,1536]{2,1,0:T(8,128)} %copy-done.19, pred[2]{0:T(512)(128)(4,1)} %compare_and_fusion, bf16[1536,128]{0,1:T(8,128)(2,1)} %copy.50, f32[2,384]{1,0:T(2,128)} %copy-done.18, pred[384,1536]{1,0:T(8,128)(4,1)} %fusion.8), kind=kOutput, calls=%fused_computation.26 | convolution fusion | flops 321259776 | bytes 10816514 | tf_op jit(solution)/shard_map/hqk,khd->qhd/dot_general | solution.py:196
  405.5 1.0 add_convert_fusion.2
  406.9 9.2 %all_to_all.64 = bf16[4,96,256]{2,1,0:T(8,128)(2,1)S(1)} all-to-all(bf16[4,96,256]{2,1,0:T(8,128)(2,1)S(1)} %convert_element_type.115), channel_id=1, replica_groups=mesh['row'=4,'col'=8,'seq'=4] {'seq'}, dimensions={0} | all-to-all | bytes 393216 | tf_op jit(solution)/shard_map/all_to_all | solution.py:123
  416.9 4.3 fusion.38
  421.5 8.7 %all_to_all.65 = bf16[4,96,256]{2,1,0:T(8,128)(2,1)S(1)} all-to-all(bf16[4,96,256]{2,1,0:T(8,128)(2,1)S(1)} %all_to_all.50), channel_id=1, replica_groups=mesh['row'=4,'col'=8,'seq'=4] {'seq'}, dimensions={0} | all-to-all | bytes 393216 | tf_op jit(solution)/shard_map/all_to_all | solution.py:123
  431.0 36.0 %reduce-scatter.21.cloned.1.call-done = bf16[96,256]{1,0:T(8,128)(2,1)} async-done(((bf16[1536,256]{1,0:T(8,128)(2,1)}), bf16[96,256]{1,0:T(8,128)(2,1)}) %reduce-scatter.21.cloned.1.call-update) | async-done | bytes 49168
  467.0 0.8 fusion.109
  468.3 0.7 copy.62
  469.0 24.3 %all_gather.23 = bf16[1536,256]{1,0:T(8,128)(2,1)S(1)} all-gather(bf16[96,256]{1,0:T(8,128)(2,1)} %copy.62), channel_id=1, replica_groups=mesh['row'=4,'col'=8,'seq'=4] {'row','seq'}, dimensions={0}, use_global_device_ids=true | all-gather | bytes 835584 | tf_op jit(solution)/shard_map/all_gather | solution.py:232
  493.2 24.7 %all-gather.11.cloned.1.call-done = bf16[1536,1024]{1,0:T(8,128)(2,1)} async-done(((bf16[96,1024]{1,0:T(8,128)(2,1)}), bf16[1536,1024]{1,0:T(8,128)(2,1)}) %all-gather.11.cloned.1.call-update) | async-done | bytes 3145744 | tf_op jit(solution)/shard_map/all_gather | solution.py:124
  518.0 3.8 fusion.114
  522.3 1.7 fusion.4
  524.4 42.9 %all-gather.7.cloned.1.call-done = bf16[1536,1024]{1,0:T(8,128)(2,1)} async-done(((bf16[96,1024]{1,0:T(8,128)(2,1)}), bf16[1536,1024]{1,0:T(8,128)(2,1)}) %all-gather.7.cloned.1.call-update) | async-done | bytes 3145744 | tf_op jit(solution)/shard_map/all_gather | solution.py:124
  567.3 5.2 convolution_convert_fusion
  572.5 1.3 fusion.66
  573.9 1.3 fusion.69
  575.2 3.1 fusion.116
  578.3 3.2 fusion.115
  581.5 19.9 %reduce-scatter.17.cloned.1.call-done = bf16[192,512]{1,0:T(8,128)(2,1)} async-done(((bf16[1536,512]{1,0:T(8,128)(2,1)}), bf16[192,512]{1,0:T(8,128)(2,1)}) %reduce-scatter.17.cloned.1.call-update) | async-done | bytes 196624 | tf_op jit(solution)/shard_map/reduce_scatter | solution.py:255
  601.4 1.1 fusion.57
  602.5 40.5 %psum.22 = f32[192]{0:T(256)S(1)} all-reduce(f32[192]{0:T(256)S(1)} %get-tuple-element.9), channel_id=1, replica_groups=mesh['row'=4,'col'=8,'seq'=4] {'row','seq'}, use_global_device_ids=true, to_apply=%region_13.15 | all-reduce | flops 192 | bytes 1536 | tf_op jit(solution)/shard_map/psum | solution.py:267
  643.0 13.0 %psum.23 = f32[512]{0:T(512)} all-reduce(f32[512]{0:T(512)S(1)} %get-tuple-element.8), channel_id=1, replica_groups=mesh['row'=4,'col'=8,'seq'=4] {'col'}, use_global_device_ids=true, to_apply=%region_15.17 | all-reduce | flops 512 | bytes 4096 | tf_op jit(solution)/shard_map/psum | solution.py:273
  656.0 2.0 fusion.50
  (101 shorter events, 11.1 us)
Async XLA Ops:
  7.2 79.9 %copy-start = (bf16[512,1024]{1,0:T(8,128)(2,1)S(1)}, bf16[512,1024]{1,0:T(8,128)(2,1)}, u32[]{:S(2)}) copy-start(bf16[512,1024]{1,0:T(8,128)(2,1)} %param.19) | copy-start | bytes 3145732
  7.2 71.3 %copy-start.9 = (bf16[512,128]{1,0:T(8,128)(2,1)S(1)}, bf16[512,128]{1,0:T(8,128)(2,1)}, u32[]{:S(2)}) copy-start(bf16[512,128]{1,0:T(8,128)(2,1)} %param.20) | copy-start | bytes 393220
  7.2 73.3 %copy-start.8 = (bf16[512,128]{1,0:T(8,128)(2,1)S(1)}, bf16[512,128]{1,0:T(8,128)(2,1)}, u32[]{:S(2)}) copy-start(bf16[512,128]{1,0:T(8,128)(2,1)} %param.21) | copy-start | bytes 393220
  7.2 71.3 %all-gather.5.cloned.1.call-start = ((), (), s32[]{:S(2)}) async-start(), calls=%async_computation.10 | async-start | bytes 1769472 | tf_op jit(solution)/shard_map/all_gather | solution.py:106
  14.3 64.2 %copy-start.3 = (bf16[192,512]{1,0:T(8,128)(2,1)}, bf16[192,512]{1,0:T(8,128)(2,1)S(1)}, u32[]{:S(2)}) copy-start(bf16[192,512]{1,0:T(8,128)(2,1)S(1)} %get-tuple-element.11) | copy-start | bytes 589828
  57.6 47.1 %all-gather.9.cloned.1.call-start = ((), (), s32[]{:S(2)}) async-start(), calls=%async_computation.14 | async-start | bytes 1769472 | tf_op jit(solution)/shard_map/all_gather | solution.py:181
  58.3 125.0 %reduce-scatter.19.cloned.1.call-start = ((), (), s32[]{:S(2)}) async-start(), calls=%async_computation.18 | async-start | bytes 1671168
  80.5 6.5 copy-start.2
  87.0 180.7 %reduce-scatter.11.cloned.1.call-start = ((), (), s32[]{:S(2)}) async-start(), calls=%async_computation.11 | async-start | bytes 6684672 | tf_op jit(solution)/shard_map/reduce_scatter | solution.py:112
  91.6 261.5 %reduce-scatter.15.cloned.1.call-start = ((), (), s32[]{:S(2)}) async-start(), calls=%async_computation.15 | async-start | bytes 6684672 | tf_op jit(solution)/shard_map/reduce_scatter | solution.py:112
  110.8 0.7 copy-start.1
  270.0 84.8 %all-to-all-start = ((bf16[96,4,256]{2,0,1:T(8,128)(2,1)}), bf16[96,4,256]{2,0,1:T(8,128)(2,1)}, u32[]{:S(2)}, u32[]{:S(2)}) async-start(bf16[96,4,256]{2,0,1:T(8,128)(2,1)} %copy.49), calls=%async_computation.1 | async-start | bytes 393216 | tf_op jit(solution)/shard_map/all_to_all | solution.py:118
  354.8 10.4 %all-to-all-start.2 = ((bf16[96,4,256]{2,0,1:T(8,128)(2,1)}), bf16[96,4,256]{2,0,1:T(8,128)(2,1)}, u32[]{:S(2)}, u32[]{:S(2)}) async-start(bf16[96,4,256]{2,0,1:T(8,128)(2,1)} %bitcast.68), calls=%async_computation.5 | async-start | bytes 393216 | tf_op jit(solution)/shard_map/all_to_all | solution.py:118
  358.8 108.2 %reduce-scatter.21.cloned.1.call-start = ((), (), s32[]{:S(2)}) async-start(), calls=%async_computation.19 | async-start | bytes 835584
  366.3 4.2 copy-start.7
  366.3 4.2 copy-start.11
  366.4 4.2 copy-start.12
  370.5 4.8 copy-start.17
  373.2 0.6 copy-start.18
  373.2 2.1 copy-start.19
  393.3 124.6 %all-gather.11.cloned.1.call-start = ((), (), s32[]{:S(2)}) async-start(), calls=%async_computation.16 | async-start | bytes 3342336 | tf_op jit(solution)/shard_map/all_gather | solution.py:124
  394.7 22.2 %copy-start.5 = (bf16[1536,128]{1,0:T(8,128)(2,1)S(1)}, bf16[1536,128]{1,0:T(8,128)(2,1)}, u32[]{:S(2)}) copy-start(bf16[1536,128]{1,0:T(8,128)(2,1)} %get-tuple-element.12) | copy-start | bytes 1179652
  416.8 150.4 %all-gather.7.cloned.1.call-start = ((), (), s32[]{:S(2)}) async-start(), calls=%async_computation.12 | async-start | bytes 3342336 | tf_op jit(solution)/shard_map/all_gather | solution.py:124
  430.9 170.4 %reduce-scatter.17.cloned.1.call-start = ((), (), s32[]{:S(2)}) async-start(), calls=%async_computation.17 | async-start | bytes 1769472 | tf_op jit(solution)/shard_map/reduce_scatter | solution.py:255
  518.0 3.8 copy-start.10
  524.1 131.9 %reduce-scatter.13.cloned.1.call-start = ((), (), s32[]{:S(2)}) async-start(), calls=%async_computation.13 | async-start | bytes 1769472 | tf_op jit(solution)/shard_map/reduce_scatter | solution.py:174
  572.5 2.6 copy-start.15
  572.5 2.6 copy-start.16
  575.2 3.1 copy-start.14
  578.3 23.1 %copy-start.4 = (bf16[192,512]{1,0:T(8,128)(2,1)S(1)}, bf16[192,512]{1,0:T(8,128)(2,1)}, u32[]{:S(2)}) copy-start(bf16[192,512]{1,0:T(8,128)(2,1)} %copy-done.3) | copy-start | bytes 589828
  578.3 23.1 %copy-start.13 = (f32[512]{0:T(512)S(1)}, f32[512]{0:T(512)}, u32[]{:S(2)}) copy-start(f32[512]{0:T(512)} %param.18) | copy-start | bytes 6148
  578.3 77.7 %copy-start.6 = (bf16[192,512]{1,0:T(8,128)(2,1)S(1)}, bf16[192,512]{1,0:T(8,128)(2,1)}, u32[]{:S(2)}) copy-start(bf16[192,512]{1,0:T(8,128)(2,1)} %param.23) | copy-start | bytes 589828
Sparse Core Ops, SparseCore 0:
  57.7 20.7 all-gather.4
  80.1 24.4 all-gather.8
  108.5 74.8 reduce-scatter.18
  186.7 81.0 reduce-scatter.10
  271.0 82.0 reduce-scatter.14
  393.5 73.4 reduce-scatter.20
  469.7 48.2 all-gather.10
  520.7 46.5 all-gather.6
  569.7 31.6 reduce-scatter.16
  603.6 32.2 reduce-scatter.12
where the time goes:
time: 667 us; the launch traced here: 665 us
  waiting for transfers between devices  360 us (54%)
  blocking collectives  163 us (24%)
  matrix products  72.6 us (11%)
  local copies, waits for them, and re-layouts  28.7 us (4%)
  other arithmetic  16.2 us (2%)
  between operations  14.6 us (2%)
  starting transfers between devices  9.06 us (1%)
    reduce_scatter x2, waiting for transfers between devices, to_heads(): lax.psum_scatter(term(jnp.int32(0), block_len * lax.axis_size(('row', 'se...  135 us
    unnamed x12, waiting for transfers between devices  103 us
    all_gather x2, waiting for transfers between devices, to_rows(): return lax.all_gather(own_share, ('row', 'seq'), axis=0, tiled=True)  67.6 us
    psum x1, blocking collectives, per_device(): squares = lax.psum(jnp.sum(residual * residual, axis=1), ('row', 'seq'))  41.8 us
    psum x1, blocking collectives, per_device(): lax.psum(jnp.sum(scaled_grad * residual, axis=1), ('row', 'seq'))  40.5 us
    all_gather x1, blocking collectives, per_device(): kv_all = lax.all_gather(kv_block, ('row', 'seq'), axis=0, tiled=True)  25.8 us
    all_gather x1, blocking collectives, per_device(): lax.all_gather(kv_grad_block, ('row', 'seq'), axis=0, tiled=True)  24.3 us
    all_gather x1, waiting for transfers between devices, per_device(): normed_all = lax.all_gather(normed, 'col', axis=0, tiled=True)  20.1 us
  transfers between devices with their start and end apart: 12, of which 10 were waited for; matrix products, arithmetic and copies ran while one was open for 12% of the time, Pallas kernels for 0%

commit v1 on v0

v1 whole, which is shorter than its diff:
```python
import jax
import jax.numpy as jnp
from jax import lax
from jax.sharding import PartitionSpec as P
from jax.experimental import pallas as pl

D = 8192
H = 64
KV = 8
HD = 128


epsilon = 1e-05
softcap = 20.0
rope_base = 500000.0


def rotary_tables(positions, head_size):
    half_size = head_size // 2
    frequency = rope_base ** (-(jnp.arange(half_size, dtype=jnp.float32) * 2.0) / head_size)
    angles = positions.astype(jnp.float32)[:, None] * frequency[None, :]
    return (jnp.cos(angles), jnp.sin(angles))


def rotate_pairs(values, cosines, sines):
    half_size = values.shape[-1] // 2
    first_half = values[..., :half_size]
    second_half = values[..., half_size:]
    cos_part = cosines[:, None, :]
    sin_part = sines[:, None, :]
    return jnp.concatenate(
        [
            first_half * cos_part - second_half * sin_part,
            second_half * cos_part + first_half * sin_part,
        ],
        axis=-1,
    )


def rotate_back(values, cosines, sines):
    half_size = values.shape[-1] // 2
    first_half = values[..., :half_size]
    second_half = values[..., half_size:]
    cos_part = cosines[:, None, :]
    sin_part = sines[:, None, :]
    return jnp.concatenate(
        [
            first_half * cos_part + second_half * sin_part,
            second_half * cos_part - first_half * sin_part,
        ],
        axis=-1,
    )


def rope_round(values, positions):
    cosines, sines = rotary_tables(positions, HD)
    row_total = values.shape[0]
    return (
        rotate_pairs(values.reshape(row_total, -1, HD), cosines, sines)
        .reshape(row_total, -1)
        .astype(jnp.bfloat16)
    )


def to_blocks(values, n_row, n_seq):
    length, width = values.shape
    return values.reshape(n_row, length // n_row, n_seq, width // n_seq).transpose(0, 2, 1, 3)


def from_blocks(blocks):
    n_row, n_seq, rows, w = blocks.shape
    return blocks.transpose(0, 2, 1, 3).reshape(n_row * rows, n_seq * w)


def project_kernel(lhs_ref, wq_ref, wkv_ref, wo_ref, out_ref):
    feat = wq_ref.shape[0]
    qw = wq_ref.shape[1]
    kw = wkv_ref.shape[1]
    ow = wo_ref.shape[0]
    emb = lhs_ref[:, :feat]
    og = lhs_ref[:, feat:]
    out_ref[:, :qw] = jnp.dot(emb, wq_ref[...], preferred_element_type=jnp.float32)
    out_ref[:, qw : qw + kw] = jnp.dot(emb, wkv_ref[...], preferred_element_type=jnp.float32)
    out_ref[:, qw + kw : qw + kw + ow] = lax.dot_general(
        og, wo_ref[...], (((1,), (1,)), ((), ())), preferred_element_type=jnp.float32
    )
    emb_f = emb.astype(jnp.float32)
    squares = jnp.sum(emb_f * emb_f, axis=1, keepdims=True)
    out_ref[:, qw + kw + ow :] = jnp.broadcast_to(
        squares, (squares.shape[0], out_ref.shape[1] - qw - kw - ow)
    )


def project_blocks(lhs, wq, wkv, wo, n_row, n_seq, out_w):
    length, lw = lhs.shape
    feat = wq.shape[0]
    qw = wq.shape[1] // n_seq
    kw = HD
    ow = wo.shape[0] // n_seq
    rows = length // n_row
    flops = 2 * length * feat * (n_seq * (qw + kw + ow))
    return pl.pallas_call(
        project_kernel,
        grid=(n_row, n_seq),
        in_specs=[
            pl.BlockSpec((rows, lw), lambda r, s: (r, 0)),
            pl.BlockSpec((feat, qw), lambda r, s: (0, s)),
            pl.BlockSpec((feat, kw), lambda r, s: (0, s % 2)),
            pl.BlockSpec((ow, feat), lambda r, s: (s, 0)),
        ],
        out_specs=pl.BlockSpec((rows, out_w), lambda r, s: (r * n_seq + s, 0)),
        out_shape=jax.ShapeDtypeStruct((n_row * n_seq * rows, out_w), jnp.float32),
        cost_estimate=pl.CostEstimate(
            flops=flops,
            transcendentals=0,
            bytes_accessed=lhs.size * 2 + (wq.size + wkv.size + wo.size) * 2
            + n_row * n_seq * rows * out_w * 4,
        ),
    )(lhs, wq, wkv, wo)


def per_device(
    motion_ids,
    audio_ids,
    segment_ids,
    motion_table,
    audio_table,
    norm_gain,
    w_query,
    w_key,
    w_value,
    w_out,
    out_grad,
):
    seq_len = segment_ids.shape[0]
    n_row = lax.axis_size("row")
    n_seq = lax.axis_size("seq")
    n_col = lax.axis_size("col")
    row_index = lax.axis_index("row")
    seq_index = lax.axis_index("seq")
    col_index = lax.axis_index("col")
    n_rs = n_row * n_seq
    block_len = seq_len // n_rs
    quarter_len = seq_len // n_row
    own_len = seq_len // n_col
    feat = motion_table.shape[1]
    query_width = w_query.shape[1]
    kv_width = w_key.shape[1]
    head_count = query_width // HD // n_seq
    part_w = head_count * HD
    score_scale = HD ** (-0.5)
    assert kv_width == HD and part_w == 2 * HD

    embedded = (
        jnp.take(motion_table, motion_ids, axis=0).astype(jnp.float32)
        + jnp.take(audio_table, audio_ids, axis=0).astype(jnp.float32)
    ).astype(jnp.bfloat16)
    residual = embedded.astype(jnp.float32)

    both_all = lax.all_gather(
        jnp.concatenate([embedded, out_grad], axis=1), "col", axis=0, tiled=True
    )
    emb_all = both_all[:, :feat]
    grad_all = both_all[:, feat:]
    emb_all_f = emb_all.astype(jnp.float32)
    gain_col = norm_gain[:, None]
    wq_gain = (w_query.astype(jnp.float32) * gain_col).astype(jnp.bfloat16)
    wkv_gain = (
        jnp.concatenate([w_key, w_value], axis=1).astype(jnp.float32) * gain_col
    ).astype(jnp.bfloat16)
    out_w = part_w + HD + part_w + 128
    blocks = project_blocks(both_all, wq_gain, wkv_gain, w_out, n_row, n_seq, out_w)
    got = lax.psum_scatter(blocks, ("row", "seq"), scatter_dimension=0, tiled=True)

    q_raw = got[:, :part_w]
    kv_raw = got[:, part_w : part_w + HD]
    d_raw = got[:, part_w + HD : 2 * part_w + HD]
    sq_q = got[:, 2 * part_w + HD]
    inv_q = lax.rsqrt(sq_q / D + epsilon)

    query_pos = row_index * quarter_len + jnp.arange(quarter_len, dtype=jnp.int32)
    queries = rope_round(q_raw * inv_q[:, None], query_pos)
    kv_scaled = kv_raw * inv_q[:, None]
    kv_piece = jnp.where(
        seq_index % 2 == 0, rope_round(kv_scaled, query_pos), kv_scaled.astype(jnp.bfloat16)
    )
    out_heads = d_raw.astype(jnp.bfloat16).reshape(quarter_len, head_count, HD)

    kv_gath = lax.all_gather(kv_piece, ("row", "seq"), axis=0, tiled=True).reshape(
        n_row, n_seq, quarter_len, HD
    )
    key_sel = kv_gath[:, 0].reshape(seq_len, HD)
    value_sel = kv_gath[:, 1].reshape(seq_len, HD)

    key_pos = jnp.arange(seq_len, dtype=jnp.int32)
    allowed = (key_pos[None, :] <= query_pos[:, None]) & (
        segment_ids[None, :] == jnp.take(segment_ids, query_pos)[:, None]
    )
    query_heads = queries.reshape(quarter_len, head_count, HD)
    raw_scores = (
        jnp.einsum("qhd,kd->hqk", query_heads, key_sel, preferred_element_type=jnp.float32)
        * score_scale
    )
    capped = softcap * jnp.tanh(raw_scores / softcap)
    weights = jnp.where(allowed[None], jnp.exp(capped), 0.0)
    totals = jnp.sum(weights, axis=2)
    attended = jnp.einsum(
        "hqk,kd->qhd", weights.astype(jnp.bfloat16), value_sel, preferred_element_type=jnp.float32
    )
    attn_out = (
        (attended / totals.T[:, :, None]).astype(jnp.bfloat16).reshape(quarter_len, part_w)
    )
    attn_probs = weights / totals[:, :, None]
    prob_grads = jnp.einsum(
        "qhd,kd->hqk", out_heads, value_sel, preferred_element_type=jnp.float32
    )
    row_dots = jnp.sum(attn_probs * prob_grads, axis=2, keepdims=True)
    grad_scores = (
        attn_probs * (prob_grads - row_dots) * (1.0 - (capped / softcap) ** 2) * score_scale
    ).astype(jnp.bfloat16)
    grad_query = jnp.einsum(
        "hqk,kd->qhd", grad_scores, key_sel, preferred_element_type=jnp.float32
    )
    grad_key_part = jnp.einsum(
        "hqk,qhd->kd", grad_scores, query_heads, preferred_element_type=jnp.float32
    )
    grad_value_part = jnp.einsum(
        "hqk,qhd->kd",
        attn_probs.astype(jnp.bfloat16),
        out_heads,
        preferred_element_type=jnp.float32,
    )
    cos_all, sin_all = rotary_tables(key_pos, HD)
    grad_key_rot = rotate_back(grad_key_part[:, None, :], cos_all, sin_all).reshape(
        seq_len, kv_width
    )
    kv_grad_sum = lax.psum_scatter(
        jnp.concatenate([grad_key_rot, grad_value_part], axis=1),
        ("row", "seq"),
        scatter_dimension=0,
        tiled=True,
    ).astype(jnp.bfloat16)
    cos_query, sin_query = rotary_tables(query_pos, HD)
    grad_query_round = (
        rotate_back(grad_query, cos_query, sin_query)
        .reshape(quarter_len, part_w)
        .astype(jnp.bfloat16)
    )
    inv_hi = inv_q.astype(jnp.bfloat16)
    inv_lo = (inv_q - inv_hi.astype(jnp.float32)).astype(jnp.bfloat16)
    inv_rows = -(-2 * quarter_len // part_w)
    inv_rows = inv_rows + (-inv_rows) % 8
    inv_pack = jnp.pad(
        jnp.concatenate([inv_hi, inv_lo]), (0, inv_rows * part_w - 2 * quarter_len)
    ).reshape(inv_rows, part_w)
    back_rows = 2 * quarter_len + block_len + inv_rows
    back_all = lax.all_gather(
        jnp.concatenate([attn_out, grad_query_round, kv_grad_sum, inv_pack], axis=0),
        ("row", "seq"),
        axis=0,
        tiled=True,
    ).reshape(n_rs, back_rows, part_w)
    inv_parts = back_all[:, 2 * quarter_len + block_len :].reshape(n_rs, -1)
    inv_blocks = inv_parts[:, :quarter_len].astype(jnp.float32) + inv_parts[
        :, quarter_len : 2 * quarter_len
    ].astype(jnp.float32)
    inv_all = inv_blocks.reshape(n_row, n_seq, quarter_len)[:, 0].reshape(seq_len)
    out_all = from_blocks(back_all[:, :quarter_len].reshape(n_row, n_seq, quarter_len, part_w))
    grad_query_all = from_blocks(
        back_all[:, quarter_len : 2 * quarter_len].reshape(n_row, n_seq, quarter_len, part_w)
    )
    kv_grad_all = back_all[:, 2 * quarter_len : 2 * quarter_len + block_len].reshape(
        seq_len, part_w
    )

    normed_all = (emb_all_f * inv_all[:, None] * norm_gain[None, :]).astype(jnp.bfloat16)
    grad_wo = jnp.einsum("ln,ld->nd", out_all, grad_all, preferred_element_type=jnp.float32)
    grad_wq = jnp.einsum(
        "ld,ln->dn", normed_all, grad_query_all, preferred_element_type=jnp.float32
    )
    grad_wk = jnp.einsum(
        "ld,ln->dn", normed_all, kv_grad_all[:, :kv_width], preferred_element_type=jnp.float32
    )
    grad_wv = jnp.einsum(
        "ld,ln->dn", normed_all, kv_grad_all[:, kv_width:], preferred_element_type=jnp.float32
    )

    branch_part = jnp.dot(out_all, w_out, preferred_element_type=jnp.float32)
    total_term = jnp.einsum(
        "ln,dn->ld", grad_query_all, w_query, preferred_element_type=jnp.float32
    )
    total_term = total_term + jnp.einsum(
        "ln,dn->ld", kv_grad_all[:, :kv_width], w_key, preferred_element_type=jnp.float32
    )
    total_term = total_term + jnp.einsum(
        "ln,dn->ld", kv_grad_all[:, kv_width:], w_value, preferred_element_type=jnp.float32
    )
    col_sum = lax.psum_scatter(
        jnp.concatenate([branch_part, total_term], axis=1).astype(jnp.bfloat16),
        "col",
        scatter_dimension=0,
        tiled=True,
    ).astype(jnp.float32)
    branch_sum = col_sum[:, :feat]
    grad_normed = col_sum[:, feat:]
    layer_out = (residual + branch_sum).astype(jnp.bfloat16)

    inverse = lax.dynamic_slice(inv_all, (col_index * own_len,), (own_len,))
    scaled_grad = grad_normed * norm_gain[None, :]
    total_dot = lax.psum(lax.psum(jnp.sum(scaled_grad * residual, axis=1), "seq"), "row")
    grad_input = (
        out_grad.astype(jnp.float32)
        + inverse[:, None] * scaled_grad
        - residual * (inverse**3 * total_dot / D)[:, None]
    ).astype(jnp.bfloat16)
    grad_gain = lax.psum(jnp.sum(grad_normed * residual * inverse[:, None], axis=0), "col")
    return (layer_out, grad_input, grad_gain, grad_wq, grad_wk, grad_wv, grad_wo)


def solution(mesh):
    placed = (
        P("col"),
        P("col"),
        P(),
        P(None, ("row", "seq")),
        P(None, ("row", "seq")),
        P(("row", "seq")),
        P(("row", "seq"), "col"),
        P(("row", "seq"), "col"),
        P(("row", "seq"), "col"),
        P("col", ("row", "seq")),
        P("col", ("row", "seq")),
    )
    return jax.shard_map(
        per_device,
        mesh=mesh,
        in_specs=placed,
        out_specs=(
            P("col", ("row", "seq")),
            P("col", ("row", "seq")),
            P(("row", "seq")),
            P(("row", "seq"), "col"),
            P(("row", "seq"), "col"),
            P(("row", "seq"), "col"),
            P("col", ("row", "seq")),
        ),
        check_vma=False,
    )
```

time: 667 us -> 501 us (0.75)
  blocking collectives: 163 us -> 34.1 us
  waiting for transfers between devices: 360 us -> 329 us
  Pallas kernels: 0 us -> 20 us
  matrix products: 72.6 us -> 52.8 us
  starting transfers between devices: 9.06 us -> 0.65 us
    psum x2, blocking collectives: 82.3 us -> 21.1 us  [the longest x1 10.7 us: per_device(): lax.psum(lax.psum(jnp.sum(scaled_grad * residual, axis=1), 'seq'), 'row')]
    all_gather x2 -> x0, blocking collectives: 50.1 us -> none  [the longest x1 25.8 us: per_device(): kv_all = lax.all_gather(kv_block, ('row', 'seq'), axis=0, tiled=True)]
    unnamed x12 -> x7, waiting for transfers between devices: 103 us -> 57.7 us
    all_gather x4 -> x3, waiting for transfers between devices: 101 us -> 131 us  [the longest x1 65 us: per_device(): lax.all_gather(jnp.concatenate([attn_out, grad_query_round, kv_grad_sum,...]
    dot_general x11 -> x7, matrix products: 57.6 us -> 34.2 us  [the longest x1 11.5 us: per_device(): jnp.einsum('hqk,kd->qhd', grad_scores, key_sel, preferred_element_type=jn...]
    pallas_call x0 -> x1, Pallas kernels: none -> 20 us  [project_blocks(): pl.pallas_call(project_kernel, grid=(n_row, n_seq), in_specs=[pl.BlockSpe...]
    all_to_all x2 -> x0, blocking collectives: 18 us -> none  [to_rows(): lax.all_to_all(heads_part, 'seq', split_axis=0, concat_axis=1, tiled=True)]
    reduce_scatter x4 -> x2, waiting for transfers between devices: 155 us -> 140 us  [the longest x1 121 us: per_device(): lax.psum_scatter(blocks, ('row', 'seq'), scatter_dimension=0, tiled=True)]
  transfers between devices with their start and end apart: 12 -> 6, of which waited for: 10 -> 6; matrix products, arithmetic and copies ran while one was open for 12% -> 8% of each run, Pallas kernels for 0% -> 0%
where the time goes in v1:
time: 501 us; the launch traced here: 500 us
  waiting for transfers between devices  329 us (66%)
  matrix products  52.8 us (11%)
  blocking collectives  34.1 us (7%)
  local copies, waits for them, and re-layouts  27.8 us (6%)
  other arithmetic  21.1 us (4%)
  Pallas kernels  20 us (4%)
  between operations  14.6 us (3%)
    reduce_scatter x1, waiting for transfers between devices, per_device(): lax.psum_scatter(blocks, ('row', 'seq'), scatter_dimension=0, tiled=True)  121 us
    all_gather x1, waiting for transfers between devices, per_device(): lax.all_gather(jnp.concatenate([attn_out, grad_query_round, kv_grad_sum,...  65 us
    unnamed x7, waiting for transfers between devices  57.7 us
    all_gather x1, waiting for transfers between devices, per_device(): lax.all_gather(kv_piece, ('row', 'seq'), axis=0, tiled=True)  37.4 us
    all_gather x1, waiting for transfers between devices, per_device(): lax.all_gather(jnp.concatenate([embedded, out_grad], axis=1), 'col', axis...  28.2 us
    pallas_call x1, Pallas kernels, project_blocks(): pl.pallas_call(project_kernel, grid=(n_row, n_seq), in_specs=[pl.BlockSpe...  20 us
    reduce_scatter x1, waiting for transfers between devices, per_device(): lax.psum_scatter(jnp.concatenate([branch_part, total_term], axis=1).astyp...  19 us
    psum x1, blocking collectives, per_device(): lax.psum(jnp.sum(grad_normed * residual * inverse[:, None], axis=0), 'col')  13 us
  transfers between devices with their start and end apart: 6, of which 6 were waited for; matrix products, arithmetic and copies ran while one was open for 8% of the time, Pallas kernels for 0%

profile of v1, /device:TPU:0, one launch (start us, length us, event | category | flops | bytes accessed | tf_op | source)
XLA Modules:
  0.0 499.7 jit_solution(5202138890383895118)
XLA Ops:
  7.3 0.8 compare_select_fusion.3
  8.1 0.7 compare_and_fusion
  8.8 0.7 compare_select_fusion.2
  9.5 2.2 gather_fusion
  11.7 1.0 gather_fusion.1
  12.8 1.7 pad_maximum_fusion.3
  14.6 0.8 multiply_convert_fusion.2.wkv_ref
  15.5 1.2 multiply_convert_fusion.1.wq_ref
  16.7 28.2 %all-gather.4.cloned.1.call-done.lhs_ref = bf16[1536,1024]{1,0:T(8,128)(2,1)} async-done(((bf16[192,1024]{1,0:T(8,128)(2,1)}), bf16[1536,1024]{1,0:T(8,128)(2,1)}) %all-gather.4.cloned.1.call-update) | async-done | bytes 3145744 | tf_op jit(solution)/shard_map/all_gather | solution.py:160
  44.9 20.0 %shard_map.162 = f32[6144,768]{1,0:T(8,128)} custom-call(bf16[1536,1024]{1,0:T(8,128)(2,1)} %all-gather.4.cloned.1.call-done.lhs_ref, bf16[512,1024]{1,0:T(8,128)(2,1)} %multiply_convert_fusion.1.wq_ref, bf16[512,256]{1,0:T(8,128)(2,1)} %multiply_convert_fusion.2.wkv_ref, bf16[1024,512]{1,0:T(8,128)(2,1)} %wo_ref.1), custom_call_target="tpu_custom_call" | custom-call | flops 4026531840 | bytes 24379392 | tf_op jit(solution)/shard_map/pallas_call | solution.py:102
  65.0 121.2 %reduce-scatter.6.cloned.1.call-done = f32[384,768]{1,0:T(8,128)} async-done(((f32[6144,768]{1,0:T(8,128)}), f32[384,768]{1,0:T(8,128)}) %reduce-scatter.6.cloned.1.call-update) | async-done | bytes 1179664 | tf_op jit(solution)/shard_map/reduce_scatter | solution.py:173
  186.2 1.2 fusion.52
  187.4 1.0 fusion.54
  188.5 0.8 fusion.47
  189.3 1.7 fusion.55
  191.0 0.2 reduce-scatter.10.cloned.1.call-start
  191.3 2.5 gather_fusion.2
  193.9 0.8 multiply_cosine_fusion.1
  194.6 1.4 fusion.8
  196.1 0.2 reshape.357
  196.5 0.5 fusion.80
  197.1 37.4 %all-gather.6.cloned.1.call-done = bf16[6144,128]{1,0:T(8,128)(2,1)} async-done(((bf16[384,128]{1,0:T(8,128)(2,1)}), bf16[6144,128]{1,0:T(8,128)(2,1)}) %all-gather.6.cloned.1.call-update) | async-done | bytes 1572880 | tf_op jit(solution)/shard_map/all_gather | solution.py:189
  234.6 1.2 fusion.79
  235.8 2.9 fusion.81
  238.7 1.7 fusion.13
  240.4 2.2 copy-done.19
  242.6 2.8 convolution_bitcast_fusion
  245.3 9.7 %convolution_bitcast_fusion.1 = f32[1536,1,128]{0,2,1:T(8,128)S(1)} fusion(f32[1536,384,2]{1,0,2:T(8,128)} %fusion.81, f32[1536,384,2]{1,0,2:T(8,128)} %copy-done.19, bf16[384,2,64]{2,0,1:T(8,128)(2,1)S(1)} %get-tuple-element.16, bf16[384,2,64]{2,0,1:T(8,128)(2,1)S(1)} %get-tuple-element.15, f32[2,384]{1,0:T(2,128)S(1)} %get-tuple-element.29, ...), kind=kOutput, calls=%fused_computation.19 | convolution fusion | flops 321259776 | bytes 11013120 | tf_op jit(solution)/shard_map/hqk,qhd->kd/dot_general | solution.py:224
  255.0 1.6 fusion.28
  256.7 1.2 pad_maximum_fusion.1
  258.0 1.6 copy.116
  259.6 0.3 all-gather.8.cloned.1.call-start
  260.0 11.5 %fusion.14 = f32[384,2,128]{2,0,1:T(8,128)S(1)} fusion(bf16[1536,128,1]{1,0,2:T(8,128)(2,1)} %bitcast.155, f32[1536,384,2]{1,0,2:T(8,128)} %fusion.81, f32[1536,384,2]{1,0,2:T(8,128)} %copy-done.19, f32[2,384]{1,0:T(2,128)S(1)} %get-tuple-element.29, pred[384,1536]{0,1:T(8,128)(4,1)} %fusion.8), kind=kOutput, calls=%fused_computation.33 | convolution fusion | flops 320866560 | bytes 10816512 | tf_op jit(solution)/shard_map/hqk,kd->qhd/dot_general | solution.py:221
  271.5 0.2 add_convert_fusion
  272.1 3.8 fusion.21
  275.9 57.6 %reduce-scatter.10.cloned.1.call-done = f32[96,256]{1,0:T(8,128)} async-done(((f32[1536,256]{1,0:T(8,128)}), f32[96,256]{1,0:T(8,128)}) %reduce-scatter.10.cloned.1.call-update) | async-done | bytes 98320
  333.6 1.0 copy.117
  334.7 1.0 copy.95
  335.7 65.0 %all-gather.8.cloned.1.call-done = bf16[13952,256]{1,0:T(8,128)(2,1)} async-done(((bf16[872,256]{1,0:T(8,128)(2,1)}), bf16[13952,256]{1,0:T(8,128)(2,1)}) %all-gather.8.cloned.1.call-update) | async-done | bytes 7143440 | tf_op jit(solution)/shard_map/all_gather | solution.py:257
  400.7 1.2 slice.133
  401.9 3.3 fusion.78
  405.2 2.4 copy.98
  407.6 0.8 copy.122
  408.4 0.4 copy-done.10
  408.9 1.8 fusion.82
  410.7 0.6 convolution_add_fusion.1
  411.3 0.6 fusion.4
  411.9 2.4 copy.96
  414.4 0.8 copy.121
  415.1 1.6 copy-done.6
  416.8 1.8 convolution_convert_fusion
  418.6 2.2 pad_maximum_fusion
  420.8 0.8 slice.137
  421.8 3.3 fusion.36
  425.2 3.0 fusion.39
  428.2 5.9 %fusion.11 = f32[1024,512]{1,0:T(8,128)} fusion(bf16[1536,1024]{1,0:T(8,128)(2,1)} %bitcast.143, bf16[1536,1024]{1,0:T(8,128)(2,1)} %all-gather.4.cloned.1.call-done.lhs_ref), kind=kOutput, calls=%fused_computation.29 | convolution fusion | flops 1610612736 | bytes 6815744 | tf_op jit(solution)/shard_map/ln,ld->nd/dot_general | solution.py:277
  434.1 3.3 fusion.77
  437.5 19.0 %reduce-scatter.8.cloned.1.call-done = bf16[192,1024]{1,0:T(8,128)(2,1)} async-done(((bf16[1536,1024]{1,0:T(8,128)(2,1)}), bf16[192,1024]{1,0:T(8,128)(2,1)}) %reduce-scatter.8.cloned.1.call-update) | async-done | bytes 393232 | tf_op jit(solution)/shard_map/reduce_scatter | solution.py:298
  456.5 1.1 convert_element_type.132
  457.6 0.2 fusion.35
  457.8 10.4 %psum.21 = f32[192]{0:T(256)S(1)} all-reduce(f32[192]{0:T(256)S(1)} %get-tuple-element.8), channel_id=1, replica_groups=mesh['row'=4,'col'=8,'seq'=4] {'seq'}, use_global_device_ids=true, to_apply=%region_6.7 | all-reduce | flops 192 | bytes 1536 | tf_op jit(solution)/shard_map/psum | solution.py:310
  468.2 10.7 %psum.22 = f32[192]{0:T(256)S(1)} all-reduce(f32[192]{0:T(256)S(1)} %psum.21), channel_id=1, replica_groups=mesh['row'=4,'col'=8,'seq'=4] {'row'}, use_global_device_ids=true, to_apply=%region_7.8 | all-reduce | flops 192 | bytes 1536 | tf_op jit(solution)/shard_map/psum | solution.py:310
  479.0 0.9 fusion.33
  479.8 13.0 %psum.23 = f32[512]{0:T(512)} all-reduce(f32[512]{0:T(512)S(1)} %get-tuple-element.7), channel_id=1, replica_groups=mesh['row'=4,'col'=8,'seq'=4] {'col'}, use_global_device_ids=true, to_apply=%region_9.10 | all-reduce | flops 512 | bytes 4096 | tf_op jit(solution)/shard_map/psum | solution.py:316
  (75 shorter events, 1.8 us)
Async XLA Ops:
  7.2 4.5 copy-start
  7.2 7.4 %copy-start.18 = (f32[512]{0:T(512)S(1)}, f32[512]{0:T(512)}, u32[]{:S(2)}) copy-start(f32[512]{0:T(512)} %param.16) | copy-start | bytes 6148
  7.2 7.4 %copy-start.15 = (bf16[512,128]{1,0:T(8,128)(2,1)S(1)}, bf16[512,128]{1,0:T(8,128)(2,1)}, u32[]{:S(2)}) copy-start(bf16[512,128]{1,0:T(8,128)(2,1)} %param.18) | copy-start | bytes 393220
  7.2 7.4 %copy-start.14 = (bf16[512,128]{1,0:T(8,128)(2,1)S(1)}, bf16[512,128]{1,0:T(8,128)(2,1)}, u32[]{:S(2)}) copy-start(bf16[512,128]{1,0:T(8,128)(2,1)} %param.19) | copy-start | bytes 393220
  7.2 8.3 %copy-start.9 = (bf16[512,1024]{1,0:T(8,128)(2,1)S(1)}, bf16[512,1024]{1,0:T(8,128)(2,1)}, u32[]{:S(2)}) copy-start(bf16[512,1024]{1,0:T(8,128)(2,1)} %param.17) | copy-start | bytes 3145732
  7.2 37.7 %all-gather.4.cloned.1.call-start = ((), (), s32[]{:S(2)}) async-start(), calls=%async_computation.3 | async-start | bytes 3538944 | tf_op jit(solution)/shard_map/all_gather | solution.py:160
  14.6 171.7 %reduce-scatter.6.cloned.1.call-start = ((), (), s32[]{:S(2)}) async-start(), calls=%async_computation.4 | async-start | bytes 20054016 | tf_op jit(solution)/shard_map/reduce_scatter | solution.py:173
  64.9 126.4 %copy-start.2 = (s32[1536]{0:T(1024)S(1)}, s32[1536]{0:T(1024)}, u32[]{:S(2)}) copy-start(s32[1536]{0:T(1024)} %param.13) | copy-start | bytes 18436
  64.9 169.6 %all-gather.6.cloned.1.call-start = ((), (), s32[]{:S(2)}) async-start(), calls=%async_computation.5 | async-start | bytes 1671168 | tf_op jit(solution)/shard_map/all_gather | solution.py:189
  186.2 9.8 %copy-start.7 = (f32[384,768]{1,0:T(8,128)S(1)}, f32[384,768]{1,0:T(8,128)}, u32[]{:S(2)}) copy-start(f32[384,768]{1,0:T(8,128)} %reduce-scatter.6.cloned.1.call-done) | copy-start | bytes 3538948
  191.0 142.5 %reduce-scatter.10.cloned.1.call-start = ((), (), s32[]{:S(2)}) async-start(), calls=%async_computation.8 | async-start | bytes 1671168
  196.5 42.1 %copy-start.12 = (pred[384,1536]{0,1:T(8,128)(4,1)S(1)}, pred[384,1536]{0,1:T(8,128)(4,1)}, u32[]{:S(2)}) copy-start(pred[384,1536]{0,1:T(8,128)(4,1)} %fusion.8) | copy-start | bytes 1769476
  235.8 4.6 copy-start.17
  240.4 2.2 copy-start.19
  259.6 141.1 %all-gather.8.cloned.1.call-start = ((), (), s32[]{:S(2)}) async-start(), calls=%async_computation.6 | async-start | bytes 7589888 | tf_op jit(solution)/shard_map/all_gather | solution.py:257
  260.0 12.0 %copy-start.13 = (pred[384,1536]{0,1:T(8,128)(4,1)S(1)}, pred[384,1536]{0,1:T(8,128)(4,1)}, u32[]{:S(2)}) copy-start(pred[384,1536]{0,1:T(8,128)(4,1)} %fusion.8) | copy-start | bytes 1769476
  335.7 120.8 %reduce-scatter.8.cloned.1.call-start = ((), (), s32[]{:S(2)}) async-start(), calls=%async_computation.7 | async-start | bytes 3538944 | tf_op jit(solution)/shard_map/reduce_scatter | solution.py:298
  407.6 1.2 copy-start.10
  408.4 2.3 copy-start.4
  408.9 1.9 copy-start.16
  414.4 2.4 copy-start.8
  415.1 1.7 copy-start.6
  428.2 5.9 %copy-start.3 = (bf16[1536,1024]{1,0:T(8,128)(2,1)S(1)}, bf16[1536,1024]{1,0:T(8,128)(2,1)}, u32[]{:S(2)}) copy-start(bf16[1536,1024]{1,0:T(8,128)(2,1)} %all-gather.4.cloned.1.call-done.lhs_ref) | copy-start | bytes 9437188
  428.2 5.9 %copy-start.5 = (bf16[192,8,4,256]{3,1,2,0:T(8,128)(2,1)S(1)}, bf16[192,8,4,256]{3,1,2,0:T(8,128)(2,1)}, u32[]{:S(2)}) copy-start(bf16[192,8,4,256]{3,1,2,0:T(8,128)(2,1)} %copy-done.4) | copy-start | bytes 9437188
  428.2 64.6 %copy-start.1 = (bf16[1024,512]{1,0:T(8,128)(2,1)S(1)}, bf16[1024,512]{1,0:T(8,128)(2,1)}, u32[]{:S(2)}) copy-start(bf16[1024,512]{1,0:T(8,128)(2,1)} %param.15) | copy-start | bytes 3145732
  434.1 44.8 %copy-start.11 = (bf16[192,512]{1,0:T(8,128)(2,1)S(1)}, bf16[192,512]{1,0:T(8,128)(2,1)}, u32[]{:S(2)}) copy-start(bf16[192,512]{1,0:T(8,128)(2,1)} %param.21) | copy-start | bytes 589828
Sparse Core Ops, SparseCore 0:
  14.7 30.1 all-gather.3
  65.0 121.1 reduce-scatter.5
  191.2 43.3 all-gather.5
  259.7 73.8 reduce-scatter.9
  336.1 64.5 all-gather.7
  420.9 35.5 reduce-scatter.7

commit v2 on v1

--- a/solution.py
+++ b/solution.py
@@ -13,6 +13,7 @@
 epsilon = 1e-05
 softcap = 20.0
 rope_base = 500000.0
+MAX_DOC = 768
 
 
 def rotary_tables(positions, head_size):
@@ -189,12 +190,18 @@
     kv_gath = lax.all_gather(kv_piece, ("row", "seq"), axis=0, tiled=True).reshape(
         n_row, n_seq, quarter_len, HD
     )
-    key_sel = kv_gath[:, 0].reshape(seq_len, HD)
-    value_sel = kv_gath[:, 1].reshape(seq_len, HD)
-
-    key_pos = jnp.arange(seq_len, dtype=jnp.int32)
+    key_all = kv_gath[:, 0].reshape(seq_len, HD)
+    value_all = kv_gath[:, 1].reshape(seq_len, HD)
+
+    doc_back = -(-(MAX_DOC - 1) // quarter_len) * quarter_len
+    win = min(seq_len, quarter_len + doc_back)
+    win_start = jnp.clip(row_index * quarter_len - doc_back, 0, seq_len - win)
+    key_pos = win_start + jnp.arange(win, dtype=jnp.int32)
+    key_sel = lax.dynamic_slice(key_all, (win_start, 0), (win, HD))
+    value_sel = lax.dynamic_slice(value_all, (win_start, 0), (win, HD))
+    key_seg = lax.dynamic_slice(segment_ids, (win_start,), (win,))
     allowed = (key_pos[None, :] <= query_pos[:, None]) & (
-        segment_ids[None, :] == jnp.take(segment_ids, query_pos)[:, None]
+        key_seg[None, :] == jnp.take(segment_ids, query_pos)[:, None]
     )
     query_heads = queries.reshape(quarter_len, head_count, HD)
     raw_scores = (
@@ -232,14 +239,9 @@
     )
     cos_all, sin_all = rotary_tables(key_pos, HD)
     grad_key_rot = rotate_back(grad_key_part[:, None, :], cos_all, sin_all).reshape(
-        seq_len, kv_width
-    )
-    kv_grad_sum = lax.psum_scatter(
-        jnp.concatenate([grad_key_rot, grad_value_part], axis=1),
-        ("row", "seq"),
-        scatter_dimension=0,
-        tiled=True,
-    ).astype(jnp.bfloat16)
+        win, kv_width
+    )
+    kv_grad_win = jnp.concatenate([grad_key_rot, grad_value_part], axis=1).astype(jnp.bfloat16)
     cos_query, sin_query = rotary_tables(query_pos, HD)
     grad_query_round = (
         rotate_back(grad_query, cos_query, sin_query)
@@ -253,14 +255,14 @@
     inv_pack = jnp.pad(
         jnp.concatenate([inv_hi, inv_lo]), (0, inv_rows * part_w - 2 * quarter_len)
     ).reshape(inv_rows, part_w)
-    back_rows = 2 * quarter_len + block_len + inv_rows
+    back_rows = 2 * quarter_len + win + inv_rows
     back_all = lax.all_gather(
-        jnp.concatenate([attn_out, grad_query_round, kv_grad_sum, inv_pack], axis=0),
+        jnp.concatenate([attn_out, grad_query_round, kv_grad_win, inv_pack], axis=0),
         ("row", "seq"),
         axis=0,
         tiled=True,
     ).reshape(n_rs, back_rows, part_w)
-    inv_parts = back_all[:, 2 * quarter_len + block_len :].reshape(n_rs, -1)
+    inv_parts = back_all[:, 2 * quarter_len + win :].reshape(n_rs, -1)
     inv_blocks = inv_parts[:, :quarter_len].astype(jnp.float32) + inv_parts[
         :, quarter_len : 2 * quarter_len
     ].astype(jnp.float32)
@@ -269,9 +271,17 @@
     grad_query_all = from_blocks(
         back_all[:, quarter_len : 2 * quarter_len].reshape(n_row, n_seq, quarter_len, part_w)
     )
-    kv_grad_all = back_all[:, 2 * quarter_len : 2 * quarter_len + block_len].reshape(
-        seq_len, part_w
-    )
+    kv_terms = (
+        back_all[:, 2 * quarter_len : 2 * quarter_len + win]
+        .astype(jnp.float32)
+        .reshape(n_row, n_seq, win, part_w)
+        .sum(axis=1)
+    )
+    kv_grad_f = jnp.zeros((seq_len, part_w), jnp.float32)
+    for quarter in range(n_row):
+        first = min(max(quarter * quarter_len - doc_back, 0), seq_len - win)
+        kv_grad_f = kv_grad_f.at[first : first + win].add(kv_terms[quarter])
+    kv_grad_all = kv_grad_f.astype(jnp.bfloat16)
 
     normed_all = (emb_all_f * inv_all[:, None] * norm_gain[None, :]).astype(jnp.bfloat16)
     grad_wo = jnp.einsum("ln,ld->nd", out_all, grad_all, preferred_element_type=jnp.float32)

time: 501 us -> 480 us (0.958)
  waiting for transfers between devices: 329 us -> 314 us
  matrix products: 52.8 us -> 43.9 us
    unnamed x7 -> x5, waiting for transfers between devices: 57.7 us -> 0.08 us
    all_gather x1, waiting for transfers between devices: 65 us -> 105 us  [per_device(): lax.all_gather(jnp.concatenate([attn_out, grad_query_round, kv_grad_win,...]
    reduce_sum x0 -> x1, other arithmetic: none -> 5.68 us  [per_device(): kv_terms = back_all[:, 2 * quarter_len:2 * quarter_len + win].astype(jnp....]
  transfers between devices with their start and end apart: 6 -> 5, of which waited for: 6 -> 5; matrix products, arithmetic and copies ran while one was open for 8% -> 5% of each run, Pallas kernels for 0% -> 0%
where the time goes in v2:
time: 480 us; the launch traced here: 475 us
  waiting for transfers between devices  314 us (65%)
  matrix products  43.9 us (9%)
  blocking collectives  34 us (7%)
  other arithmetic  24.5 us (5%)
  local copies, waits for them, and re-layouts  23.9 us (5%)
  Pallas kernels  20 us (4%)
  between operations  14.8 us (3%)
    reduce_scatter x1, waiting for transfers between devices, per_device(): lax.psum_scatter(blocks, ('row', 'seq'), scatter_dimension=0, tiled=True)  121 us
    all_gather x1, waiting for transfers between devices, per_device(): lax.all_gather(jnp.concatenate([attn_out, grad_query_round, kv_grad_win,...  105 us
    all_gather x1, waiting for transfers between devices, per_device(): lax.all_gather(kv_piece, ('row', 'seq'), axis=0, tiled=True)  37 us
    all_gather x1, waiting for transfers between devices, per_device(): lax.all_gather(jnp.concatenate([embedded, out_grad], axis=1), 'col', axis...  28.2 us
    reduce_scatter x1, waiting for transfers between devices, per_device(): lax.psum_scatter(jnp.concatenate([branch_part, total_term], axis=1).astyp...  21.8 us
    pallas_call x1, Pallas kernels, project_blocks(): pl.pallas_call(project_kernel, grid=(n_row, n_seq), in_specs=[pl.BlockSpe...  20 us
    psum x1, blocking collectives, per_device(): lax.psum(jnp.sum(grad_normed * residual * inverse[:, None], axis=0), 'col')  13 us
    psum x1, blocking collectives, per_device(): lax.psum(lax.psum(jnp.sum(scaled_grad * residual, axis=1), 'seq'), 'row')  10.7 us
  transfers between devices with their start and end apart: 5, of which 5 were waited for; matrix products, arithmetic and copies ran while one was open for 5% of the time, Pallas kernels for 0%

profile of v2, /device:TPU:0, one launch (start us, length us, event | category | flops | bytes accessed | tf_op | source)
XLA Modules:
  0.0 475.5 jit_solution(216245766785972835)
XLA Ops:
  7.3 0.9 compare_select_fusion.2
  8.1 0.7 compare_and_fusion.1
  8.9 2.2 gather_fusion
  11.0 1.0 gather_fusion.1
  12.0 0.1 add_convert_fusion.2
  12.2 0.8 pad_maximum_fusion.2
  13.1 0.8 multiply_convert_fusion.2.wkv_ref
  13.9 1.2 multiply_convert_fusion.1.wq_ref
  15.1 28.2 %all-gather.4.cloned.1.call-done.lhs_ref = bf16[1536,1024]{1,0:T(8,128)(2,1)} async-done(((bf16[192,1024]{1,0:T(8,128)(2,1)}), bf16[1536,1024]{1,0:T(8,128)(2,1)}) %all-gather.4.cloned.1.call-update) | async-done | bytes 3145744 | tf_op jit(solution)/shard_map/all_gather | solution.py:161
  43.4 20.0 %shard_map.162 = f32[6144,768]{1,0:T(8,128)} custom-call(bf16[1536,1024]{1,0:T(8,128)(2,1)} %all-gather.4.cloned.1.call-done.lhs_ref, bf16[512,1024]{1,0:T(8,128)(2,1)} %multiply_convert_fusion.1.wq_ref, bf16[512,256]{1,0:T(8,128)(2,1)} %multiply_convert_fusion.2.wkv_ref, bf16[1024,512]{1,0:T(8,128)(2,1)} %wo_ref.1), custom_call_target="tpu_custom_call" | custom-call | flops 4026531840 | bytes 24379392 | tf_op jit(solution)/shard_map/pallas_call | solution.py:103
  63.5 121.2 %reduce-scatter.3.cloned.1.call-done = f32[384,768]{1,0:T(8,128)} async-done(((f32[6144,768]{1,0:T(8,128)}), f32[384,768]{1,0:T(8,128)}) %reduce-scatter.3.cloned.1.call-update) | async-done | bytes 1179664 | tf_op jit(solution)/shard_map/reduce_scatter | solution.py:174
  184.7 1.2 fusion.82
  185.9 1.0 fusion.84
  186.9 0.8 fusion.77
  187.7 1.7 fusion.85
  189.5 0.2 all-gather.8.cloned.1.call-start
  189.8 2.5 gather_fusion.2
  192.4 0.8 multiply_cosine_fusion.1
  193.2 1.6 compare_and_fusion
  194.8 0.2 reshape.475
  195.1 0.2 copy.120
  195.4 0.5 fusion.116
  196.0 37.0 %all-gather.6.cloned.1.call-done = bf16[6144,128]{1,0:T(8,128)(2,1)} async-done(((bf16[384,128]{1,0:T(8,128)(2,1)}), bf16[6144,128]{1,0:T(8,128)(2,1)}) %all-gather.6.cloned.1.call-update) | async-done | bytes 1572880 | tf_op jit(solution)/shard_map/all_gather | solution.py:190
  233.0 1.2 fusion.115
  234.2 2.4 convolution_bitcast_fusion
  236.6 3.1 fusion.11
  239.8 7.4 %fusion.26 = f32[384,2,128]{2,0,1:T(8,128)S(1)} fusion(f32[1152,384,2]{1,0,2:T(8,128)} %get-tuple-element.78, f32[2,384,1152]{1,2,0:T(8,128)} %convolution_bitcast_fusion, bf16[1536,128]{1,0:T(8,128)(2,1)S(1)} %bitcast.162, s32[]{:T(128)S(6)} %min.4, f32[2,384]{1,0:T(2,128)S(1)} %get-tuple-element.77, pred[384,1152]{0,1:T(8,128)(4,1)S(1)} %copy-done.15), kind=kOutput, calls=%fused_computation.38 | convolution fusion | flops 238880640 | bytes 15734788 | tf_op jit(solution)/shard_map/hqk,kd->qhd/dot_general | solution.py:228
  247.1 8.4 %convolution_bitcast_fusion.2 = f32[1152,1,128]{0,2,1:T(8,128)S(1)} fusion(f32[1152,384,2]{1,0,2:T(8,128)} %get-tuple-element.78, f32[2,384,1152]{1,2,0:T(8,128)} %convolution_bitcast_fusion, bf16[384,2,64]{2,0,1:T(8,128)(2,1)} %copy-done.17, bf16[384,2,64]{2,0,1:T(8,128)(2,1)S(1)} %get-tuple-element.63, f32[2,384]{1,0:T(2,128)S(1)} %get-tuple-element.77, ...), kind=kOutput, calls=%fused_computation.23 | convolution fusion | flops 239273856 | bytes 8309760 | tf_op jit(solution)/shard_map/hqk,qhd->kd/dot_general | solution.py:231
  255.5 4.0 fusion.9
  259.5 1.0 fusion.40
  260.5 0.2 add_convert_fusion
  260.8 0.2 copy.89
  261.0 1.3 fusion.61
  262.5 1.3 copy.95
  263.8 0.3 reduce-scatter.5.cloned.1.call-start
  264.1 105.5 %all-gather.8.cloned.1.call-done = bf16[30848,256]{1,0:T(8,128)(2,1)} async-done(((bf16[1928,256]{1,0:T(8,128)(2,1)}), bf16[30848,256]{1,0:T(8,128)(2,1)}) %all-gather.8.cloned.1.call-update) | async-done | bytes 15794192 | tf_op jit(solution)/shard_map/all_gather | solution.py:259
  369.6 5.7 %convert_reduce_fusion = f32[4,1152,256]{2,1,0:T(8,128)S(1)} fusion(bf16[16,1928,256]{2,1,0:T(8,128)(2,1)} %bitcast.144), kind=kLoop, calls=%fused_computation.4 | loop fusion | flops 8257536 | bytes 14155776 | tf_op jit(solution)/shard_map/reduce_sum | solution.py:278
  375.2 3.3 fusion.114
  378.7 0.2 fusion.43
  378.9 0.2 fusion.35
  379.1 0.3 fusion.33
  379.4 2.4 copy.98
  381.9 0.8 copy.122
  382.7 1.7 copy-done.4
  384.3 1.8 fusion.117
  386.2 0.6 convolution_add_fusion.1
  386.8 0.6 fusion.8
  387.4 2.7 copy.96
  390.1 0.8 copy.121
  390.9 1.6 copy-done.6
  392.5 1.8 convolution_convert_fusion
  394.3 2.1 pad_maximum_fusion
  396.5 0.8 slice.228
  397.5 3.2 fusion.54
  400.7 3.2 fusion.57
  403.9 3.1 fusion.24
  407.1 3.3 fusion.108
  410.4 21.8 %reduce-scatter.5.cloned.1.call-done = bf16[192,1024]{1,0:T(8,128)(2,1)} async-done(((bf16[1536,1024]{1,0:T(8,128)(2,1)}), bf16[192,1024]{1,0:T(8,128)(2,1)}) %reduce-scatter.5.cloned.1.call-update) | async-done | bytes 393232 | tf_op jit(solution)/shard_map/reduce_scatter | solution.py:308
  432.2 1.1 convert_element_type.128
  433.3 0.2 fusion.53
  433.5 10.4 %psum.21 = f32[192]{0:T(256)S(1)} all-reduce(f32[192]{0:T(256)S(1)} %get-tuple-element.56), channel_id=1, replica_groups=mesh['row'=4,'col'=8,'seq'=4] {'seq'}, use_global_device_ids=true, to_apply=%region_6.7 | all-reduce | flops 192 | bytes 1536 | tf_op jit(solution)/shard_map/psum | solution.py:320
  443.9 10.7 %psum.22 = f32[192]{0:T(256)S(1)} all-reduce(f32[192]{0:T(256)S(1)} %psum.21), channel_id=1, replica_groups=mesh['row'=4,'col'=8,'seq'=4] {'row'}, use_global_device_ids=true, to_apply=%region_7.8 | all-reduce | flops 192 | bytes 1536 | tf_op jit(solution)/shard_map/psum | solution.py:320
  454.6 0.9 fusion.51
  455.5 13.0 %psum.23 = f32[512]{0:T(512)} all-reduce(f32[512]{0:T(512)S(1)} %get-tuple-element.55), channel_id=1, replica_groups=mesh['row'=4,'col'=8,'seq'=4] {'col'}, use_global_device_ids=true, to_apply=%region_9.10 | all-reduce | flops 512 | bytes 4096 | tf_op jit(solution)/shard_map/psum | solution.py:326
  (75 shorter events, 1.6 us)
Async XLA Ops:
  7.2 3.9 copy-start
  7.2 5.0 %copy-start.12 = (bf16[192,512]{1,0:T(8,128)(2,1)S(1)}, bf16[192,512]{1,0:T(8,128)(2,1)}, u32[]{:S(2)}) copy-start(bf16[192,512]{1,0:T(8,128)(2,1)} %param.29) | copy-start | bytes 589828
  7.2 5.9 %copy-start.18 = (f32[512]{0:T(512)S(1)}, f32[512]{0:T(512)}, u32[]{:S(2)}) copy-start(f32[512]{0:T(512)} %param.24) | copy-start | bytes 6148
  7.2 5.9 %copy-start.14 = (bf16[512,128]{1,0:T(8,128)(2,1)S(1)}, bf16[512,128]{1,0:T(8,128)(2,1)}, u32[]{:S(2)}) copy-start(bf16[512,128]{1,0:T(8,128)(2,1)} %param.26) | copy-start | bytes 393220
  7.2 5.9 %copy-start.13 = (bf16[512,128]{1,0:T(8,128)(2,1)S(1)}, bf16[512,128]{1,0:T(8,128)(2,1)}, u32[]{:S(2)}) copy-start(bf16[512,128]{1,0:T(8,128)(2,1)} %param.27) | copy-start | bytes 393220
  7.2 6.7 %copy-start.10 = (bf16[512,1024]{1,0:T(8,128)(2,1)S(1)}, bf16[512,1024]{1,0:T(8,128)(2,1)}, u32[]{:S(2)}) copy-start(bf16[512,1024]{1,0:T(8,128)(2,1)} %param.25) | copy-start | bytes 3145732
  7.2 36.1 %all-gather.4.cloned.1.call-start = ((), (), s32[]{:S(2)}) async-start(), calls=%async_computation.2 | async-start | bytes 3538944 | tf_op jit(solution)/shard_map/all_gather | solution.py:161
  13.0 171.7 %reduce-scatter.3.cloned.1.call-start = ((), (), s32[]{:S(2)}) async-start(), calls=%async_computation.3 | async-start | bytes 20054016 | tf_op jit(solution)/shard_map/reduce_scatter | solution.py:174
  63.4 126.4 %copy-start.2 = (s32[1536]{0:T(1024)S(1)}, s32[1536]{0:T(1024)}, u32[]{:S(2)}) copy-start(s32[1536]{0:T(1024)} %param.21) | copy-start | bytes 18436
  63.4 169.6 %all-gather.6.cloned.1.call-start = ((), (), s32[]{:S(2)}) async-start(), calls=%async_computation.4 | async-start | bytes 1671168 | tf_op jit(solution)/shard_map/all_gather | solution.py:190
  184.7 10.0 %copy-start.8 = (f32[384,768]{1,0:T(8,128)S(1)}, f32[384,768]{1,0:T(8,128)}, u32[]{:S(2)}) copy-start(f32[384,768]{1,0:T(8,128)} %reduce-scatter.3.cloned.1.call-done) | copy-start | bytes 3538948
  189.5 180.1 %all-gather.8.cloned.1.call-start = ((), (), s32[]{:S(2)}) async-start(), calls=%async_computation.5 | async-start | bytes 16781312 | tf_op jit(solution)/shard_map/all_gather | solution.py:259
  196.0 43.8 %copy-start.17 = (bf16[384,2,64]{2,0,1:T(8,128)(2,1)}, bf16[384,2,64]{2,0,1:T(8,128)(2,1)S(1)}, u32[]{:S(2)}) copy-start(bf16[384,2,64]{2,0,1:T(8,128)(2,1)S(1)} %get-tuple-element.64) | copy-start | bytes 294916
  196.0 40.6 %copy-start.15 = (pred[384,1152]{0,1:T(8,128)(4,1)S(1)}, pred[384,1152]{0,1:T(8,128)(4,1)}, u32[]{:S(2)}) copy-start(pred[384,1152]{0,1:T(8,128)(4,1)} %compare_and_fusion) | copy-start | bytes 1327108
  255.5 4.0 copy-start.19
  260.5 1.9 copy-start.16
  263.8 168.4 %reduce-scatter.5.cloned.1.call-start = ((), (), s32[]{:S(2)}) async-start(), calls=%async_computation.6 | async-start | bytes 3538944 | tf_op jit(solution)/shard_map/reduce_scatter | solution.py:308
  381.9 2.5 copy-start.11
  382.7 1.7 copy-start.4
  390.1 2.4 copy-start.9
  390.9 1.6 copy-start.6
  397.5 6.4 %copy-start.7 = (bf16[192,8,4,256]{3,1,2,0:T(8,128)(2,1)S(1)}, bf16[192,8,4,256]{3,1,2,0:T(8,128)(2,1)}, u32[]{:S(2)}) copy-start(bf16[192,8,4,256]{3,1,2,0:T(8,128)(2,1)} %copy-done.6) | copy-start | bytes 9437188
  400.7 3.2 copy-start.3
  403.9 3.1 copy-start.5
  407.1 61.4 %copy-start.1 = (bf16[1024,512]{1,0:T(8,128)(2,1)S(1)}, bf16[1024,512]{1,0:T(8,128)(2,1)}, u32[]{:S(2)}) copy-start(bf16[1024,512]{1,0:T(8,128)(2,1)} %param.23) | copy-start | bytes 3145732
Sparse Core Ops, SparseCore 0:
  13.1 30.1 all-gather.3
  63.5 121.1 reduce-scatter.2
  189.6 43.3 all-gather.5
  263.9 105.5 all-gather.7
  396.6 35.5 reduce-scatter.4

commit v3 on v2

--- a/solution.py
+++ b/solution.py
@@ -305,6 +305,13 @@
     total_term = total_term + jnp.einsum(
         "ln,dn->ld", kv_grad_all[:, kv_width:], w_value, preferred_element_type=jnp.float32
     )
+    emb_inv_all = emb_all_f * inv_all[:, None]
+    gain_terms = jnp.sum(total_term * emb_inv_all, axis=0)
+    dot_terms = jnp.sum(total_term * (emb_all_f * norm_gain[None, :]), axis=1)
+    col_terms = lax.psum(jnp.concatenate([gain_terms, dot_terms]), "col")
+    grad_gain = col_terms[:feat]
+    own_dots = lax.dynamic_slice(col_terms[feat:], (col_index * own_len,), (own_len,))
+    total_dot = lax.psum(lax.psum(own_dots, "seq"), "row")
     col_sum = lax.psum_scatter(
         jnp.concatenate([branch_part, total_term], axis=1).astype(jnp.bfloat16),
         "col",
@@ -317,13 +324,11 @@
 
     inverse = lax.dynamic_slice(inv_all, (col_index * own_len,), (own_len,))
     scaled_grad = grad_normed * norm_gain[None, :]
-    total_dot = lax.psum(lax.psum(jnp.sum(scaled_grad * residual, axis=1), "seq"), "row")
     grad_input = (
         out_grad.astype(jnp.float32)
         + inverse[:, None] * scaled_grad
         - residual * (inverse**3 * total_dot / D)[:, None]
     ).astype(jnp.bfloat16)
-    grad_gain = lax.psum(jnp.sum(grad_normed * residual * inverse[:, None], axis=0), "col")
     return (layer_out, grad_input, grad_gain, grad_wq, grad_wk, grad_wv, grad_wo)
 
 

time: 480 us -> 459 us (0.956)
  waiting for transfers between devices: 314 us -> 292 us
  local copies, waits for them, and re-layouts: 23.9 us -> 28.7 us
    reduce_scatter x1, waiting for transfers between devices: 21.8 us -> 0.01 us  [per_device(): lax.psum_scatter(jnp.concatenate([branch_part, total_term], axis=1).astyp...]
  transfers between devices with their start and end apart: 5 -> 5, of which waited for: 5 -> 4; matrix products, arithmetic and copies ran while one was open for 5% -> 5% of each run, Pallas kernels for 0% -> 0%
where the time goes in v3:
time: 459 us; the launch traced here: 458 us
  waiting for transfers between devices  292 us (64%)
  matrix products  44.4 us (10%)
  blocking collectives  33.7 us (7%)
  local copies, waits for them, and re-layouts  28.7 us (6%)
  other arithmetic  24.3 us (5%)
  Pallas kernels  20 us (4%)
  between operations  14.4 us (3%)
    reduce_scatter x1, waiting for transfers between devices, per_device(): lax.psum_scatter(blocks, ('row', 'seq'), scatter_dimension=0, tiled=True)  121 us
    all_gather x1, waiting for transfers between devices, per_device(): lax.all_gather(jnp.concatenate([attn_out, grad_query_round, kv_grad_win,...  105 us
    all_gather x1, waiting for transfers between devices, per_device(): lax.all_gather(kv_piece, ('row', 'seq'), axis=0, tiled=True)  37 us
    all_gather x1, waiting for transfers between devices, per_device(): lax.all_gather(jnp.concatenate([embedded, out_grad], axis=1), 'col', axis...  28.2 us
    pallas_call x1, Pallas kernels, project_blocks(): pl.pallas_call(project_kernel, grid=(n_row, n_seq), in_specs=[pl.BlockSpe...  20 us
    psum x2, blocking collectives, per_device(): total_dot = lax.psum(lax.psum(own_dots, 'seq'), 'row')  18.9 us
    psum x1, blocking collectives, per_device(): col_terms = lax.psum(jnp.concatenate([gain_terms, dot_terms]), 'col')  14.8 us
  transfers between devices with their start and end apart: 5, of which 4 were waited for; matrix products, arithmetic and copies ran while one was open for 5% of the time, Pallas kernels for 0%

profile of v3, /device:TPU:0, one launch (start us, length us, event | category | flops | bytes accessed | tf_op | source)
XLA Modules:
  0.0 457.9 jit_solution(6838377807037389879)
XLA Ops:
  7.3 0.9 compare_select_fusion.2
  8.1 0.7 compare_and_fusion.1
  8.9 2.2 gather_fusion
  11.0 1.0 gather_fusion.1
  12.2 0.8 pad_maximum_fusion.2
  13.1 0.8 multiply_convert_fusion.1.wkv_ref
  13.9 1.2 multiply_convert_fusion.wq_ref
  15.1 28.2 %all-gather.4.cloned.1.call-done.lhs_ref = bf16[1536,1024]{1,0:T(8,128)(2,1)} async-done(((bf16[192,1024]{1,0:T(8,128)(2,1)}), bf16[1536,1024]{1,0:T(8,128)(2,1)}) %all-gather.4.cloned.1.call-update) | async-done | bytes 3145744 | tf_op jit(solution)/shard_map/all_gather | solution.py:161
  43.4 20.0 %shard_map.162 = f32[6144,768]{1,0:T(8,128)} custom-call(bf16[1536,1024]{1,0:T(8,128)(2,1)} %all-gather.4.cloned.1.call-done.lhs_ref, bf16[512,1024]{1,0:T(8,128)(2,1)} %multiply_convert_fusion.wq_ref, bf16[512,256]{1,0:T(8,128)(2,1)} %multiply_convert_fusion.1.wkv_ref, bf16[1024,512]{1,0:T(8,128)(2,1)} %wo_ref.1), custom_call_target="tpu_custom_call" | custom-call | flops 4026531840 | bytes 24379392 | tf_op jit(solution)/shard_map/pallas_call | solution.py:103
  63.5 121.2 %reduce-scatter.3.cloned.1.call-done = f32[384,768]{1,0:T(8,128)} async-done(((f32[6144,768]{1,0:T(8,128)}), f32[384,768]{1,0:T(8,128)}) %reduce-scatter.3.cloned.1.call-update) | async-done | bytes 1179664 | tf_op jit(solution)/shard_map/reduce_scatter | solution.py:174
  184.7 1.2 fusion.86
  185.9 1.0 fusion.88
  186.9 0.8 fusion.81
  187.7 1.7 fusion.89
  189.5 0.2 all-gather.8.cloned.1.call-start
  189.8 2.5 gather_fusion.2
  192.4 0.8 multiply_cosine_fusion.1
  193.2 1.6 compare_and_fusion
  194.9 0.2 reshape.475
  195.1 0.2 copy.120
  195.4 0.5 fusion.123
  196.0 37.0 %all-gather.6.cloned.1.call-done = bf16[6144,128]{1,0:T(8,128)(2,1)} async-done(((bf16[384,128]{1,0:T(8,128)(2,1)}), bf16[6144,128]{1,0:T(8,128)(2,1)}) %all-gather.6.cloned.1.call-update) | async-done | bytes 1572880 | tf_op jit(solution)/shard_map/all_gather | solution.py:190
  233.0 1.2 fusion.122
  234.2 2.5 convolution_bitcast_fusion
  236.7 3.1 fusion.16
  239.8 7.4 %fusion.31 = f32[384,2,128]{2,0,1:T(8,128)S(1)} fusion(f32[1152,384,2]{1,0,2:T(8,128)} %get-tuple-element.81, f32[2,384,1152]{1,2,0:T(8,128)} %convolution_bitcast_fusion, bf16[1536,128]{1,0:T(8,128)(2,1)S(1)} %bitcast.162, s32[]{:T(128)S(6)} %min.4, f32[2,384]{1,0:T(2,128)S(1)} %get-tuple-element.80, pred[384,1152]{0,1:T(8,128)(4,1)S(1)} %copy-done.16), kind=kOutput, calls=%fused_computation.44 | convolution fusion | flops 238880640 | bytes 15734788 | tf_op jit(solution)/shard_map/hqk,kd->qhd/dot_general | solution.py:228
  247.2 7.2 %convolution_bitcast_fusion.2 = f32[1152,1,128]{0,2,1:T(8,128)S(1)} fusion(f32[1152,384,2]{1,0,2:T(8,128)} %get-tuple-element.81, f32[2,384,1152]{1,2,0:T(8,128)} %convolution_bitcast_fusion, bf16[384,2,64]{2,0,1:T(8,128)(2,1)S(1)} %get-tuple-element.67, bf16[384,2,64]{2,0,1:T(8,128)(2,1)S(1)} %get-tuple-element.66, f32[2,384]{1,0:T(2,128)S(1)} %get-tuple-element.80, ...), kind=kOutput, calls=%fused_computation.29 | convolution fusion | flops 239273856 | bytes 8309760 | tf_op jit(solution)/shard_map/hqk,qhd->kd/dot_general | solution.py:231
  254.5 3.3 fusion.14
  257.8 1.6 fusion.45
  259.4 0.2 add_convert_fusion
  259.8 0.2 copy.89
  259.9 1.3 fusion.65
  261.4 1.3 copy.95
  262.7 0.3 reduce-scatter.5.cloned.1.call-start
  263.0 105.5 %all-gather.8.cloned.1.call-done = bf16[30848,256]{1,0:T(8,128)(2,1)} async-done(((bf16[1928,256]{1,0:T(8,128)(2,1)}), bf16[30848,256]{1,0:T(8,128)(2,1)}) %all-gather.8.cloned.1.call-update) | async-done | bytes 15794192 | tf_op jit(solution)/shard_map/all_gather | solution.py:259
  368.5 5.7 %convert_reduce_fusion = f32[4,1152,256]{2,1,0:T(8,128)S(1)} fusion(bf16[16,1928,256]{2,1,0:T(8,128)(2,1)} %bitcast.144), kind=kLoop, calls=%fused_computation.4 | loop fusion | flops 8257536 | bytes 14155776 | tf_op jit(solution)/shard_map/reduce_sum | solution.py:278
  374.1 0.8 slice.236
  375.0 6.3 %fusion.121 = (bf16[16,384,256]{2,1,0:T(8,128)(2,1)}, bf16[16,384,256]{2,1,0:T(8,128)(2,1)}) fusion(bf16[16,1928,256]{2,1,0:T(8,128)(2,1)} %bitcast.146), kind=kLoop, calls=%fused_computation.166 | loop fusion | bytes 12582912 | tf_op jit(solution)/shard_map/slice | solution.py:270
  381.5 0.2 fusion.48
  381.6 0.2 fusion.40
  381.9 0.3 fusion.38
  382.3 4.3 copy.98
  386.6 0.8 copy.122
  387.4 0.4 copy-done.13
  387.9 1.8 fusion.124
  389.7 0.7 copy-done.3
  390.4 2.4 copy.96
  392.9 0.8 copy.121
  393.6 0.4 copy-done.11
  394.1 2.1 convolution_convert_fusion
  396.2 0.6 convolution_add_fusion.1
  396.8 1.3 copy-done.4
  398.0 1.9 fusion.10
  399.9 2.1 pad_maximum_fusion
  402.1 14.8 %psum.21 = f32[2048]{0:T(1024)S(1)} all-reduce(f32[2048]{0:T(1024)S(1)} %pad_maximum_fusion.7), channel_id=1, replica_groups=mesh['row'=4,'col'=8,'seq'=4] {'col'}, use_global_device_ids=true, to_apply=%region_7.8 | all-reduce | flops 2048 | bytes 16384 | tf_op jit(solution)/shard_map/psum | solution.py:311
  416.9 0.6 slice.243
  417.6 10.4 %psum.22 = f32[192]{0:T(256)S(1)} all-reduce(f32[192]{0:T(256)S(1)} %dynamic_slice.19), channel_id=1, replica_groups=mesh['row'=4,'col'=8,'seq'=4] {'seq'}, use_global_device_ids=true, to_apply=%region_8.9 | all-reduce | flops 192 | bytes 1536 | tf_op jit(solution)/shard_map/psum | solution.py:314
  428.0 8.5 %psum.23 = f32[192]{0:T(256)S(1)} all-reduce(f32[192]{0:T(256)S(1)} %psum.22), channel_id=1, replica_groups=mesh['row'=4,'col'=8,'seq'=4] {'row'}, use_global_device_ids=true, to_apply=%region_9.10 | all-reduce | flops 192 | bytes 1536 | tf_op jit(solution)/shard_map/psum | solution.py:314
  436.5 3.2 fusion.58
  439.7 3.2 fusion.61
  442.9 3.1 fusion.29
  446.1 3.3 fusion.114
  449.4 1.1 convert_element_type.128
  450.5 0.9 fusion.55
  (81 shorter events, 1.8 us)
Async XLA Ops:
  7.2 3.9 copy-start
  7.2 5.0 %copy-start.14 = (bf16[192,512]{1,0:T(8,128)(2,1)S(1)}, bf16[192,512]{1,0:T(8,128)(2,1)}, u32[]{:S(2)}) copy-start(bf16[192,512]{1,0:T(8,128)(2,1)} %param.29) | copy-start | bytes 589828
  7.2 5.9 %copy-start.20 = (f32[512]{0:T(512)S(1)}, f32[512]{0:T(512)}, u32[]{:S(2)}) copy-start(f32[512]{0:T(512)} %param.24) | copy-start | bytes 6148
  7.2 5.9 %copy-start.15 = (bf16[512,128]{1,0:T(8,128)(2,1)S(1)}, bf16[512,128]{1,0:T(8,128)(2,1)}, u32[]{:S(2)}) copy-start(bf16[512,128]{1,0:T(8,128)(2,1)} %param.26) | copy-start | bytes 393220
  7.2 5.9 %copy-start.18 = (bf16[512,128]{1,0:T(8,128)(2,1)S(1)}, bf16[512,128]{1,0:T(8,128)(2,1)}, u32[]{:S(2)}) copy-start(bf16[512,128]{1,0:T(8,128)(2,1)} %param.27) | copy-start | bytes 393220
  7.2 6.7 %copy-start.12 = (bf16[512,1024]{1,0:T(8,128)(2,1)S(1)}, bf16[512,1024]{1,0:T(8,128)(2,1)}, u32[]{:S(2)}) copy-start(bf16[512,1024]{1,0:T(8,128)(2,1)} %param.25) | copy-start | bytes 3145732
  7.2 36.1 %all-gather.4.cloned.1.call-start = ((), (), s32[]{:S(2)}) async-start(), calls=%async_computation.2 | async-start | bytes 3538944 | tf_op jit(solution)/shard_map/all_gather | solution.py:161
  13.0 171.7 %reduce-scatter.3.cloned.1.call-start = ((), (), s32[]{:S(2)}) async-start(), calls=%async_computation.3 | async-start | bytes 20054016 | tf_op jit(solution)/shard_map/reduce_scatter | solution.py:174
  63.4 126.4 %copy-start.2 = (s32[1536]{0:T(1024)S(1)}, s32[1536]{0:T(1024)}, u32[]{:S(2)}) copy-start(s32[1536]{0:T(1024)} %param.21) | copy-start | bytes 18436
  63.4 169.6 %all-gather.6.cloned.1.call-start = ((), (), s32[]{:S(2)}) async-start(), calls=%async_computation.4 | async-start | bytes 1671168 | tf_op jit(solution)/shard_map/all_gather | solution.py:190
  184.7 10.1 %copy-start.10 = (f32[384,768]{1,0:T(8,128)S(1)}, f32[384,768]{1,0:T(8,128)}, u32[]{:S(2)}) copy-start(f32[384,768]{1,0:T(8,128)} %reduce-scatter.3.cloned.1.call-done) | copy-start | bytes 3538948
  189.5 179.0 %all-gather.8.cloned.1.call-start = ((), (), s32[]{:S(2)}) async-start(), calls=%async_computation.5 | async-start | bytes 16781312 | tf_op jit(solution)/shard_map/all_gather | solution.py:259
  196.0 40.7 %copy-start.16 = (pred[384,1152]{0,1:T(8,128)(4,1)S(1)}, pred[384,1152]{0,1:T(8,128)(4,1)}, u32[]{:S(2)}) copy-start(pred[384,1152]{0,1:T(8,128)(4,1)} %compare_and_fusion) | copy-start | bytes 1327108
  254.5 3.3 copy-start.21
  259.4 1.9 copy-start.17
  262.7 186.7 %reduce-scatter.5.cloned.1.call-start = ((), (), s32[]{:S(2)}) async-start(), calls=%async_computation.6 | async-start | bytes 3538944 | tf_op jit(solution)/shard_map/reduce_scatter | solution.py:315
  386.6 1.2 copy-start.13
  387.4 2.3 copy-start.6
  387.9 2.6 copy-start.3
  392.8 1.2 copy-start.11
  393.6 2.5 copy-start.8
  396.1 1.9 copy-start.4
  396.2 1.9 copy-start.19
  436.5 6.4 %copy-start.9 = (bf16[192,8,4,256]{3,1,2,0:T(8,128)(2,1)S(1)}, bf16[192,8,4,256]{3,1,2,0:T(8,128)(2,1)}, u32[]{:S(2)}) copy-start(bf16[192,8,4,256]{3,1,2,0:T(8,128)(2,1)} %copy-done.8) | copy-start | bytes 9437188
  439.7 3.2 copy-start.5
  442.9 3.1 copy-start.7
  446.1 5.3 %copy-start.1 = (bf16[1024,512]{1,0:T(8,128)(2,1)S(1)}, bf16[1024,512]{1,0:T(8,128)(2,1)}, u32[]{:S(2)}) copy-start(bf16[1024,512]{1,0:T(8,128)(2,1)} %param.23) | copy-start | bytes 3145732
Sparse Core Ops, SparseCore 0:
  13.1 30.1 all-gather.3
  63.5 121.1 reduce-scatter.2
  189.6 43.3 all-gather.5
  262.9 105.5 all-gather.7
  402.2 35.6 reduce-scatter.4

commit v4 on v3

--- a/solution.py
+++ b/solution.py
@@ -82,13 +82,8 @@
     og = lhs_ref[:, feat:]
     out_ref[:, :qw] = jnp.dot(emb, wq_ref[...], preferred_element_type=jnp.float32)
     out_ref[:, qw : qw + kw] = jnp.dot(emb, wkv_ref[...], preferred_element_type=jnp.float32)
-    out_ref[:, qw + kw : qw + kw + ow] = lax.dot_general(
+    out_ref[:, qw + kw :] = lax.dot_general(
         og, wo_ref[...], (((1,), (1,)), ((), ())), preferred_element_type=jnp.float32
-    )
-    emb_f = emb.astype(jnp.float32)
-    squares = jnp.sum(emb_f * emb_f, axis=1, keepdims=True)
-    out_ref[:, qw + kw + ow :] = jnp.broadcast_to(
-        squares, (squares.shape[0], out_ref.shape[1] - qw - kw - ow)
     )
 
 
@@ -169,15 +164,16 @@
     wkv_gain = (
         jnp.concatenate([w_key, w_value], axis=1).astype(jnp.float32) * gain_col
     ).astype(jnp.bfloat16)
-    out_w = part_w + HD + part_w + 128
+    out_w = part_w + HD + part_w
+    squares = lax.psum(lax.psum(jnp.sum(emb_all_f * emb_all_f, axis=1), "seq"), "row")
+    inv_all = lax.rsqrt(squares / D + epsilon)
     blocks = project_blocks(both_all, wq_gain, wkv_gain, w_out, n_row, n_seq, out_w)
     got = lax.psum_scatter(blocks, ("row", "seq"), scatter_dimension=0, tiled=True)
 
     q_raw = got[:, :part_w]
     kv_raw = got[:, part_w : part_w + HD]
     d_raw = got[:, part_w + HD : 2 * part_w + HD]
-    sq_q = got[:, 2 * part_w + HD]
-    inv_q = lax.rsqrt(sq_q / D + epsilon)
+    inv_q = lax.dynamic_slice(inv_all, (row_index * quarter_len,), (quarter_len,))
 
     query_pos = row_index * quarter_len + jnp.arange(quarter_len, dtype=jnp.int32)
     queries = rope_round(q_raw * inv_q[:, None], query_pos)
@@ -248,25 +244,13 @@
         .reshape(quarter_len, part_w)
         .astype(jnp.bfloat16)
     )
-    inv_hi = inv_q.astype(jnp.bfloat16)
-    inv_lo = (inv_q - inv_hi.astype(jnp.float32)).astype(jnp.bfloat16)
-    inv_rows = -(-2 * quarter_len // part_w)
-    inv_rows = inv_rows + (-inv_rows) % 8
-    inv_pack = jnp.pad(
-        jnp.concatenate([inv_hi, inv_lo]), (0, inv_rows * part_w - 2 * quarter_len)
-    ).reshape(inv_rows, part_w)
-    back_rows = 2 * quarter_len + win + inv_rows
+    back_rows = 2 * quarter_len + win
     back_all = lax.all_gather(
-        jnp.concatenate([attn_out, grad_query_round, kv_grad_win, inv_pack], axis=0),
+        jnp.concatenate([attn_out, grad_query_round, kv_grad_win], axis=0),
         ("row", "seq"),
         axis=0,
         tiled=True,
     ).reshape(n_rs, back_rows, part_w)
-    inv_parts = back_all[:, 2 * quarter_len + win :].reshape(n_rs, -1)
-    inv_blocks = inv_parts[:, :quarter_len].astype(jnp.float32) + inv_parts[
-        :, quarter_len : 2 * quarter_len
-    ].astype(jnp.float32)
-    inv_all = inv_blocks.reshape(n_row, n_seq, quarter_len)[:, 0].reshape(seq_len)
     out_all = from_blocks(back_all[:, :quarter_len].reshape(n_row, n_seq, quarter_len, part_w))
     grad_query_all = from_blocks(
         back_all[:, quarter_len : 2 * quarter_len].reshape(n_row, n_seq, quarter_len, part_w)

time: 459 us -> 529 us (1.15)
  local copies, waits for them, and re-layouts: 28.7 us -> 84.6 us
  waiting for transfers between devices: 292 us -> 252 us
  other arithmetic: 24.3 us -> 49.9 us
  blocking collectives: 33.7 us -> 55.2 us
    reduce_scatter x1, waiting for transfers between devices: 121 us -> 82.7 us  [per_device(): lax.psum_scatter(blocks, ('row', 'seq'), scatter_dimension=0, tiled=True)]
    unnamed x47 -> x48, local copies, waits for them, and re-layouts: 4.48 us -> 32 us
    psum x0 -> x2, blocking collectives: none -> 21.5 us  [the longest x1 10.9 us: per_device(): lax.psum(lax.psum(jnp.sum(emb_all_f * emb_all_f, axis=1), 'seq'), 'row')]
    reshape x5 -> x1, local copies, waits for them, and re-layouts: 6.89 us -> 21.7 us  [per_device(): kv_terms = back_all[:, 2 * quarter_len:2 * quarter_len + win].astype(jnp....]
    reduce_sum x1, other arithmetic: 5.68 us -> 18.1 us  [per_device(): kv_terms = back_all[:, 2 * quarter_len:2 * quarter_len + win].astype(jnp....]
    reshape x0 -> x1, other arithmetic: none -> 11.6 us  [per_device(): kv_terms = back_all[:, 2 * quarter_len:2 * quarter_len + win].astype(jnp....]
    slice x2 -> x1, local copies, waits for them, and re-layouts: 0.87 us -> 10.1 us  [per_device(): kv_grad_f = kv_grad_f.at[first:first + win].add(kv_terms[quarter])]
    transpose x0 -> x2, local copies, waits for them, and re-layouts: none -> 8.64 us  [from_blocks(): return blocks.transpose(0, 2, 1, 3).reshape(n_row * rows, n_seq * w)]
where the time goes in v4:
time: 529 us; the launch traced here: 524 us
  waiting for transfers between devices  252 us (48%)
  local copies, waits for them, and re-layouts  84.6 us (16%)
  blocking collectives  55.2 us (10%)
  other arithmetic  49.9 us (9%)
  matrix products  47.3 us (9%)
  Pallas kernels  19.1 us (4%)
  between operations  14.6 us (3%)
    all_gather x1, waiting for transfers between devices, per_device(): lax.all_gather(jnp.concatenate([attn_out, grad_query_round, kv_grad_win],...  105 us
    reduce_scatter x1, waiting for transfers between devices, per_device(): lax.psum_scatter(blocks, ('row', 'seq'), scatter_dimension=0, tiled=True)  82.7 us
    all_gather x1, waiting for transfers between devices, per_device(): lax.all_gather(kv_piece, ('row', 'seq'), axis=0, tiled=True)  36.2 us
    unnamed x48, local copies, waits for them, and re-layouts  32 us
    all_gather x1, waiting for transfers between devices, per_device(): lax.all_gather(jnp.concatenate([embedded, out_grad], axis=1), 'col', axis...  28.2 us
    reshape x1, local copies, waits for them, and re-layouts, per_device(): kv_terms = back_all[:, 2 * quarter_len:2 * quarter_len + win].astype(jnp....  21.7 us
    pallas_call x1, Pallas kernels, project_blocks(): pl.pallas_call(project_kernel, grid=(n_row, n_seq), in_specs=[pl.BlockSpe...  19.1 us
    psum x2, blocking collectives, per_device(): total_dot = lax.psum(lax.psum(own_dots, 'seq'), 'row')  18.9 us
  transfers between devices with their start and end apart: 5, of which 4 were waited for; matrix products, arithmetic and copies ran while one was open for 5% of the time, Pallas kernels for 0%

profile of v4, /device:TPU:0, one launch (start us, length us, event | category | flops | bytes accessed | tf_op | source)
XLA Modules:
  0.0 524.0 jit_solution(13458075443750411590)
XLA Ops:
  7.3 0.9 compare_and_fusion.1
  8.1 0.7 compare_select_fusion.2
  8.9 2.2 gather_fusion
  11.0 1.0 gather_fusion.1
  12.2 0.8 pad_maximum_fusion.1
  13.1 0.8 multiply_convert_fusion.1.wkv_ref
  13.9 1.2 multiply_convert_fusion.wq_ref
  15.1 28.2 %all-gather.4.cloned.1.call-done.lhs_ref = bf16[1536,1024]{1,0:T(8,128)(2,1)} async-done(((bf16[192,1024]{1,0:T(8,128)(2,1)}), bf16[1536,1024]{1,0:T(8,128)(2,1)}) %all-gather.4.cloned.1.call-update) | async-done | bytes 3145744 | tf_op jit(solution)/shard_map/all_gather | solution.py:156
  43.4 19.1 %shard_map.162 = f32[6144,640]{1,0:T(8,128)} custom-call(bf16[1536,1024]{1,0:T(8,128)(2,1)} %all-gather.4.cloned.1.call-done.lhs_ref, bf16[512,1024]{1,0:T(8,128)(2,1)} %multiply_convert_fusion.wq_ref, bf16[512,256]{1,0:T(8,128)(2,1)} %multiply_convert_fusion.1.wkv_ref, bf16[1024,512]{1,0:T(8,128)(2,1)} %wo_ref.1), custom_call_target="tpu_custom_call" | custom-call | flops 4026531840 | bytes 21233664 | tf_op jit(solution)/shard_map/pallas_call | solution.py:98
  62.6 1.8 fusion.12
  64.4 10.6 %psum.35 = f32[1536]{0:T(1024)S(1)} all-reduce(f32[1536]{0:T(1024)S(1)} %fusion.12), channel_id=1, replica_groups=mesh['row'=4,'col'=8,'seq'=4] {'seq'}, use_global_device_ids=true, to_apply=%region_2.3 | all-reduce | flops 1536 | bytes 12288 | tf_op jit(solution)/shard_map/psum | solution.py:168
  75.0 10.9 %psum.36 = f32[1536]{0:T(1024)S(1)} all-reduce(f32[1536]{0:T(1024)S(1)} %psum.35), channel_id=1, replica_groups=mesh['row'=4,'col'=8,'seq'=4] {'row'}, use_global_device_ids=true, to_apply=%region_3.4 | all-reduce | flops 1536 | bytes 12288 | tf_op jit(solution)/shard_map/psum | solution.py:168
  86.0 82.7 %reduce-scatter.3.cloned.1.call-done = f32[384,640]{1,0:T(8,128)} async-done(((f32[6144,640]{1,0:T(8,128)}), f32[384,640]{1,0:T(8,128)}) %reduce-scatter.3.cloned.1.call-update) | async-done | bytes 983056 | tf_op jit(solution)/shard_map/reduce_scatter | solution.py:171
  168.7 1.1 fusion.85
  169.8 0.8 fusion.81
  170.7 1.7 fusion.86
  172.4 0.6 all-gather.8.cloned.1.call-start
  173.0 2.5 gather_fusion.2
  175.7 0.8 multiply_cosine_fusion.1
  176.4 1.6 compare_and_fusion
  178.5 0.5 fusion.118
  179.1 36.2 %all-gather.6.cloned.1.call-done = bf16[6144,128]{1,0:T(8,128)(2,1)} async-done(((bf16[384,128]{1,0:T(8,128)(2,1)}), bf16[6144,128]{1,0:T(8,128)(2,1)}) %all-gather.6.cloned.1.call-update) | async-done | bytes 1572880 | tf_op jit(solution)/shard_map/all_gather | solution.py:186
  215.3 1.2 fusion.117
  216.4 2.4 convolution_bitcast_fusion
  218.9 3.0 fusion.17
  221.9 7.2 %fusion.32 = f32[384,2,128]{2,0,1:T(8,128)S(1)} fusion(f32[1152,384,2]{1,0,2:T(8,128)} %get-tuple-element.83, f32[2,384,1152]{1,2,0:T(8,128)} %convolution_bitcast_fusion, bf16[1536,128]{1,0:T(8,128)(2,1)S(1)} %bitcast.162, s32[]{:T(128)S(6)} %min.4, f32[2,384]{1,0:T(2,128)S(1)} %get-tuple-element.82, pred[384,1152]{0,1:T(8,128)(4,1)S(1)} %copy-done.17), kind=kOutput, calls=%fused_computation.46 | convolution fusion | flops 238880640 | bytes 15734788 | tf_op jit(solution)/shard_map/hqk,kd->qhd/dot_general | solution.py:224
  229.2 7.7 %convolution_bitcast_fusion.2 = f32[1152,1,128]{0,2,1:T(8,128)S(1)} fusion(f32[1152,384,2]{1,0,2:T(8,128)} %get-tuple-element.83, f32[2,384,1152]{1,2,0:T(8,128)} %convolution_bitcast_fusion, bf16[384,2,64]{2,0,1:T(8,128)(2,1)S(1)} %get-tuple-element.69, bf16[384,2,64]{2,0,1:T(8,128)(2,1)S(1)} %get-tuple-element.68, f32[2,384]{1,0:T(2,128)S(1)} %get-tuple-element.82, ...), kind=kOutput, calls=%fused_computation.31 | convolution fusion | flops 239273856 | bytes 8309760 | tf_op jit(solution)/shard_map/hqk,qhd->kd/dot_general | solution.py:227
  236.8 3.2 fusion.15
  240.6 3.0 fusion.45
  243.6 1.3 fusion.65
  244.9 1.0 maximum_maximum_fusion
  246.2 105.2 %all-gather.8.cloned.1.call-done = bf16[30720,256]{0,1:T(8,128)(2,1)} async-done(((bf16[1920,256]{0,1:T(8,128)(2,1)}), bf16[30720,256]{0,1:T(8,128)(2,1)}) %all-gather.8.cloned.1.call-update) | async-done | bytes 15728656 | tf_op jit(solution)/shard_map/all_gather | solution.py:248
  351.4 9.7 %copy.151 = bf16[32,8,16,1920]{3,2,1,0:T(8,128)(2,1)S(1)} copy(bf16[32,8,16,1920]{3,1,2,0:T(8,128)(2,1)} %bitcast.145) | data formatting | bytes 31457280
  361.1 5.4 %copy-done.3 = bf16[32,8,16,1920]{3,2,1,0:T(8,128)(2,1)} copy-done((bf16[32,8,16,1920]{3,2,1,0:T(8,128)(2,1)}, bf16[32,8,16,1920]{3,2,1,0:T(8,128)(2,1)S(1)}, u32[]{:S(2)}) %copy-start.3) | copy-done | bytes 15728664
  366.6 3.3 fusion.115
  369.9 11.6 %slice_convert_fusion = f32[16,1152,256]{1,0,2:T(8,128)} fusion(bf16[16,1920,256]{1,0,2:T(8,128)(2,1)} %bitcast.144), kind=kLoop, calls=%fused_computation.4 | loop fusion | flops 4718592 | bytes 28311552 | tf_op jit(solution)/shard_map/reshape | solution.py:261
  381.6 5.0 copy.145
  386.6 4.3 copy.116
  390.9 0.8 copy.152
  391.7 0.4 copy-done.13
  392.1 1.8 convolution_convert_fusion
  393.9 5.2 copy.146
  399.1 4.3 copy.119
  403.5 0.8 copy.153
  404.2 1.7 copy-done.8
  405.9 3.5 fusion.119
  409.4 21.7 %reshape.477 = f32[4,4,1152,256]{2,1,0,3:T(4,128)} reshape(f32[16,1152,256]{1,0,2:T(8,128)} %slice_convert_fusion) | data formatting | bytes 37748736 | tf_op jit(solution)/shard_map/reshape | solution.py:261
  431.1 18.1 %reduce_sum.57 = f32[4,1152,256]{1,0,2:T(4,128)} reduce(f32[4,4,1152,256]{2,1,0,3:T(4,128)} %reshape.477, f32[]{:T(128)} %constant.182.clone.1), dimensions={1}, to_apply=%region_6.7 | reduce | flops 3538944 | bytes 23592964 | tf_op jit(solution)/shard_map/reduce_sum | solution.py:262
  449.2 10.1 %fusion.116 = (f32[1,1152,256]{1,0,2:T(1,128)S(1)}, f32[1,1152,256]{1,0,2:T(1,128)S(1)}, f32[1,1152,256]{1,0,2:T(1,128)S(1)}, f32[1,1152,256]{1,0,2:T(1,128)S(1)}) fusion(f32[4,1152,256]{1,0,2:T(4,128)} %reduce_sum.57), kind=kLoop, calls=%fused_computation.158 | loop fusion | bytes 9437184 | tf_op jit(solution)/shard_map/slice | solution.py:267
  460.4 1.5 copy-done.10
  461.9 0.6 convolution_add_fusion.1
  462.5 1.3 copy-done.4
  463.8 2.0 fusion.10
  465.8 2.1 pad_maximum_fusion
  467.9 14.8 %psum.37 = f32[2048]{0:T(1024)S(1)} all-reduce(f32[2048]{0:T(1024)S(1)} %pad_maximum_fusion.6), channel_id=1, replica_groups=mesh['row'=4,'col'=8,'seq'=4] {'col'}, use_global_device_ids=true, to_apply=%region_10.11 | all-reduce | flops 2048 | bytes 16384 | tf_op jit(solution)/shard_map/psum | solution.py:295
  482.8 0.6 slice.218
  483.4 10.4 %psum.38 = f32[192]{0:T(256)S(1)} all-reduce(f32[192]{0:T(256)S(1)} %dynamic_slice.23), channel_id=1, replica_groups=mesh['row'=4,'col'=8,'seq'=4] {'seq'}, use_global_device_ids=true, to_apply=%region_11.12 | all-reduce | flops 192 | bytes 1536 | tf_op jit(solution)/shard_map/psum | solution.py:298
  493.8 8.5 %psum.39 = f32[192]{0:T(256)S(1)} all-reduce(f32[192]{0:T(256)S(1)} %psum.38), channel_id=1, replica_groups=mesh['row'=4,'col'=8,'seq'=4] {'row'}, use_global_device_ids=true, to_apply=%region_12.13 | all-reduce | flops 192 | bytes 1536 | tf_op jit(solution)/shard_map/psum | solution.py:298
  502.4 3.2 fusion.61
  505.6 3.2 fusion.58
  508.8 3.1 fusion.30
  511.9 3.3 fusion.108
  515.2 1.1 convert_element_type.109
  516.3 0.9 fusion.55
  (78 shorter events, 3.3 us)
Async XLA Ops:
  7.2 3.9 copy-start
  7.2 5.0 copy-start.15
  7.2 5.9 %copy-start.20 = (f32[512]{0:T(512)S(1)}, f32[512]{0:T(512)}, u32[]{:S(2)}) copy-start(f32[512]{0:T(512)} %param.24) | copy-start | bytes 6148
  7.2 5.9 %copy-start.18 = (bf16[512,128]{1,0:T(8,128)(2,1)S(1)}, bf16[512,128]{1,0:T(8,128)(2,1)}, u32[]{:S(2)}) copy-start(bf16[512,128]{1,0:T(8,128)(2,1)} %param.27) | copy-start | bytes 393220
  7.2 5.9 %copy-start.16 = (bf16[512,128]{1,0:T(8,128)(2,1)S(1)}, bf16[512,128]{1,0:T(8,128)(2,1)}, u32[]{:S(2)}) copy-start(bf16[512,128]{1,0:T(8,128)(2,1)} %param.26) | copy-start | bytes 393220
  7.2 6.7 %copy-start.11 = (bf16[512,1024]{1,0:T(8,128)(2,1)S(1)}, bf16[512,1024]{1,0:T(8,128)(2,1)}, u32[]{:S(2)}) copy-start(bf16[512,1024]{1,0:T(8,128)(2,1)} %param.25) | copy-start | bytes 3145732
  7.2 36.1 %all-gather.4.cloned.1.call-start = ((), (), s32[]{:S(2)}) async-start(), calls=%async_computation.2 | async-start | bytes 3538944 | tf_op jit(solution)/shard_map/all_gather | solution.py:156
  13.0 155.7 %reduce-scatter.3.cloned.1.call-start = ((), (), s32[]{:S(2)}) async-start(), calls=%async_computation.3 | async-start | bytes 16711680 | tf_op jit(solution)/shard_map/reduce_scatter | solution.py:171
  62.5 110.5 %copy-start.2 = (s32[1536]{0:T(1024)S(1)}, s32[1536]{0:T(1024)}, u32[]{:S(2)}) copy-start(s32[1536]{0:T(1024)} %param.21) | copy-start | bytes 18436
  62.5 152.8 %all-gather.6.cloned.1.call-start = ((), (), s32[]{:S(2)}) async-start(), calls=%async_computation.4 | async-start | bytes 1671168 | tf_op jit(solution)/shard_map/all_gather | solution.py:186
  168.7 9.3 %copy-start.14 = (f32[384,640]{1,0:T(8,128)S(1)}, f32[384,640]{1,0:T(8,128)}, u32[]{:S(2)}) copy-start(f32[384,640]{1,0:T(8,128)} %reduce-scatter.3.cloned.1.call-done) | copy-start | bytes 2949124
  172.4 179.0 %all-gather.8.cloned.1.call-start = ((), (), s32[]{:S(2)}) async-start(), calls=%async_computation.5 | async-start | bytes 16711680 | tf_op jit(solution)/shard_map/all_gather | solution.py:248
  179.1 39.8 %copy-start.17 = (pred[384,1152]{0,1:T(8,128)(4,1)S(1)}, pred[384,1152]{0,1:T(8,128)(4,1)}, u32[]{:S(2)}) copy-start(pred[384,1152]{0,1:T(8,128)(4,1)} %compare_and_fusion) | copy-start | bytes 1327108
  246.0 269.3 %reduce-scatter.5.cloned.1.call-start = ((), (), s32[]{:S(2)}) async-start(), calls=%async_computation.6 | async-start | bytes 3538944 | tf_op jit(solution)/shard_map/reduce_scatter | solution.py:299
  361.1 5.4 %copy-start.3 = (bf16[32,8,16,1920]{3,2,1,0:T(8,128)(2,1)}, bf16[32,8,16,1920]{3,2,1,0:T(8,128)(2,1)S(1)}, u32[]{:S(2)}) copy-start(bf16[32,8,16,1920]{3,2,1,0:T(8,128)(2,1)S(1)} %copy.151) | copy-start | bytes 47185924
  390.9 1.2 copy-start.13
  391.7 2.3 copy-start.6
  403.4 2.5 copy-start.12
  404.2 1.7 copy-start.8
  460.0 1.9 copy-start.10
  461.9 1.9 copy-start.4
  461.9 1.9 copy-start.19
  502.4 6.4 %copy-start.7 = (bf16[192,8,4,256]{3,1,2,0:T(8,128)(2,1)S(1)}, bf16[192,8,4,256]{3,1,2,0:T(8,128)(2,1)}, u32[]{:S(2)}) copy-start(bf16[192,8,4,256]{3,1,2,0:T(8,128)(2,1)} %copy-done.6) | copy-start | bytes 9437188
  505.6 3.2 copy-start.5
  508.8 3.1 copy-start.9
  511.9 5.3 %copy-start.1 = (bf16[1024,512]{1,0:T(8,128)(2,1)S(1)}, bf16[1024,512]{1,0:T(8,128)(2,1)}, u32[]{:S(2)}) copy-start(bf16[1024,512]{1,0:T(8,128)(2,1)} %param.23) | copy-start | bytes 3145732
Sparse Core Ops, SparseCore 0:
  13.1 30.1 all-gather.3
  62.6 106.0 reduce-scatter.2
  172.5 42.7 all-gather.5
  246.1 105.2 all-gather.7
  468.0 35.6 reduce-scatter.4

commit v5 on v4

--- a/solution.py
+++ b/solution.py
@@ -244,9 +244,11 @@
         .reshape(quarter_len, part_w)
         .astype(jnp.bfloat16)
     )
-    back_rows = 2 * quarter_len + win
+    back_rows = 2 * quarter_len + win + 8
     back_all = lax.all_gather(
-        jnp.concatenate([attn_out, grad_query_round, kv_grad_win], axis=0),
+        jnp.concatenate(
+            [attn_out, grad_query_round, kv_grad_win, jnp.zeros((8, part_w), jnp.bfloat16)], axis=0
+        ),
         ("row", "seq"),
         axis=0,
         tiled=True,

time: 529 us -> 441 us (0.83)
  local copies, waits for them, and re-layouts: 84.6 us -> 22.7 us
  other arithmetic: 49.9 us -> 27.1 us
    unnamed x48, local copies, waits for them, and re-layouts: 32 us -> 3.34 us
    reshape x1 -> x2, local copies, waits for them, and re-layouts: 21.7 us -> 4.86 us  [the longest x1 2.43 us: per_device(): back_all[:, :quarter_len].reshape(n_row, n_seq, quarter_len, part_w)]
    reduce_sum x1, other arithmetic: 18.1 us -> 5.68 us  [per_device(): kv_terms = back_all[:, 2 * quarter_len:2 * quarter_len + win].astype(jnp....]
    reshape x1 -> x0, other arithmetic: 11.6 us -> none  [per_device(): kv_terms = back_all[:, 2 * quarter_len:2 * quarter_len + win].astype(jnp....]
    slice x1 -> x0, local copies, waits for them, and re-layouts: 10.1 us -> none  [per_device(): kv_grad_f = kv_grad_f.at[first:first + win].add(kv_terms[quarter])]
    transpose x2 -> x0, local copies, waits for them, and re-layouts: 8.64 us -> none  [from_blocks(): return blocks.transpose(0, 2, 1, 3).reshape(n_row * rows, n_seq * w)]
  transfers between devices with their start and end apart: 5 -> 5, of which waited for: 4 -> 4; matrix products, arithmetic and copies ran while one was open for 5% -> 6% of each run, Pallas kernels for 0% -> 0%
where the time goes in v5:
time: 441 us; the launch traced here: 437 us
  waiting for transfers between devices  251 us (57%)
  blocking collectives  55.2 us (13%)
  matrix products  46.7 us (11%)
  other arithmetic  27.1 us (6%)
  local copies, waits for them, and re-layouts  22.7 us (5%)
  Pallas kernels  19.1 us (4%)
  between operations  14.8 us (3%)
    all_gather x1, waiting for transfers between devices, per_device(): lax.all_gather(jnp.concatenate([attn_out, grad_query_round, kv_grad_win,...  105 us
    reduce_scatter x1, waiting for transfers between devices, per_device(): lax.psum_scatter(blocks, ('row', 'seq'), scatter_dimension=0, tiled=True)  82.9 us
    all_gather x1, waiting for transfers between devices, per_device(): lax.all_gather(kv_piece, ('row', 'seq'), axis=0, tiled=True)  34.4 us
    all_gather x1, waiting for transfers between devices, per_device(): lax.all_gather(jnp.concatenate([embedded, out_grad], axis=1), 'col', axis...  28.2 us
    pallas_call x1, Pallas kernels, project_blocks(): pl.pallas_call(project_kernel, grid=(n_row, n_seq), in_specs=[pl.BlockSpe...  19.1 us
    psum x2, blocking collectives, per_device(): total_dot = lax.psum(lax.psum(own_dots, 'seq'), 'row')  18.9 us
    psum x1, blocking collectives, per_device(): col_terms = lax.psum(jnp.concatenate([gain_terms, dot_terms]), 'col')  14.8 us
    psum x1, blocking collectives, per_device(): lax.psum(lax.psum(jnp.sum(emb_all_f * emb_all_f, axis=1), 'seq'), 'row')  10.9 us
  transfers between devices with their start and end apart: 5, of which 4 were waited for; matrix products, arithmetic and copies ran while one was open for 6% of the time, Pallas kernels for 0%

profile of v5, /device:TPU:0, one launch (start us, length us, event | category | flops | bytes accessed | tf_op | source)
XLA Modules:
  0.0 437.2 jit_solution(14099134044966411656)
XLA Ops:
  7.3 0.9 compare_select_fusion.2
  8.1 0.7 compare_and_fusion.1
  8.9 2.2 gather_fusion
  11.0 1.0 gather_fusion.1
  12.2 0.8 pad_maximum_fusion.1
  13.1 0.8 multiply_convert_fusion.1.wkv_ref
  13.9 1.2 multiply_convert_fusion.wq_ref
  15.1 28.2 %all-gather.4.cloned.1.call-done.lhs_ref = bf16[1536,1024]{1,0:T(8,128)(2,1)} async-done(((bf16[192,1024]{1,0:T(8,128)(2,1)}), bf16[1536,1024]{1,0:T(8,128)(2,1)}) %all-gather.4.cloned.1.call-update) | async-done | bytes 3145744 | tf_op jit(solution)/shard_map/all_gather | solution.py:156
  43.4 19.1 %shard_map.162 = f32[6144,640]{1,0:T(8,128)} custom-call(bf16[1536,1024]{1,0:T(8,128)(2,1)} %all-gather.4.cloned.1.call-done.lhs_ref, bf16[512,1024]{1,0:T(8,128)(2,1)} %multiply_convert_fusion.wq_ref, bf16[512,256]{1,0:T(8,128)(2,1)} %multiply_convert_fusion.1.wkv_ref, bf16[1024,512]{1,0:T(8,128)(2,1)} %wo_ref.1), custom_call_target="tpu_custom_call" | custom-call | flops 4026531840 | bytes 21233664 | tf_op jit(solution)/shard_map/pallas_call | solution.py:98
  62.6 1.8 fusion.12
  64.3 10.6 %psum.35 = f32[1536]{0:T(1024)S(1)} all-reduce(f32[1536]{0:T(1024)S(1)} %fusion.12), channel_id=1, replica_groups=mesh['row'=4,'col'=8,'seq'=4] {'seq'}, use_global_device_ids=true, to_apply=%region_2.3 | all-reduce | flops 1536 | bytes 12288 | tf_op jit(solution)/shard_map/psum | solution.py:168
  74.9 10.9 %psum.36 = f32[1536]{0:T(1024)S(1)} all-reduce(f32[1536]{0:T(1024)S(1)} %psum.35), channel_id=1, replica_groups=mesh['row'=4,'col'=8,'seq'=4] {'row'}, use_global_device_ids=true, to_apply=%region_3.4 | all-reduce | flops 1536 | bytes 12288 | tf_op jit(solution)/shard_map/psum | solution.py:168
  85.9 82.9 %reduce-scatter.3.cloned.1.call-done = f32[384,640]{1,0:T(8,128)} async-done(((f32[6144,640]{1,0:T(8,128)}), f32[384,640]{1,0:T(8,128)}) %reduce-scatter.3.cloned.1.call-update) | async-done | bytes 983056 | tf_op jit(solution)/shard_map/reduce_scatter | solution.py:171
  168.8 1.0 fusion.86
  169.9 0.8 fusion.82
  170.7 1.7 fusion.87
  172.4 0.2 all-gather.8.cloned.1.call-start
  172.7 2.5 gather_fusion.2
  175.4 0.8 multiply_cosine_fusion.1
  176.1 0.9 compare_and_fusion
  177.0 1.3 slice_multiply_fusion.1
  178.3 0.2 reshape.462
  178.5 1.0 slice.290
  179.7 0.5 fusion.118
  180.2 0.8 subtract_convert_fusion.1
  181.0 34.4 %all-gather.6.cloned.1.call-done = bf16[6144,128]{1,0:T(8,128)(2,1)} async-done(((bf16[384,128]{1,0:T(8,128)(2,1)}), bf16[6144,128]{1,0:T(8,128)(2,1)}) %all-gather.6.cloned.1.call-update) | async-done | bytes 1572880 | tf_op jit(solution)/shard_map/all_gather | solution.py:186
  215.4 1.2 fusion.117
  216.6 2.4 convolution_bitcast_fusion
  219.0 3.1 fusion.17
  222.1 7.5 %fusion.32 = f32[384,2,128]{2,0,1:T(8,128)S(1)} fusion(f32[1152,384,2]{1,0,2:T(8,128)} %get-tuple-element.79, f32[2,384,1152]{1,2,0:T(8,128)} %convolution_bitcast_fusion, bf16[1536,128]{1,0:T(8,128)(2,1)} %bitcast.159, s32[]{:T(128)S(6)} %min.4, f32[2,384]{1,0:T(2,128)S(1)} %get-tuple-element.78, pred[384,1152]{0,1:T(8,128)(4,1)S(1)} %compare_and_fusion), kind=kOutput, calls=%fused_computation.46 | convolution fusion | flops 238880640 | bytes 15734788 | tf_op jit(solution)/shard_map/hqk,kd->qhd/dot_general | solution.py:224
  229.7 8.7 %convolution_bitcast_fusion.2 = f32[1152,1,128]{0,2,1:T(8,128)S(1)} fusion(f32[1152,384,2]{1,0,2:T(8,128)} %get-tuple-element.79, f32[2,384,1152]{1,2,0:T(8,128)} %convolution_bitcast_fusion, bf16[384,2,64]{2,0,1:T(8,128)(2,1)} %get-tuple-element.65, bf16[384,2,64]{2,0,1:T(8,128)(2,1)} %copy-done.17, f32[2,384]{1,0:T(2,128)S(1)} %get-tuple-element.78, ...), kind=kOutput, calls=%fused_computation.31 | convolution fusion | flops 239273856 | bytes 8309760 | tf_op jit(solution)/shard_map/hqk,qhd->kd/dot_general | solution.py:227
  238.4 4.1 fusion.15
  242.5 1.6 fusion.46
  244.2 0.2 add_convert_fusion
  244.7 1.3 fusion.66
  246.0 1.2 maximum_maximum_fusion
  247.2 1.3 copy.92
  248.5 0.3 reduce-scatter.5.cloned.1.call-start
  248.8 105.5 %all-gather.8.cloned.1.call-done = bf16[30848,256]{1,0:T(8,128)(2,1)} async-done(((bf16[1928,256]{1,0:T(8,128)(2,1)}), bf16[30848,256]{1,0:T(8,128)(2,1)}) %all-gather.8.cloned.1.call-update) | async-done | bytes 15794192 | tf_op jit(solution)/shard_map/all_gather | solution.py:248
  354.3 5.7 %convert_reduce_fusion = f32[4,1152,256]{2,1,0:T(8,128)S(1)} fusion(bf16[16,1928,256]{2,1,0:T(8,128)(2,1)} %bitcast.142), kind=kLoop, calls=%fused_computation.4 | loop fusion | flops 8257536 | bytes 14155776 | tf_op jit(solution)/shard_map/reduce_sum | solution.py:264
  360.0 3.3 fusion.116
  363.6 0.2 fusion.41
  363.8 0.3 fusion.39
  364.2 2.4 copy.95
  366.6 0.8 copy.119
  367.4 1.8 fusion.119
  369.2 2.4 copy.93
  371.7 0.8 copy.118
  372.5 0.4 copy-done.10
  372.9 2.1 convolution_convert_fusion
  375.0 0.6 convolution_add_fusion.1
  375.6 1.3 copy-done.3
  376.9 1.9 fusion.10
  378.8 2.1 pad_maximum_fusion
  380.9 14.8 %psum.37 = f32[2048]{0:T(1024)S(1)} all-reduce(f32[2048]{0:T(1024)S(1)} %pad_maximum_fusion.6), channel_id=1, replica_groups=mesh['row'=4,'col'=8,'seq'=4] {'col'}, use_global_device_ids=true, to_apply=%region_10.11 | all-reduce | flops 2048 | bytes 16384 | tf_op jit(solution)/shard_map/psum | solution.py:297
  395.8 0.6 slice.218
  396.4 10.4 %psum.38 = f32[192]{0:T(256)S(1)} all-reduce(f32[192]{0:T(256)S(1)} %dynamic_slice.23), channel_id=1, replica_groups=mesh['row'=4,'col'=8,'seq'=4] {'seq'}, use_global_device_ids=true, to_apply=%region_11.12 | all-reduce | flops 192 | bytes 1536 | tf_op jit(solution)/shard_map/psum | solution.py:300
  406.8 8.5 %psum.39 = f32[192]{0:T(256)S(1)} all-reduce(f32[192]{0:T(256)S(1)} %psum.38), channel_id=1, replica_groups=mesh['row'=4,'col'=8,'seq'=4] {'row'}, use_global_device_ids=true, to_apply=%region_12.13 | all-reduce | flops 192 | bytes 1536 | tf_op jit(solution)/shard_map/psum | solution.py:300
  415.4 3.2 fusion.59
  418.6 3.2 fusion.62
  421.8 3.1 fusion.30
  425.0 3.3 fusion.109
  428.3 1.1 convert_element_type.109
  429.4 0.9 fusion.56
  (79 shorter events, 1.8 us)
Async XLA Ops:
  7.2 3.9 copy-start
  7.2 5.0 %copy-start.11 = (bf16[192,512]{1,0:T(8,128)(2,1)S(1)}, bf16[192,512]{1,0:T(8,128)(2,1)}, u32[]{:S(2)}) copy-start(bf16[192,512]{1,0:T(8,128)(2,1)} %param.29) | copy-start | bytes 589828
  7.2 5.9 %copy-start.21 = (f32[512]{0:T(512)S(1)}, f32[512]{0:T(512)}, u32[]{:S(2)}) copy-start(f32[512]{0:T(512)} %param.24) | copy-start | bytes 6148
  7.2 5.9 %copy-start.12 = (bf16[512,128]{1,0:T(8,128)(2,1)S(1)}, bf16[512,128]{1,0:T(8,128)(2,1)}, u32[]{:S(2)}) copy-start(bf16[512,128]{1,0:T(8,128)(2,1)} %param.26) | copy-start | bytes 393220
  7.2 5.9 %copy-start.19 = (bf16[512,128]{1,0:T(8,128)(2,1)S(1)}, bf16[512,128]{1,0:T(8,128)(2,1)}, u32[]{:S(2)}) copy-start(bf16[512,128]{1,0:T(8,128)(2,1)} %param.27) | copy-start | bytes 393220
  7.2 6.7 %copy-start.9 = (bf16[512,1024]{1,0:T(8,128)(2,1)S(1)}, bf16[512,1024]{1,0:T(8,128)(2,1)}, u32[]{:S(2)}) copy-start(bf16[512,1024]{1,0:T(8,128)(2,1)} %param.25) | copy-start | bytes 3145732
  7.2 36.1 %all-gather.4.cloned.1.call-start = ((), (), s32[]{:S(2)}) async-start(), calls=%async_computation.2 | async-start | bytes 3538944 | tf_op jit(solution)/shard_map/all_gather | solution.py:156
  13.0 155.8 %reduce-scatter.3.cloned.1.call-start = ((), (), s32[]{:S(2)}) async-start(), calls=%async_computation.3 | async-start | bytes 16711680 | tf_op jit(solution)/shard_map/reduce_scatter | solution.py:171
  62.5 110.3 %copy-start.2 = (s32[1536]{0:T(1024)S(1)}, s32[1536]{0:T(1024)}, u32[]{:S(2)}) copy-start(s32[1536]{0:T(1024)} %param.21) | copy-start | bytes 18436
  62.5 152.9 %all-gather.6.cloned.1.call-start = ((), (), s32[]{:S(2)}) async-start(), calls=%async_computation.4 | async-start | bytes 1671168 | tf_op jit(solution)/shard_map/all_gather | solution.py:186
  172.4 181.8 %all-gather.8.cloned.1.call-start = ((), (), s32[]{:S(2)}) async-start(), calls=%async_computation.5 | async-start | bytes 16781312 | tf_op jit(solution)/shard_map/all_gather | solution.py:248
  177.0 45.1 %copy-start.14 = (pred[384,1152]{0,1:T(8,128)(4,1)}, pred[384,1152]{0,1:T(8,128)(4,1)S(1)}, u32[]{:S(2)}) copy-start(pred[384,1152]{0,1:T(8,128)(4,1)S(1)} %compare_and_fusion) | copy-start | bytes 1327108
  181.0 41.2 %copy-start.17 = (bf16[384,2,64]{2,0,1:T(8,128)(2,1)}, bf16[384,2,64]{2,0,1:T(8,128)(2,1)S(1)}, u32[]{:S(2)}) copy-start(bf16[384,2,64]{2,0,1:T(8,128)(2,1)S(1)} %get-tuple-element.64) | copy-start | bytes 294916
  215.4 3.7 copy-start.18
  216.6 5.6 %copy-start.16 = (bf16[4,1,384,128]{3,2,1,0:T(8,128)(2,1)}, bf16[4,1,384,128]{3,2,1,0:T(8,128)(2,1)S(1)}, u32[]{:S(2)}) copy-start(bf16[4,1,384,128]{3,2,1,0:T(8,128)(2,1)S(1)} %get-tuple-element.63) | copy-start | bytes 1179652
  238.4 4.1 copy-start.15
  238.4 4.1 copy-start.22
  248.5 179.7 %reduce-scatter.5.cloned.1.call-start = ((), (), s32[]{:S(2)}) async-start(), calls=%async_computation.6 | async-start | bytes 3538944 | tf_op jit(solution)/shard_map/reduce_scatter | solution.py:301
  367.4 1.9 copy-start.5
  371.7 1.2 copy-start.10
  372.5 2.5 copy-start.7
  372.9 2.1 copy-start.13
  375.0 1.9 copy-start.3
  375.0 1.9 copy-start.20
  415.4 6.4 %copy-start.8 = (bf16[192,8,4,256]{3,1,2,0:T(8,128)(2,1)S(1)}, bf16[192,8,4,256]{3,1,2,0:T(8,128)(2,1)}, u32[]{:S(2)}) copy-start(bf16[192,8,4,256]{3,1,2,0:T(8,128)(2,1)} %copy-done.7) | copy-start | bytes 9437188
  418.6 3.2 copy-start.4
  421.8 3.1 copy-start.6
  425.0 5.3 %copy-start.1 = (bf16[1024,512]{1,0:T(8,128)(2,1)S(1)}, bf16[1024,512]{1,0:T(8,128)(2,1)}, u32[]{:S(2)}) copy-start(bf16[1024,512]{1,0:T(8,128)(2,1)} %param.23) | copy-start | bytes 3145732
Sparse Core Ops, SparseCore 0:
  13.1 30.1 all-gather.3
  62.6 106.1 reduce-scatter.2
  172.6 42.7 all-gather.5
  248.7 105.5 all-gather.7
  381.0 35.6 reduce-scatter.4

commit v6 on v5

--- a/solution.py
+++ b/solution.py
@@ -3,6 +3,7 @@
 from jax import lax
 from jax.sharding import PartitionSpec as P
 from jax.experimental import pallas as pl
+from jax.experimental.pallas import tpu as pltpu
 
 D = 8192
 H = 64
@@ -113,6 +114,93 @@
             + n_row * n_seq * rows * out_w * 4,
         ),
     )(lhs, wq, wkv, wo)
+
+
+def attention_kernel(
+    q_ref, do_ref, k_ref, v_ref, qpos_ref, qseg_ref, kpos_ref, kseg_ref,
+    out_ref, gq_ref, gk_ref, gv_ref,
+):
+    head = pl.program_id(0)
+    score_scale = HD ** (-0.5)
+    query = q_ref[0]
+    dout = do_ref[0]
+    key = k_ref[...]
+    value = v_ref[...]
+    allowed = (kpos_ref[...] <= qpos_ref[...]) & (kseg_ref[...] == qseg_ref[...])
+    nt = (((1,), (1,)), ((), ()))
+    tn = (((0,), (0,)), ((), ()))
+    raw_scores = (
+        lax.dot_general(query, key, nt, preferred_element_type=jnp.float32) * score_scale
+    )
+    capped = softcap * jnp.tanh(raw_scores / softcap)
+    weights = jnp.where(allowed, jnp.exp(capped), 0.0)
+    totals = jnp.sum(weights, axis=1, keepdims=True)
+    attended = jnp.dot(
+        weights.astype(jnp.bfloat16), value, preferred_element_type=jnp.float32
+    )
+    out_ref[0] = (attended / totals).astype(out_ref.dtype)
+    probs = weights / totals
+    prob_grads = lax.dot_general(dout, value, nt, preferred_element_type=jnp.float32)
+    row_dots = jnp.sum(probs * prob_grads, axis=1, keepdims=True)
+    grad_scores = (
+        probs * (prob_grads - row_dots) * (1.0 - (capped / softcap) ** 2) * score_scale
+    ).astype(jnp.bfloat16)
+    gq_ref[0] = jnp.dot(grad_scores, key, preferred_element_type=jnp.float32)
+    gk_term = lax.dot_general(grad_scores, query, tn, preferred_element_type=jnp.float32)
+    gv_term = lax.dot_general(
+        probs.astype(jnp.bfloat16), dout, tn, preferred_element_type=jnp.float32
+    )
+
+    @pl.when(head == 0)
+    def _():
+        gk_ref[...] = gk_term
+        gv_ref[...] = gv_term
+
+    @pl.when(head != 0)
+    def _():
+        gk_ref[...] += gk_term
+        gv_ref[...] += gv_term
+
+
+def attention_block(q, dout, key, value, qpos, qseg, kpos, kseg):
+    heads, rows, hd = q.shape
+    win = key.shape[0]
+    full = lambda h: (0, 0)
+    per_head = lambda h: (h, 0, 0)
+    return pl.pallas_call(
+        attention_kernel,
+        grid=(heads,),
+        in_specs=[
+            pl.BlockSpec((1, rows, hd), per_head),
+            pl.BlockSpec((1, rows, hd), per_head),
+            pl.BlockSpec((win, hd), full),
+            pl.BlockSpec((win, hd), full),
+            pl.BlockSpec((rows, 1), full),
+            pl.BlockSpec((rows, 1), full),
+            pl.BlockSpec((1, win), full),
+            pl.BlockSpec((1, win), full),
+        ],
+        out_specs=[
+            pl.BlockSpec((1, rows, hd), per_head),
+            pl.BlockSpec((1, rows, hd), per_head),
+            pl.BlockSpec((win, hd), full),
+            pl.BlockSpec((win, hd), full),
+        ],
+        out_shape=[
+            jax.ShapeDtypeStruct((heads, rows, hd), jnp.bfloat16),
+            jax.ShapeDtypeStruct((heads, rows, hd), jnp.float32),
+            jax.ShapeDtypeStruct((win, hd), jnp.float32),
+            jax.ShapeDtypeStruct((win, hd), jnp.float32),
+        ],
+        compiler_params=pltpu.CompilerParams(
+            dimension_semantics=("arbitrary",), vmem_limit_bytes=48 * 1024 * 1024
+        ),
+        cost_estimate=pl.CostEstimate(
+            flops=12 * heads * rows * win * hd,
+            transcendentals=2 * heads * rows * win,
+            bytes_accessed=4 * heads * rows * hd * 2 + 4 * win * hd * 4,
+        ),
+    )(q, dout, key, value, qpos, qseg, kpos, kseg)
 
 
 def per_device(
@@ -196,43 +284,19 @@
     key_sel = lax.dynamic_slice(key_all, (win_start, 0), (win, HD))
     value_sel = lax.dynamic_slice(value_all, (win_start, 0), (win, HD))
     key_seg = lax.dynamic_slice(segment_ids, (win_start,), (win,))
-    allowed = (key_pos[None, :] <= query_pos[:, None]) & (
-        key_seg[None, :] == jnp.take(segment_ids, query_pos)[:, None]
-    )
-    query_heads = queries.reshape(quarter_len, head_count, HD)
-    raw_scores = (
-        jnp.einsum("qhd,kd->hqk", query_heads, key_sel, preferred_element_type=jnp.float32)
-        * score_scale
-    )
-    capped = softcap * jnp.tanh(raw_scores / softcap)
-    weights = jnp.where(allowed[None], jnp.exp(capped), 0.0)
-    totals = jnp.sum(weights, axis=2)
-    attended = jnp.einsum(
-        "hqk,kd->qhd", weights.astype(jnp.bfloat16), value_sel, preferred_element_type=jnp.float32
-    )
-    attn_out = (
-        (attended / totals.T[:, :, None]).astype(jnp.bfloat16).reshape(quarter_len, part_w)
-    )
-    attn_probs = weights / totals[:, :, None]
-    prob_grads = jnp.einsum(
-        "qhd,kd->hqk", out_heads, value_sel, preferred_element_type=jnp.float32
-    )
-    row_dots = jnp.sum(attn_probs * prob_grads, axis=2, keepdims=True)
-    grad_scores = (
-        attn_probs * (prob_grads - row_dots) * (1.0 - (capped / softcap) ** 2) * score_scale
-    ).astype(jnp.bfloat16)
-    grad_query = jnp.einsum(
-        "hqk,kd->qhd", grad_scores, key_sel, preferred_element_type=jnp.float32
-    )
-    grad_key_part = jnp.einsum(
-        "hqk,qhd->kd", grad_scores, query_heads, preferred_element_type=jnp.float32
-    )
-    grad_value_part = jnp.einsum(
-        "hqk,qhd->kd",
-        attn_probs.astype(jnp.bfloat16),
-        out_heads,
-        preferred_element_type=jnp.float32,
-    )
+    query_seg = jnp.take(segment_ids, query_pos)
+    attn_heads, grad_query_heads, grad_key_part, grad_value_part = attention_block(
+        queries.reshape(quarter_len, head_count, HD).transpose(1, 0, 2),
+        out_heads.transpose(1, 0, 2),
+        key_sel,
+        value_sel,
+        query_pos[:, None],
+        query_seg[:, None],
+        key_pos[None, :],
+        key_seg[None, :],
+    )
+    attn_out = attn_heads.transpose(1, 0, 2).reshape(quarter_len, part_w)
+    grad_query = grad_query_heads.transpose(1, 0, 2)
     cos_all, sin_all = rotary_tables(key_pos, HD)
     grad_key_rot = rotate_back(grad_key_part[:, None, :], cos_all, sin_all).reshape(
         win, kv_width

time: 441 us -> 416 us (0.943)
  matrix products: 46.7 us -> 19.2 us
  Pallas kernels: 19.1 us -> 24.3 us
    dot_general x6 -> x0, matrix products: 27.5 us -> none  [the longest x1 8.7 us: per_device(): jnp.einsum('hqk,qhd->kd', grad_scores, query_heads, preferred_element_typ...]
    pallas_call x0 -> x1, Pallas kernels: none -> 5.25 us  [attention_block(): pl.pallas_call(attention_kernel, grid=(heads,), in_specs=[pl.BlockSpec((1...]
    reshape x3 -> x1, local copies, waits for them, and re-layouts: 5.07 us -> 0.02 us  [per_device(): attn_out = attn_heads.transpose(1, 0, 2).reshape(quarter_len, part_w)]
    transpose x0 -> x2, local copies, waits for them, and re-layouts: none -> 4.86 us  [from_blocks(): return blocks.transpose(0, 2, 1, 3).reshape(n_row * rows, n_seq * w)]
  transfers between devices with their start and end apart: 5 -> 5, of which waited for: 4 -> 4; matrix products, arithmetic and copies ran while one was open for 6% -> 5% of each run, Pallas kernels for 0% -> 0%
where the time goes in v6:
time: 416 us; the launch traced here: 415 us
  waiting for transfers between devices  254 us (61%)
  blocking collectives  55.2 us (13%)
  other arithmetic  26.5 us (6%)
  Pallas kernels  24.3 us (6%)
  local copies, waits for them, and re-layouts  21.2 us (5%)
  matrix products  19.2 us (5%)
  between operations  14.3 us (3%)
    all_gather x1, waiting for transfers between devices, per_device(): lax.all_gather(jnp.concatenate([attn_out, grad_query_round, kv_grad_win,...  106 us
    reduce_scatter x1, waiting for transfers between devices, per_device(): lax.psum_scatter(blocks, ('row', 'seq'), scatter_dimension=0, tiled=True)  82.7 us
    all_gather x1, waiting for transfers between devices, per_device(): lax.all_gather(kv_piece, ('row', 'seq'), axis=0, tiled=True)  37.8 us
    all_gather x1, waiting for transfers between devices, per_device(): lax.all_gather(jnp.concatenate([embedded, out_grad], axis=1), 'col', axis...  28.2 us
    pallas_call x1, Pallas kernels, project_blocks(): pl.pallas_call(project_kernel, grid=(n_row, n_seq), in_specs=[pl.BlockSpe...  19.1 us
    psum x2, blocking collectives, per_device(): total_dot = lax.psum(lax.psum(own_dots, 'seq'), 'row')  18.9 us
    psum x1, blocking collectives, per_device(): col_terms = lax.psum(jnp.concatenate([gain_terms, dot_terms]), 'col')  14.8 us
    psum x1, blocking collectives, per_device(): lax.psum(lax.psum(jnp.sum(emb_all_f * emb_all_f, axis=1), 'seq'), 'row')  10.9 us
  transfers between devices with their start and end apart: 5, of which 4 were waited for; matrix products, arithmetic and copies ran while one was open for 5% of the time, Pallas kernels for 0%

profile of v6, /device:TPU:0, one launch (start us, length us, event | category | flops | bytes accessed | tf_op | source)
XLA Modules:
  0.0 415.4 jit_solution(7162672943492602190)
XLA Ops:
  7.3 0.9 compare_select_fusion.1
  8.1 0.7 compare_and_fusion
  8.9 2.2 gather_fusion
  11.0 1.0 gather_fusion.1
  12.0 0.1 add_convert_fusion.2
  12.2 0.8 pad_maximum_fusion.1
  13.1 0.8 multiply_convert_fusion.1.wkv_ref
  13.9 1.2 multiply_convert_fusion.wq_ref
  15.1 28.2 %all-gather.4.cloned.1.call-done.lhs_ref = bf16[1536,1024]{1,0:T(8,128)(2,1)} async-done(((bf16[192,1024]{1,0:T(8,128)(2,1)}), bf16[1536,1024]{1,0:T(8,128)(2,1)}) %all-gather.4.cloned.1.call-update) | async-done | bytes 3145744 | tf_op jit(solution)/shard_map/all_gather | solution.py:244
  43.4 19.1 %shard_map.162 = f32[6144,640]{1,0:T(8,128)} custom-call(bf16[1536,1024]{1,0:T(8,128)(2,1)} %all-gather.4.cloned.1.call-done.lhs_ref, bf16[512,1024]{1,0:T(8,128)(2,1)} %multiply_convert_fusion.wq_ref, bf16[512,256]{1,0:T(8,128)(2,1)} %multiply_convert_fusion.1.wkv_ref, bf16[1024,512]{1,0:T(8,128)(2,1)} %wo_ref.1), custom_call_target="tpu_custom_call" | custom-call | flops 4026531840 | bytes 21233664 | tf_op jit(solution)/shard_map/pallas_call | solution.py:99
  62.6 1.8 fusion.4
  64.4 10.6 %psum.35 = f32[1536]{0:T(1024)S(1)} all-reduce(f32[1536]{0:T(1024)S(1)} %fusion.4), channel_id=1, replica_groups=mesh['row'=4,'col'=8,'seq'=4] {'seq'}, use_global_device_ids=true, to_apply=%region_2.3 | all-reduce | flops 1536 | bytes 12288 | tf_op jit(solution)/shard_map/psum | solution.py:256
  75.0 10.9 %psum.36 = f32[1536]{0:T(1024)S(1)} all-reduce(f32[1536]{0:T(1024)S(1)} %psum.35), channel_id=1, replica_groups=mesh['row'=4,'col'=8,'seq'=4] {'row'}, use_global_device_ids=true, to_apply=%region_3.4 | all-reduce | flops 1536 | bytes 12288 | tf_op jit(solution)/shard_map/psum | solution.py:256
  86.0 82.7 %reduce-scatter.3.cloned.1.call-done = f32[384,640]{1,0:T(8,128)} async-done(((f32[6144,640]{1,0:T(8,128)}), f32[384,640]{1,0:T(8,128)}) %reduce-scatter.3.cloned.1.call-update) | async-done | bytes 983056 | tf_op jit(solution)/shard_map/reduce_scatter | solution.py:259
  168.6 1.1 fusion.43
  169.8 0.8 fusion.39
  170.6 1.7 fusion.45
  172.4 0.1 fusion.44
  172.6 2.5 gather_fusion.2
  175.4 0.8 multiply_cosine_fusion.2
  176.3 0.2 copy.57
  176.5 0.2 copy.80
  176.7 0.2 copy.81
  176.9 0.2 copy.60
  177.0 0.2 copy.61
  177.3 0.1 maximum_bitcast_fusion.1.q_ref
  177.4 37.8 %all-gather.6.cloned.1.call-done = bf16[6144,128]{1,0:T(8,128)(2,1)} async-done(((bf16[384,128]{1,0:T(8,128)(2,1)}), bf16[6144,128]{1,0:T(8,128)(2,1)}) %all-gather.6.cloned.1.call-update) | async-done | bytes 1572880 | tf_op jit(solution)/shard_map/all_gather | solution.py:274
  215.3 1.2 fusion.53
  216.6 5.3 %shard_map.163 = (bf16[2,384,128]{2,1,0:T(8,128)(2,1)S(1)}, f32[2,384,128]{2,1,0:T(8,128)S(1)}, f32[1152,128]{1,0:T(8,128)S(1)}, f32[1152,128]{1,0:T(8,128)S(1)}) custom-call(bf16[2,384,128]{2,1,0:T(8,128)(2,1)S(1)} %maximum_bitcast_fusion.1.q_ref, bf16[2,384,128]{2,1,0:T(8,128)(2,1)S(1)} %bitcast.81, ...), custom_call_target="tpu_custom_call" | custom-call | flops 1358954496 | bytes 3145728 | tf_op jit(solution)/shard_map/pallas_call | solution.py:170
  221.9 0.2 add_convert_fusion
  222.2 0.2 copy.67
  222.4 0.1 copy.69
  222.6 2.7 fusion.19
  225.3 0.2 maximum_bitcast_fusion
  225.5 1.3 maximum_maximum_fusion
  226.8 0.2 reduce-scatter.5.cloned.1.call-start
  227.0 105.5 %all-gather.8.cloned.1.call-done = bf16[30848,256]{1,0:T(8,128)(2,1)} async-done(((bf16[1928,256]{1,0:T(8,128)(2,1)}), bf16[30848,256]{1,0:T(8,128)(2,1)}) %all-gather.8.cloned.1.call-update) | async-done | bytes 15794192 | tf_op jit(solution)/shard_map/all_gather | solution.py:312
  332.6 5.7 %convert_reduce_fusion = f32[4,1152,256]{2,1,0:T(8,128)S(1)} fusion(bf16[16,1928,256]{2,1,0:T(8,128)(2,1)} %bitcast.82), kind=kLoop, calls=%fused_computation.3 | loop fusion | flops 8257536 | bytes 14155776 | tf_op jit(solution)/shard_map/reduce_sum | solution.py:328
  338.2 3.3 fusion.52
  341.7 0.2 fusion.22
  341.9 0.2 fusion.12
  342.1 0.3 fusion.10
  342.4 2.4 copy.72
  344.9 0.8 copy.86
  345.7 0.4 copy-done.10
  346.1 1.8 fusion.55
  348.0 2.4 copy.70
  350.4 0.8 copy.85
  351.2 0.4 copy-done.11
  351.6 2.0 convolution_convert_fusion
  353.7 0.6 convolution_add_fusion.1
  354.3 1.3 copy-done.3
  355.6 1.9 fusion.2
  357.4 2.1 pad_maximum_fusion
  359.6 14.8 %psum.37 = f32[2048]{0:T(1024)S(1)} all-reduce(f32[2048]{0:T(1024)S(1)} %pad_maximum_fusion.3), channel_id=1, replica_groups=mesh['row'=4,'col'=8,'seq'=4] {'col'}, use_global_device_ids=true, to_apply=%region_8.9 | all-reduce | flops 2048 | bytes 16384 | tf_op jit(solution)/shard_map/psum | solution.py:361
  374.5 0.6 slice.218
  375.1 10.4 %psum.38 = f32[192]{0:T(256)S(1)} all-reduce(f32[192]{0:T(256)S(1)} %dynamic_slice.23), channel_id=1, replica_groups=mesh['row'=4,'col'=8,'seq'=4] {'seq'}, use_global_device_ids=true, to_apply=%region_9.10 | all-reduce | flops 192 | bytes 1536 | tf_op jit(solution)/shard_map/psum | solution.py:364
  385.5 8.5 %psum.39 = f32[192]{0:T(256)S(1)} all-reduce(f32[192]{0:T(256)S(1)} %psum.38), channel_id=1, replica_groups=mesh['row'=4,'col'=8,'seq'=4] {'row'}, use_global_device_ids=true, to_apply=%region_10.11 | all-reduce | flops 192 | bytes 1536 | tf_op jit(solution)/shard_map/psum | solution.py:364
  394.1 3.2 fusion.28
  397.3 3.2 fusion.31
  400.5 3.1 fusion.7
  403.6 3.3 fusion.50
  406.9 1.1 convert_element_type.93
  408.0 0.9 fusion.25
  (71 shorter events, 1.7 us)
Async XLA Ops:
  7.2 3.9 copy-start
  7.2 5.0 %copy-start.13 = (bf16[192,512]{1,0:T(8,128)(2,1)S(1)}, bf16[192,512]{1,0:T(8,128)(2,1)}, u32[]{:S(2)}) copy-start(bf16[192,512]{1,0:T(8,128)(2,1)} %param.29) | copy-start | bytes 589828
  7.2 5.9 %copy-start.16 = (f32[512]{0:T(512)S(1)}, f32[512]{0:T(512)}, u32[]{:S(2)}) copy-start(f32[512]{0:T(512)} %param.24) | copy-start | bytes 6148
  7.2 5.9 %copy-start.14 = (bf16[512,128]{1,0:T(8,128)(2,1)S(1)}, bf16[512,128]{1,0:T(8,128)(2,1)}, u32[]{:S(2)}) copy-start(bf16[512,128]{1,0:T(8,128)(2,1)} %param.26) | copy-start | bytes 393220
  7.2 5.9 %copy-start.15 = (bf16[512,128]{1,0:T(8,128)(2,1)S(1)}, bf16[512,128]{1,0:T(8,128)(2,1)}, u32[]{:S(2)}) copy-start(bf16[512,128]{1,0:T(8,128)(2,1)} %param.27) | copy-start | bytes 393220
  7.2 6.7 %copy-start.9 = (bf16[512,1024]{1,0:T(8,128)(2,1)S(1)}, bf16[512,1024]{1,0:T(8,128)(2,1)}, u32[]{:S(2)}) copy-start(bf16[512,1024]{1,0:T(8,128)(2,1)} %param.25) | copy-start | bytes 3145732
  7.2 36.1 %all-gather.4.cloned.1.call-start = ((), (), s32[]{:S(2)}) async-start(), calls=%async_computation.2 | async-start | bytes 3538944 | tf_op jit(solution)/shard_map/all_gather | solution.py:244
  13.0 155.6 %reduce-scatter.3.cloned.1.call-start = ((), (), s32[]{:S(2)}) async-start(), calls=%async_computation.3 | async-start | bytes 16711680 | tf_op jit(solution)/shard_map/reduce_scatter | solution.py:259
  62.5 110.1 %copy-start.2 = (s32[1536]{0:T(1024)S(1)}, s32[1536]{0:T(1024)}, u32[]{:S(2)}) copy-start(s32[1536]{0:T(1024)} %param.21) | copy-start | bytes 18436
  62.5 152.8 %all-gather.6.cloned.1.call-start = ((), (), s32[]{:S(2)}) async-start(), calls=%async_computation.4 | async-start | bytes 1671168 | tf_op jit(solution)/shard_map/all_gather | solution.py:274
  168.6 7.5 %copy-start.12 = (f32[384,640]{1,0:T(8,128)S(1)}, f32[384,640]{1,0:T(8,128)}, u32[]{:S(2)}) copy-start(f32[384,640]{1,0:T(8,128)} %reduce-scatter.3.cloned.1.call-done) | copy-start | bytes 2949124
  172.4 160.2 %all-gather.8.cloned.1.call-start = ((), (), s32[]{:S(2)}) async-start(), calls=%async_computation.5 | async-start | bytes 16781312 | tf_op jit(solution)/shard_map/all_gather | solution.py:312
  226.8 180.1 %reduce-scatter.5.cloned.1.call-start = ((), (), s32[]{:S(2)}) async-start(), calls=%async_computation.6 | async-start | bytes 3538944 | tf_op jit(solution)/shard_map/reduce_scatter | solution.py:365
  344.9 1.2 copy-start.10
  345.7 2.3 copy-start.5
  350.4 1.2 copy-start.11
  351.2 2.5 copy-start.7
  353.7 1.9 copy-start.3
  394.0 6.4 %copy-start.8 = (bf16[192,8,4,256]{3,1,2,0:T(8,128)(2,1)S(1)}, bf16[192,8,4,256]{3,1,2,0:T(8,128)(2,1)}, u32[]{:S(2)}) copy-start(bf16[192,8,4,256]{3,1,2,0:T(8,128)(2,1)} %copy-done.7) | copy-start | bytes 9437188
  397.3 3.2 copy-start.4
  400.5 3.1 copy-start.6
  403.6 5.3 %copy-start.1 = (bf16[1024,512]{1,0:T(8,128)(2,1)S(1)}, bf16[1024,512]{1,0:T(8,128)(2,1)}, u32[]{:S(2)}) copy-start(bf16[1024,512]{1,0:T(8,128)(2,1)} %param.23) | copy-start | bytes 3145732
Sparse Core Ops, SparseCore 0:
  13.1 30.1 all-gather.3
  62.6 106.0 reduce-scatter.2
  172.5 42.7 all-gather.5
  226.9 105.5 all-gather.7
  359.7 35.6 reduce-scatter.4

commit v7 on v6

--- a/solution.py
+++ b/solution.py
@@ -317,10 +317,8 @@
         axis=0,
         tiled=True,
     ).reshape(n_rs, back_rows, part_w)
-    out_all = from_blocks(back_all[:, :quarter_len].reshape(n_row, n_seq, quarter_len, part_w))
-    grad_query_all = from_blocks(
-        back_all[:, quarter_len : 2 * quarter_len].reshape(n_row, n_seq, quarter_len, part_w)
-    )
+    out_blk = back_all[:, :quarter_len].reshape(n_row, n_seq, quarter_len, part_w)
+    gq_blk = back_all[:, quarter_len : 2 * quarter_len].reshape(n_row, n_seq, quarter_len, part_w)
     kv_terms = (
         back_all[:, 2 * quarter_len : 2 * quarter_len + win]
         .astype(jnp.float32)
@@ -334,10 +332,18 @@
     kv_grad_all = kv_grad_f.astype(jnp.bfloat16)
 
     normed_all = (emb_all_f * inv_all[:, None] * norm_gain[None, :]).astype(jnp.bfloat16)
-    grad_wo = jnp.einsum("ln,ld->nd", out_all, grad_all, preferred_element_type=jnp.float32)
+    grad_wo = jnp.einsum(
+        "rspn,rpd->snd",
+        out_blk,
+        grad_all.reshape(n_row, quarter_len, feat),
+        preferred_element_type=jnp.float32,
+    ).reshape(query_width, feat)
     grad_wq = jnp.einsum(
-        "ld,ln->dn", normed_all, grad_query_all, preferred_element_type=jnp.float32
-    )
+        "rpd,rspn->dsn",
+        normed_all.reshape(n_row, quarter_len, feat),
+        gq_blk,
+        preferred_element_type=jnp.float32,
+    ).reshape(feat, query_width)
     grad_wk = jnp.einsum(
         "ld,ln->dn", normed_all, kv_grad_all[:, :kv_width], preferred_element_type=jnp.float32
     )
@@ -345,10 +351,18 @@
         "ld,ln->dn", normed_all, kv_grad_all[:, kv_width:], preferred_element_type=jnp.float32
     )
 
-    branch_part = jnp.dot(out_all, w_out, preferred_element_type=jnp.float32)
+    branch_part = jnp.einsum(
+        "rspn,snd->rpd",
+        out_blk,
+        w_out.reshape(n_seq, part_w, feat),
+        preferred_element_type=jnp.float32,
+    ).reshape(seq_len, feat)
     total_term = jnp.einsum(
-        "ln,dn->ld", grad_query_all, w_query, preferred_element_type=jnp.float32
-    )
+        "rspn,dsn->rpd",
+        gq_blk,
+        w_query.reshape(feat, n_seq, part_w),
+        preferred_element_type=jnp.float32,
+    ).reshape(seq_len, feat)
     total_term = total_term + jnp.einsum(
         "ln,dn->ld", kv_grad_all[:, :kv_width], w_key, preferred_element_type=jnp.float32
     )

time: 416 us -> 420 us (level)
  local copies, waits for them, and re-layouts: 21.2 us -> 26 us
    reshape x0 -> x4, local copies, waits for them, and re-layouts: none -> 7.97 us  [the longest x2 4.93 us: per_device(): back_all[:, quarter_len:2 * quarter_len]]
    transpose x2 -> x0, local copies, waits for them, and re-layouts: 4.86 us -> none  [from_blocks(): return blocks.transpose(0, 2, 1, 3).reshape(n_row * rows, n_seq * w)]
  transfers between devices with their start and end apart: 5 -> 5, of which waited for: 4 -> 4; matrix products, arithmetic and copies ran while one was open for 5% -> 7% of each run, Pallas kernels for 0% -> 0%
where the time goes in v7:
time: 420 us; the launch traced here: 419 us
  waiting for transfers between devices  252 us (60%)
  blocking collectives  55.4 us (13%)
  other arithmetic  28.2 us (7%)
  local copies, waits for them, and re-layouts  26 us (6%)
  Pallas kernels  24.3 us (6%)
  matrix products  17.9 us (4%)
  between operations  14.4 us (3%)
    all_gather x1, waiting for transfers between devices, per_device(): lax.all_gather(jnp.concatenate([attn_out, grad_query_round, kv_grad_win,...  105 us
    reduce_scatter x1, waiting for transfers between devices, per_device(): lax.psum_scatter(blocks, ('row', 'seq'), scatter_dimension=0, tiled=True)  82.4 us
    all_gather x1, waiting for transfers between devices, per_device(): lax.all_gather(kv_piece, ('row', 'seq'), axis=0, tiled=True)  36.2 us
    all_gather x1, waiting for transfers between devices, per_device(): lax.all_gather(jnp.concatenate([embedded, out_grad], axis=1), 'col', axis...  28.2 us
    psum x2, blocking collectives, per_device(): total_dot = lax.psum(lax.psum(own_dots, 'seq'), 'row')  19.1 us
    pallas_call x1, Pallas kernels, project_blocks(): pl.pallas_call(project_kernel, grid=(n_row, n_seq), in_specs=[pl.BlockSpe...  19.1 us
    psum x1, blocking collectives, per_device(): col_terms = lax.psum(jnp.concatenate([gain_terms, dot_terms]), 'col')  14.9 us
    psum x1, blocking collectives, per_device(): lax.psum(lax.psum(jnp.sum(emb_all_f * emb_all_f, axis=1), 'seq'), 'row')  10.9 us
  transfers between devices with their start and end apart: 5, of which 4 were waited for; matrix products, arithmetic and copies ran while one was open for 7% of the time, Pallas kernels for 0%

profile of v7, /device:TPU:0, one launch (start us, length us, event | category | flops | bytes accessed | tf_op | source)
XLA Modules:
  0.0 419.1 jit_solution(3992233612363298589)
XLA Ops:
  7.2 0.8 compare_select_fusion.1
  8.0 0.7 compare_and_fusion
  8.8 2.2 gather_fusion
  11.0 1.0 gather_fusion.1
  12.1 0.8 pad_maximum_fusion.1
  13.0 0.8 multiply_convert_fusion.1.wkv_ref
  13.9 1.2 multiply_convert_fusion.wq_ref
  15.1 28.2 %all-gather.4.cloned.1.call-done.lhs_ref = bf16[1536,1024]{1,0:T(8,128)(2,1)} async-done(((bf16[192,1024]{1,0:T(8,128)(2,1)}), bf16[1536,1024]{1,0:T(8,128)(2,1)}) %all-gather.4.cloned.1.call-update) | async-done | bytes 3145744 | tf_op jit(solution)/shard_map/all_gather | solution.py:244
  43.3 19.1 %shard_map.162 = f32[6144,640]{1,0:T(8,128)} custom-call(bf16[1536,1024]{1,0:T(8,128)(2,1)} %all-gather.4.cloned.1.call-done.lhs_ref, bf16[512,1024]{1,0:T(8,128)(2,1)} %multiply_convert_fusion.wq_ref, bf16[512,256]{1,0:T(8,128)(2,1)} %multiply_convert_fusion.1.wkv_ref, bf16[1024,512]{1,0:T(8,128)(2,1)} %wo_ref.1), custom_call_target="tpu_custom_call" | custom-call | flops 4026531840 | bytes 21233664 | tf_op jit(solution)/shard_map/pallas_call | solution.py:99
  62.5 0.5 multiply_power_fusion
  63.0 0.6 add_convert_fusion.4
  63.6 0.7 copy-done.5
  64.3 0.4 fusion.4
  64.7 10.5 %psum.35 = f32[1536]{0:T(1024)S(1)} all-reduce(f32[1536]{0:T(1024)S(1)} %fusion.4), channel_id=1, replica_groups=mesh['row'=4,'col'=8,'seq'=4] {'seq'}, use_global_device_ids=true, to_apply=%region_2.3 | all-reduce | flops 1536 | bytes 12288 | tf_op jit(solution)/shard_map/psum | solution.py:256
  75.2 10.9 %psum.36 = f32[1536]{0:T(1024)S(1)} all-reduce(f32[1536]{0:T(1024)S(1)} %psum.35), channel_id=1, replica_groups=mesh['row'=4,'col'=8,'seq'=4] {'row'}, use_global_device_ids=true, to_apply=%region_3.4 | all-reduce | flops 1536 | bytes 12288 | tf_op jit(solution)/shard_map/psum | solution.py:256
  86.2 82.4 %reduce-scatter.3.cloned.1.call-done = f32[384,640]{1,0:T(8,128)} async-done(((f32[6144,640]{1,0:T(8,128)}), f32[384,640]{1,0:T(8,128)}) %reduce-scatter.3.cloned.1.call-update) | async-done | bytes 983056 | tf_op jit(solution)/shard_map/reduce_scatter | solution.py:259
  168.6 1.0 fusion.44
  169.6 1.5 fusion.40
  171.2 1.8 fusion.46
  173.2 2.5 gather_fusion.2
  176.0 0.8 multiply_cosine_fusion.2
  177.1 0.7 fusion.51
  177.8 1.1 copy.86
  178.9 0.2 copy.87
  179.1 0.2 copy.57
  179.3 0.2 copy.58
  179.7 36.2 %all-gather.6.cloned.1.call-done = bf16[6144,128]{1,0:T(8,128)(2,1)} async-done(((bf16[384,128]{1,0:T(8,128)(2,1)}), bf16[6144,128]{1,0:T(8,128)(2,1)}) %all-gather.6.cloned.1.call-update) | async-done | bytes 1572880 | tf_op jit(solution)/shard_map/all_gather | solution.py:274
  215.9 1.2 fusion.50
  217.3 5.2 %shard_map.163 = (bf16[2,384,128]{2,1,0:T(8,128)(2,1)S(1)}, f32[2,384,128]{2,1,0:T(8,128)S(1)}, f32[1152,128]{1,0:T(8,128)S(1)}, f32[1152,128]{1,0:T(8,128)S(1)}) custom-call(bf16[2,384,128]{2,1,0:T(8,128)(2,1)S(1)} %maximum_bitcast_fusion.1.q_ref, bf16[2,384,128]{2,1,0:T(8,128)(2,1)S(1)} %bitcast.103, ...), custom_call_target="tpu_custom_call" | custom-call | flops 1358954496 | bytes 3145728 | tf_op jit(solution)/shard_map/pallas_call | solution.py:170
  222.5 0.2 add_convert_fusion
  222.9 0.2 copy.64
  223.3 2.7 fusion.20
  226.1 1.3 maximum_maximum_fusion
  227.4 0.2 reduce-scatter.5.cloned.1.call-start
  227.7 105.5 %all-gather.8.cloned.1.call-done = bf16[30848,256]{1,0:T(8,128)(2,1)} async-done(((bf16[1928,256]{1,0:T(8,128)(2,1)}), bf16[30848,256]{1,0:T(8,128)(2,1)}) %all-gather.8.cloned.1.call-update) | async-done | bytes 15794192 | tf_op jit(solution)/shard_map/all_gather | solution.py:312
  333.2 5.7 %convert_reduce_fusion = f32[4,1152,256]{2,1,0:T(8,128)S(1)} fusion(bf16[16,1928,256]{2,1,0:T(8,128)(2,1)} %bitcast.108), kind=kLoop, calls=%fused_computation.3 | loop fusion | flops 8257536 | bytes 14155776 | tf_op jit(solution)/shard_map/reduce_sum | solution.py:326
  338.8 3.3 fusion.49
  342.5 0.2 fusion.11
  342.7 0.3 fusion.9
  343.1 0.7 copy-done.3
  343.8 0.2 copy.70
  344.0 0.2 copy.67
  344.3 1.0 copy-done.12
  345.3 1.9 convolution_bitcast_fusion
  347.2 0.6 convolution_add_fusion.1
  347.8 0.6 copy-done.13
  348.4 1.8 fusion.7
  350.3 3.3 fusion.2
  353.6 2.2 pad_maximum_fusion
  355.8 4.7 %copy.75 = bf16[4,4,384,256]{2,3,1,0:T(8,128)(2,1)} copy(bf16[4,4,384,256]{3,2,1,0:T(8,128)(2,1)} %bitcast.107) | data formatting | bytes 6291456 | tf_op jit(solution)/shard_map/reshape | solution.py:321
  360.5 0.7 pad_maximum_fusion.3
  361.2 14.9 %psum.37 = f32[2048]{0:T(1024)S(1)} all-reduce(f32[2048]{0:T(1024)S(1)} %pad_maximum_fusion.3), channel_id=1, replica_groups=mesh['row'=4,'col'=8,'seq'=4] {'col'}, use_global_device_ids=true, to_apply=%region_8.9 | all-reduce | flops 2048 | bytes 16384 | tf_op jit(solution)/shard_map/psum | solution.py:375
  376.1 0.6 slice.218
  376.7 2.8 copy.77
  379.6 10.4 %psum.38 = f32[192]{0:T(256)S(1)} all-reduce(f32[192]{0:T(256)S(1)} %dynamic_slice.23), channel_id=1, replica_groups=mesh['row'=4,'col'=8,'seq'=4] {'seq'}, use_global_device_ids=true, to_apply=%region_9.10 | all-reduce | flops 192 | bytes 1536 | tf_op jit(solution)/shard_map/psum | solution.py:378
  390.0 8.8 %psum.39 = f32[192]{0:T(256)S(1)} all-reduce(f32[192]{0:T(256)S(1)} %psum.38), channel_id=1, replica_groups=mesh['row'=4,'col'=8,'seq'=4] {'row'}, use_global_device_ids=true, to_apply=%region_10.11 | all-reduce | flops 192 | bytes 1536 | tf_op jit(solution)/shard_map/psum | solution.py:378
  398.7 0.8 fusion.48
  399.5 2.8 fusion.29
  402.3 1.3 fusion.32
  403.6 0.7 copy-done.9
  404.3 3.2 convolution_bitcast_fusion.3
  407.5 3.1 convolution_bitcast_fusion.2
  410.6 1.1 convert_element_type.93
  411.7 0.9 fusion.26
  (93 shorter events, 2.8 us)
Async XLA Ops:
  7.2 3.7 copy-start
  7.2 4.9 %copy-start.15 = (bf16[192,512]{1,0:T(8,128)(2,1)S(1)}, bf16[192,512]{1,0:T(8,128)(2,1)}, u32[]{:S(2)}) copy-start(bf16[192,512]{1,0:T(8,128)(2,1)} %param.29) | copy-start | bytes 589828
  7.2 36.1 %all-gather.4.cloned.1.call-start = ((), (), s32[]{:S(2)}) async-start(), calls=%async_computation.2 | async-start | bytes 3538944 | tf_op jit(solution)/shard_map/all_gather | solution.py:244
  10.9 2.1 copy-start.16
  10.9 2.1 copy-start.18
  10.9 2.1 copy-start.20
  11.0 2.9 copy-start.11
  13.0 155.6 %reduce-scatter.3.cloned.1.call-start = ((), (), s32[]{:S(2)}) async-start(), calls=%async_computation.3 | async-start | bytes 16711680 | tf_op jit(solution)/shard_map/reduce_scatter | solution.py:259
  62.4 1.9 copy-start.5
  62.4 110.8 %copy-start.2 = (s32[1536]{0:T(1024)S(1)}, s32[1536]{0:T(1024)}, u32[]{:S(2)}) copy-start(s32[1536]{0:T(1024)} %param.21) | copy-start | bytes 18436
  62.4 153.5 %all-gather.6.cloned.1.call-start = ((), (), s32[]{:S(2)}) async-start(), calls=%async_computation.4 | async-start | bytes 1671168 | tf_op jit(solution)/shard_map/all_gather | solution.py:274
  75.2 100.8 %copy-start.23 = (f32[384]{0:T(512)S(1)}, f32[384]{0:T(512)}, u32[]{:S(2)}) copy-start(f32[384]{0:T(512)} %add_convert_fusion.4) | copy-start | bytes 4612
  75.2 100.8 %copy-start.26 = (f32[64]{0:T(128)S(1)}, f32[64]{0:T(128)}, u32[]{:S(2)}) copy-start(f32[64]{0:T(128)} %multiply_power_fusion) | copy-start | bytes 772
  86.1 264.1 %copy-start.24 = (f32[1536]{0:T(1024)}, f32[1536]{0:T(1024)S(1)}, u32[]{:S(2)}) copy-start(f32[1536]{0:T(1024)S(1)} %add_rsqrt_fusion) | copy-start | bytes 18436
  171.2 5.6 %copy-start.14 = (f32[384,640]{1,0:T(8,128)S(1)}, f32[384,640]{1,0:T(8,128)}, u32[]{:S(2)}) copy-start(f32[384,640]{1,0:T(8,128)} %reduce-scatter.3.cloned.1.call-done) | copy-start | bytes 2949124
  173.0 160.2 %all-gather.8.cloned.1.call-start = ((), (), s32[]{:S(2)}) async-start(), calls=%async_computation.5 | async-start | bytes 16781312 | tf_op jit(solution)/shard_map/all_gather | solution.py:312
  227.4 183.1 %reduce-scatter.5.cloned.1.call-start = ((), (), s32[]{:S(2)}) async-start(), calls=%async_computation.6 | async-start | bytes 3538944 | tf_op jit(solution)/shard_map/reduce_scatter | solution.py:379
  342.1 1.7 copy-start.3
  343.1 7.1 %copy-start.7 = (bf16[1536,256]{1,0:T(8,128)(2,1)}, bf16[1536,256]{1,0:T(8,128)(2,1)S(1)}, u32[]{:S(2)}) copy-start(bf16[1536,256]{1,0:T(8,128)(2,1)S(1)} %convert_element_type.92) | copy-start | bytes 2359300
  344.0 1.2 copy-start.12
  345.2 1.9 copy-start.17
  347.2 1.2 copy-start.13
  348.4 1.9 copy-start.6
  348.4 1.9 copy-start.19
  348.4 1.9 copy-start.21
  355.7 4.7 %copy-start.25 = (f32[1536]{0:T(1024)S(1)}, f32[1536]{0:T(1024)}, u32[]{:S(2)}) copy-start(f32[1536]{0:T(1024)} %get-tuple-element.64) | copy-start | bytes 18436
  379.5 22.7 %copy-start.4 = (bf16[1536,512]{1,0:T(8,128)(2,1)S(1)}, bf16[1536,512]{1,0:T(8,128)(2,1)}, u32[]{:S(2)}) copy-start(bf16[1536,512]{1,0:T(8,128)(2,1)} %get-tuple-element.69) | copy-start | bytes 4718596
  379.5 22.7 %copy-start.8 = (bf16[1536,256]{1,0:T(8,128)(2,1)S(1)}, bf16[1536,256]{1,0:T(8,128)(2,1)}, u32[]{:S(2)}) copy-start(bf16[1536,256]{1,0:T(8,128)(2,1)} %copy-done.7) | copy-start | bytes 2359300
  402.3 2.0 copy-start.9
  404.3 3.2 slice-start
  404.3 3.2 copy-start.10
  407.5 4.2 copy-start.22
  407.5 5.1 %copy-start.1 = (bf16[1024,512]{1,0:T(8,128)(2,1)S(1)}, bf16[1024,512]{1,0:T(8,128)(2,1)}, u32[]{:S(2)}) copy-start(bf16[1024,512]{1,0:T(8,128)(2,1)} %param.23) | copy-start | bytes 3145732
Sparse Core Ops, SparseCore 0:
  13.1 30.1 all-gather.3
  62.5 106.0 reduce-scatter.2
  173.1 42.7 all-gather.5
  227.6 105.5 all-gather.7
  355.9 35.5 reduce-scatter.4

commit v8 on v6

--- a/solution.py
+++ b/solution.py
@@ -271,11 +271,13 @@
     )
     out_heads = d_raw.astype(jnp.bfloat16).reshape(quarter_len, head_count, HD)
 
-    kv_gath = lax.all_gather(kv_piece, ("row", "seq"), axis=0, tiled=True).reshape(
-        n_row, n_seq, quarter_len, HD
-    )
-    key_all = kv_gath[:, 0].reshape(seq_len, HD)
-    value_all = kv_gath[:, 1].reshape(seq_len, HD)
+    half_len = quarter_len // 2
+    kv_half = lax.dynamic_slice(kv_piece, ((seq_index // 2) * half_len, 0), (half_len, HD))
+    kv_gath = lax.all_gather(kv_half, ("row", "seq"), axis=0, tiled=True).reshape(
+        n_row, 2, 2, half_len, HD
+    )
+    key_all = kv_gath[:, :, 0].reshape(seq_len, HD)
+    value_all = kv_gath[:, :, 1].reshape(seq_len, HD)
 
     doc_back = -(-(MAX_DOC - 1) // quarter_len) * quarter_len
     win = min(seq_len, quarter_len + doc_back)

time: 416 us -> 398 us (0.957)
  waiting for transfers between devices: 254 us -> 211 us
  blocking collectives: 55.2 us -> 79.2 us
    all_gather x1 -> x0, waiting for transfers between devices: 37.8 us -> none  [per_device(): lax.all_gather(kv_piece, ('row', 'seq'), axis=0, tiled=True)]
    all_gather x0 -> x1, blocking collectives: none -> 23.3 us  [per_device(): lax.all_gather(kv_half, ('row', 'seq'), axis=0, tiled=True)]
    reduce_scatter x1, waiting for transfers between devices: 82.7 us -> 77.8 us  [per_device(): lax.psum_scatter(blocks, ('row', 'seq'), scatter_dimension=0, tiled=True)]
  transfers between devices with their start and end apart: 5 -> 4, of which waited for: 4 -> 3; matrix products, arithmetic and copies ran while one was open for 5% -> 5% of each run, Pallas kernels for 0% -> 0%
where the time goes in v8:
time: 398 us; the launch traced here: 397 us
  waiting for transfers between devices  211 us (53%)
  blocking collectives  79.2 us (20%)
  other arithmetic  26.8 us (7%)
  Pallas kernels  24.3 us (6%)
  local copies, waits for them, and re-layouts  21.5 us (5%)
  matrix products  19.2 us (5%)
  between operations  14.4 us (4%)
    all_gather x1, waiting for transfers between devices, per_device(): lax.all_gather(jnp.concatenate([attn_out, grad_query_round, kv_grad_win,...  105 us
    reduce_scatter x1, waiting for transfers between devices, per_device(): lax.psum_scatter(blocks, ('row', 'seq'), scatter_dimension=0, tiled=True)  77.8 us
    all_gather x1, waiting for transfers between devices, per_device(): lax.all_gather(jnp.concatenate([embedded, out_grad], axis=1), 'col', axis...  28.2 us
    all_gather x1, blocking collectives, per_device(): lax.all_gather(kv_half, ('row', 'seq'), axis=0, tiled=True)  23.3 us
    pallas_call x1, Pallas kernels, project_blocks(): pl.pallas_call(project_kernel, grid=(n_row, n_seq), in_specs=[pl.BlockSpe...  19.1 us
    psum x2, blocking collectives, per_device(): total_dot = lax.psum(lax.psum(own_dots, 'seq'), 'row')  18.9 us
    psum x1, blocking collectives, per_device(): col_terms = lax.psum(jnp.concatenate([gain_terms, dot_terms]), 'col')  14.8 us
    psum x1, blocking collectives, per_device(): lax.psum(jnp.sum(emb_all_f * emb_all_f, axis=1), 'seq')  11.1 us
  transfers between devices with their start and end apart: 4, of which 3 were waited for; matrix products, arithmetic and copies ran while one was open for 5% of the time, Pallas kernels for 0%

profile of v8, /device:TPU:0, one launch (start us, length us, event | category | flops | bytes accessed | tf_op | source)
XLA Modules:
  0.0 396.9 jit_solution(2298457761804006091)
XLA Ops:
  7.3 0.9 compare_select_fusion.1
  8.1 0.7 compare_and_fusion
  8.9 2.2 gather_fusion
  11.0 1.0 gather_fusion.1
  12.2 0.8 pad_maximum_fusion.1
  13.1 0.8 multiply_convert_fusion.1.wkv_ref
  13.9 1.2 multiply_convert_fusion.wq_ref
  15.1 28.2 %all-gather.3.cloned.1.call-done.lhs_ref = bf16[1536,1024]{1,0:T(8,128)(2,1)} async-done(((bf16[192,1024]{1,0:T(8,128)(2,1)}), bf16[1536,1024]{1,0:T(8,128)(2,1)}) %all-gather.3.cloned.1.call-update) | async-done | bytes 3145744 | tf_op jit(solution)/shard_map/all_gather | solution.py:244
  43.4 19.1 %shard_map.162 = f32[6144,640]{1,0:T(8,128)} custom-call(bf16[1536,1024]{1,0:T(8,128)(2,1)} %all-gather.3.cloned.1.call-done.lhs_ref, bf16[512,1024]{1,0:T(8,128)(2,1)} %multiply_convert_fusion.wq_ref, bf16[512,256]{1,0:T(8,128)(2,1)} %multiply_convert_fusion.1.wkv_ref, bf16[1024,512]{1,0:T(8,128)(2,1)} %wo_ref.1), custom_call_target="tpu_custom_call" | custom-call | flops 4026531840 | bytes 21233664 | tf_op jit(solution)/shard_map/pallas_call | solution.py:99
  62.6 0.1 fusion.42
  62.7 0.4 copy-done.2
  63.1 2.5 gather_fusion.2
  66.0 0.8 multiply_cosine_fusion.2
  66.7 1.8 fusion.4
  68.5 11.1 %psum.35 = f32[1536]{0:T(1024)S(1)} all-reduce(f32[1536]{0:T(1024)S(1)} %fusion.4), channel_id=1, replica_groups=mesh['row'=4,'col'=8,'seq'=4] {'seq'}, use_global_device_ids=true, to_apply=%region_2.3 | all-reduce | flops 1536 | bytes 12288 | tf_op jit(solution)/shard_map/psum | solution.py:256
  79.7 11.1 %psum.36 = f32[1536]{0:T(1024)S(1)} all-reduce(f32[1536]{0:T(1024)S(1)} %psum.35), channel_id=1, replica_groups=mesh['row'=4,'col'=8,'seq'=4] {'row'}, use_global_device_ids=true, to_apply=%region_3.4 | all-reduce | flops 1536 | bytes 12288 | tf_op jit(solution)/shard_map/psum | solution.py:256
  90.9 77.8 %reduce-scatter.3.cloned.1.call-done = f32[384,640]{1,0:T(8,128)} async-done(((f32[6144,640]{1,0:T(8,128)}), f32[384,640]{1,0:T(8,128)}) %reduce-scatter.3.cloned.1.call-update) | async-done | bytes 983056 | tf_op jit(solution)/shard_map/reduce_scatter | solution.py:259
  168.7 1.0 fusion.62
  169.7 0.8 fusion.39
  170.7 1.0 slice_multiply_fusion.2
  171.8 23.3 %all_gather.10 = bf16[3072,128]{1,0:T(8,128)(2,1)S(1)} all-gather(bf16[192,128]{1,0:T(8,128)(2,1)S(1)} %fusion.43), channel_id=1, replica_groups=mesh['row'=4,'col'=8,'seq'=4] {'row','seq'}, dimensions={0}, use_global_device_ids=true | all-gather | bytes 835584 | tf_op jit(solution)/shard_map/all_gather | solution.py:276
  195.3 1.1 slice_multiply_fusion.1
  196.4 0.2 copy.57
  196.6 0.2 copy.80
  196.8 0.2 copy.81
  197.0 1.0 slice.284
  198.0 0.2 copy.60
  198.2 0.2 copy.61
  198.6 5.2 %shard_map.163 = (bf16[2,384,128]{2,1,0:T(8,128)(2,1)S(1)}, f32[2,384,128]{2,1,0:T(8,128)S(1)}, f32[1152,128]{1,0:T(8,128)S(1)}, f32[1152,128]{1,0:T(8,128)S(1)}) custom-call(bf16[2,384,128]{2,1,0:T(8,128)(2,1)S(1)} %maximum_bitcast_fusion.1.q_ref, bf16[2,384,128]{2,1,0:T(8,128)(2,1)S(1)} %bitcast.79, ...), custom_call_target="tpu_custom_call" | custom-call | flops 1358954496 | bytes 3145728 | tf_op jit(solution)/shard_map/pallas_call | solution.py:170
  203.8 0.2 add_convert_fusion
  204.2 0.2 copy.67
  204.4 0.1 copy.69
  204.6 2.7 fusion.19
  207.3 0.2 maximum_bitcast_fusion
  207.5 1.3 maximum_maximum_fusion
  208.8 0.2 reduce-scatter.5.cloned.1.call-start
  209.0 105.0 %all-gather.5.cloned.1.call-done = bf16[30848,256]{1,0:T(8,128)(2,1)} async-done(((bf16[1928,256]{1,0:T(8,128)(2,1)}), bf16[30848,256]{1,0:T(8,128)(2,1)}) %all-gather.5.cloned.1.call-update) | async-done | bytes 15794192 | tf_op jit(solution)/shard_map/all_gather | solution.py:314
  314.0 5.7 %convert_reduce_fusion = f32[4,1152,256]{2,1,0:T(8,128)S(1)} fusion(bf16[16,1928,256]{2,1,0:T(8,128)(2,1)} %bitcast.80), kind=kLoop, calls=%fused_computation.3 | loop fusion | flops 8257536 | bytes 14155776 | tf_op jit(solution)/shard_map/reduce_sum | solution.py:330
  319.7 3.3 fusion.50
  323.1 0.2 fusion.22
  323.3 0.2 fusion.12
  323.5 0.3 fusion.10
  323.9 2.4 copy.72
  326.3 0.8 copy.86
  327.1 0.4 copy-done.10
  327.5 1.8 fusion.53
  329.4 2.4 copy.70
  331.8 0.8 copy.85
  332.6 0.4 copy-done.11
  333.1 2.0 convolution_convert_fusion
  335.1 0.6 convolution_add_fusion.1
  335.7 1.3 copy-done.3
  337.0 1.9 fusion.2
  338.9 2.1 pad_maximum_fusion
  341.0 14.8 %psum.37 = f32[2048]{0:T(1024)S(1)} all-reduce(f32[2048]{0:T(1024)S(1)} %pad_maximum_fusion.3), channel_id=1, replica_groups=mesh['row'=4,'col'=8,'seq'=4] {'col'}, use_global_device_ids=true, to_apply=%region_8.9 | all-reduce | flops 2048 | bytes 16384 | tf_op jit(solution)/shard_map/psum | solution.py:363
  355.9 0.6 slice.218
  356.5 10.4 %psum.38 = f32[192]{0:T(256)S(1)} all-reduce(f32[192]{0:T(256)S(1)} %dynamic_slice.27), channel_id=1, replica_groups=mesh['row'=4,'col'=8,'seq'=4] {'seq'}, use_global_device_ids=true, to_apply=%region_9.10 | all-reduce | flops 192 | bytes 1536 | tf_op jit(solution)/shard_map/psum | solution.py:366
  366.9 8.5 %psum.39 = f32[192]{0:T(256)S(1)} all-reduce(f32[192]{0:T(256)S(1)} %psum.38), channel_id=1, replica_groups=mesh['row'=4,'col'=8,'seq'=4] {'row'}, use_global_device_ids=true, to_apply=%region_10.11 | all-reduce | flops 192 | bytes 1536 | tf_op jit(solution)/shard_map/psum | solution.py:366
  375.5 3.2 fusion.28
  378.7 3.2 fusion.31
  381.9 3.1 fusion.7
  385.1 3.3 fusion.48
  388.4 1.1 convert_element_type.93
  389.5 0.9 fusion.25
  (79 shorter events, 2.0 us)
Async XLA Ops:
  7.2 3.9 copy-start
  7.2 5.0 %copy-start.12 = (bf16[192,512]{1,0:T(8,128)(2,1)S(1)}, bf16[192,512]{1,0:T(8,128)(2,1)}, u32[]{:S(2)}) copy-start(bf16[192,512]{1,0:T(8,128)(2,1)} %param.29) | copy-start | bytes 589828
  7.2 5.9 %copy-start.16 = (f32[512]{0:T(512)S(1)}, f32[512]{0:T(512)}, u32[]{:S(2)}) copy-start(f32[512]{0:T(512)} %param.24) | copy-start | bytes 6148
  7.2 5.9 %copy-start.13 = (bf16[512,128]{1,0:T(8,128)(2,1)S(1)}, bf16[512,128]{1,0:T(8,128)(2,1)}, u32[]{:S(2)}) copy-start(bf16[512,128]{1,0:T(8,128)(2,1)} %param.26) | copy-start | bytes 393220
  7.2 5.9 %copy-start.14 = (bf16[512,128]{1,0:T(8,128)(2,1)S(1)}, bf16[512,128]{1,0:T(8,128)(2,1)}, u32[]{:S(2)}) copy-start(bf16[512,128]{1,0:T(8,128)(2,1)} %param.27) | copy-start | bytes 393220
  7.2 6.7 %copy-start.9 = (bf16[512,1024]{1,0:T(8,128)(2,1)S(1)}, bf16[512,1024]{1,0:T(8,128)(2,1)}, u32[]{:S(2)}) copy-start(bf16[512,1024]{1,0:T(8,128)(2,1)} %param.25) | copy-start | bytes 3145732
  7.2 36.1 %all-gather.3.cloned.1.call-start = ((), (), s32[]{:S(2)}) async-start(), calls=%async_computation.2 | async-start | bytes 3538944 | tf_op jit(solution)/shard_map/all_gather | solution.py:244
  13.0 155.7 %reduce-scatter.3.cloned.1.call-start = ((), (), s32[]{:S(2)}) async-start(), calls=%async_computation.3 | async-start | bytes 16711680 | tf_op jit(solution)/shard_map/reduce_scatter | solution.py:259
  62.4 0.7 copy-start.2
  62.5 251.5 %all-gather.5.cloned.1.call-start = ((), (), s32[]{:S(2)}) async-start(), calls=%async_computation.4 | async-start | bytes 16781312 | tf_op jit(solution)/shard_map/all_gather | solution.py:314
  65.8 104.9 %copy-start.19 = (f32[64]{0:T(128)}, f32[64]{0:T(128)S(1)}, u32[]{:S(2)}) copy-start(f32[64]{0:T(128)S(1)} %multiply_power_fusion) | copy-start | bytes 772
  90.8 79.9 %copy-start.17 = (f32[1536]{0:T(1024)}, f32[1536]{0:T(1024)S(1)}, u32[]{:S(2)}) copy-start(f32[1536]{0:T(1024)S(1)} %add_rsqrt_fusion) | copy-start | bytes 18436
  203.8 0.8 copy-start.20
  208.8 179.6 %reduce-scatter.5.cloned.1.call-start = ((), (), s32[]{:S(2)}) async-start(), calls=%async_computation.5 | async-start | bytes 3538944 | tf_op jit(solution)/shard_map/reduce_scatter | solution.py:367
  326.3 1.2 copy-start.10
  327.1 2.3 copy-start.5
  331.8 1.2 copy-start.11
  332.6 2.5 copy-start.7
  335.1 1.9 copy-start.3
  335.1 1.9 copy-start.15
  335.1 1.9 copy-start.18
  375.5 6.4 %copy-start.8 = (bf16[192,8,4,256]{3,1,2,0:T(8,128)(2,1)S(1)}, bf16[192,8,4,256]{3,1,2,0:T(8,128)(2,1)}, u32[]{:S(2)}) copy-start(bf16[192,8,4,256]{3,1,2,0:T(8,128)(2,1)} %copy-done.7) | copy-start | bytes 9437188
  378.7 3.2 copy-start.4
  381.9 3.1 copy-start.6
  385.1 5.3 %copy-start.1 = (bf16[1024,512]{1,0:T(8,128)(2,1)S(1)}, bf16[1024,512]{1,0:T(8,128)(2,1)}, u32[]{:S(2)}) copy-start(bf16[1024,512]{1,0:T(8,128)(2,1)} %param.23) | copy-start | bytes 3145732
Sparse Core Ops, SparseCore 0:
  13.1 30.1 all-gather.2
  62.6 106.0 reduce-scatter.2
  208.9 105.0 all-gather.4
  341.1 35.6 reduce-scatter.4

commit v9 on v8

--- a/solution.py
+++ b/solution.py
@@ -78,14 +78,17 @@
     feat = wq_ref.shape[0]
     qw = wq_ref.shape[1]
     kw = wkv_ref.shape[1]
-    ow = wo_ref.shape[0]
-    emb = lhs_ref[:, :feat]
-    og = lhs_ref[:, feat:]
-    out_ref[:, :qw] = jnp.dot(emb, wq_ref[...], preferred_element_type=jnp.float32)
-    out_ref[:, qw : qw + kw] = jnp.dot(emb, wkv_ref[...], preferred_element_type=jnp.float32)
-    out_ref[:, qw + kw :] = lax.dot_general(
-        og, wo_ref[...], (((1,), (1,)), ((), ())), preferred_element_type=jnp.float32
-    )
+    n_row, _, rows, _ = out_ref.shape
+    for r in range(n_row):
+        emb = lhs_ref[r * rows : (r + 1) * rows, :feat]
+        og = lhs_ref[r * rows : (r + 1) * rows, feat:]
+        out_ref[r, 0, :, :qw] = jnp.dot(emb, wq_ref[...], preferred_element_type=jnp.float32)
+        out_ref[r, 0, :, qw : qw + kw] = jnp.dot(
+            emb, wkv_ref[...], preferred_element_type=jnp.float32
+        )
+        out_ref[r, 0, :, qw + kw :] = lax.dot_general(
+            og, wo_ref[...], (((1,), (1,)), ((), ())), preferred_element_type=jnp.float32
+        )
 
 
 def project_blocks(lhs, wq, wkv, wo, n_row, n_seq, out_w):
@@ -96,17 +99,18 @@
     ow = wo.shape[0] // n_seq
     rows = length // n_row
     flops = 2 * length * feat * (n_seq * (qw + kw + ow))
-    return pl.pallas_call(
+    out = pl.pallas_call(
         project_kernel,
-        grid=(n_row, n_seq),
+        grid=(n_seq,),
         in_specs=[
-            pl.BlockSpec((rows, lw), lambda r, s: (r, 0)),
-            pl.BlockSpec((feat, qw), lambda r, s: (0, s)),
-            pl.BlockSpec((feat, kw), lambda r, s: (0, s % 2)),
-            pl.BlockSpec((ow, feat), lambda r, s: (s, 0)),
-        ],
-        out_specs=pl.BlockSpec((rows, out_w), lambda r, s: (r * n_seq + s, 0)),
-        out_shape=jax.ShapeDtypeStruct((n_row * n_seq * rows, out_w), jnp.float32),
+            pl.BlockSpec((length, lw), lambda s: (0, 0)),
+            pl.BlockSpec((feat, qw), lambda s: (0, s)),
+            pl.BlockSpec((feat, kw), lambda s: (0, s % 2)),
+            pl.BlockSpec((ow, feat), lambda s: (s, 0)),
+        ],
+        out_specs=pl.BlockSpec((n_row, 1, rows, out_w), lambda s: (0, s, 0, 0)),
+        out_shape=jax.ShapeDtypeStruct((n_row, n_seq, rows, out_w), jnp.float32),
+        compiler_params=pltpu.CompilerParams(vmem_limit_bytes=48 * 1024 * 1024),
         cost_estimate=pl.CostEstimate(
             flops=flops,
             transcendentals=0,
@@ -114,6 +118,7 @@
             + n_row * n_seq * rows * out_w * 4,
         ),
     )(lhs, wq, wkv, wo)
+    return out.reshape(n_row * n_seq * rows, out_w)
 
 
 def attention_kernel(

time: 398 us -> 425 us (1.068)
  local copies, waits for them, and re-layouts: 21.5 us -> 59.7 us
  Pallas kernels: 24.3 us -> 13.4 us
    reshape x0 -> x1, local copies, waits for them, and re-layouts: none -> 15.6 us  [project_blocks(): return out.reshape(n_row * n_seq * rows, out_w)]
    pallas_call x1, Pallas kernels: 19.1 us -> 8.2 us  [project_blocks(): pl.pallas_call(project_kernel, grid=(n_seq,), in_specs=[pl.BlockSpec((len...]
    unnamed x46 -> x86, local copies, waits for them, and re-layouts: 4.54 us -> 12.7 us
where the time goes in v9:
time: 425 us; the launch traced here: 423 us
  waiting for transfers between devices  207 us (49%)
  blocking collectives  80.9 us (19%)
  local copies, waits for them, and re-layouts  59.7 us (14%)
  other arithmetic  30.3 us (7%)
  matrix products  17.2 us (4%)
  between operations  14.5 us (3%)
  Pallas kernels  13.4 us (3%)
    all_gather x1, waiting for transfers between devices, per_device(): lax.all_gather(jnp.concatenate([attn_out, grad_query_round, kv_grad_win,...  105 us
    reduce_scatter x1, waiting for transfers between devices, per_device(): lax.psum_scatter(blocks, ('row', 'seq'), scatter_dimension=0, tiled=True)  73.6 us
    all_gather x1, waiting for transfers between devices, per_device(): lax.all_gather(jnp.concatenate([embedded, out_grad], axis=1), 'col', axis...  28.7 us
    all_gather x1, blocking collectives, per_device(): lax.all_gather(kv_half, ('row', 'seq'), axis=0, tiled=True)  23.6 us
    psum x2, blocking collectives, per_device(): total_dot = lax.psum(lax.psum(own_dots, 'seq'), 'row')  18.9 us
    reshape x1, local copies, waits for them, and re-layouts, project_blocks(): return out.reshape(n_row * n_seq * rows, out_w)  15.6 us
    psum x1, blocking collectives, per_device(): col_terms = lax.psum(jnp.concatenate([gain_terms, dot_terms]), 'col')  14.8 us
    unnamed x86, local copies, waits for them, and re-layouts  12.7 us
  transfers between devices with their start and end apart: 4, of which 3 were waited for; matrix products, arithmetic and copies ran while one was open for 5% of the time, Pallas kernels for 0%

profile of v9, /device:TPU:0, one launch (start us, length us, event | category | flops | bytes accessed | tf_op | source)
XLA Modules:
  0.0 423.5 jit_solution(9570211421182076332)
XLA Ops:
  7.3 0.8 compare_select_fusion.1
  8.1 0.7 compare_and_fusion
  8.8 1.0 gather_fusion.1
  9.8 2.2 gather_fusion
  12.2 0.8 pad_maximum_fusion.1
  13.3 1.5 multiply_convert_fusion.wq_ref
  14.8 28.7 %all-gather.3.cloned.1.call-done.lhs_ref = bf16[1536,1024]{1,0:T(8,128)(2,1)} async-done(((bf16[192,1024]{1,0:T(8,128)(2,1)}), bf16[1536,1024]{1,0:T(8,128)(2,1)}) %all-gather.3.cloned.1.call-update) | async-done | bytes 3145744 | tf_op jit(solution)/shard_map/all_gather | solution.py:249
  43.4 1.9 copy-done.2
  45.3 8.2 %shard_map.162 = f32[4,4,384,640]{3,2,1,0:T(8,128)} custom-call(bf16[1536,1024]{1,0:T(8,128)(2,1)S(1)} %copy-done.2, bf16[512,1024]{1,0:T(8,128)(2,1)S(1)} %multiply_convert_fusion.wq_ref, bf16[512,256]{1,0:T(8,128)(2,1)S(1)} %multiply_convert_fusion.1.wkv_ref, bf16[1024,512]{1,0:T(8,128)(2,1)S(1)} %copy-done.6), custom_call_target="tpu_custom_call" | custom-call | flops 4026531840 | bytes 21233664 | tf_op jit(solution)/shard_map/pallas_call | solution.py:102
  53.5 15.6 %copy.66 = f32[6144,640]{0,1:T(8,128)} copy(f32[6144,640]{1,0:T(8,128)} %bitcast.77) | data formatting | bytes 31457280 | tf_op jit(solution)/shard_map/reshape | solution.py:121
  69.9 2.5 gather_fusion.2
  72.5 0.6 pad.17.clone
  73.1 0.6 add_convert_fusion.3
  73.9 1.5 multiply_cosine_fusion.1
  75.4 1.0 fusion.4
  76.4 11.5 %psum.35 = f32[1536]{0:T(1024)} all-reduce(f32[1536]{0:T(1024)} %fusion.4), channel_id=1, replica_groups=mesh['row'=4,'col'=8,'seq'=4] {'seq'}, use_global_device_ids=true, to_apply=%region_2.3 | all-reduce | flops 1536 | bytes 12288 | tf_op jit(solution)/shard_map/psum | solution.py:261
  87.9 12.1 %psum.36 = f32[1536]{0:T(1024)} all-reduce(f32[1536]{0:T(1024)} %psum.35), channel_id=1, replica_groups=mesh['row'=4,'col'=8,'seq'=4] {'row'}, use_global_device_ids=true, to_apply=%region_3.4 | all-reduce | flops 1536 | bytes 12288 | tf_op jit(solution)/shard_map/psum | solution.py:261
  99.9 0.7 add_rsqrt_fusion
  100.6 0.6 copy-done.37
  101.2 0.7 dynamic_slice.21
  101.9 73.6 %reduce-scatter.3.cloned.1.call-done = f32[384,640]{0,1:T(8,128)} async-done(((f32[6144,640]{0,1:T(8,128)}), f32[384,640]{0,1:T(8,128)}) %reduce-scatter.3.cloned.1.call-update) | async-done | bytes 983056 | tf_op jit(solution)/shard_map/reduce_scatter | solution.py:264
  175.5 1.0 slice_multiply_fusion.1
  176.5 0.8 fusion.52
  177.3 1.8 copy.87
  179.1 1.8 copy.86
  181.0 1.7 slice.284
  182.7 1.7 copy.69
  184.4 1.0 fusion.62
  185.4 1.1 fusion.40
  186.5 0.9 slice_multiply_fusion.2
  187.4 0.7 fusion.43
  188.2 1.6 copy.70
  189.8 23.6 %all_gather.10 = bf16[3072,128]{1,0:T(8,128)(2,1)S(1)} all-gather(bf16[192,128]{1,0:T(8,128)(2,1)} %copy.70), channel_id=1, replica_groups=mesh['row'=4,'col'=8,'seq'=4] {'row','seq'}, dimensions={0}, use_global_device_ids=true | all-gather | bytes 835584 | tf_op jit(solution)/shard_map/all_gather | solution.py:281
  213.9 5.2 %shard_map.163 = (bf16[2,384,128]{2,1,0:T(8,128)(2,1)S(1)}, f32[2,384,128]{2,1,0:T(8,128)S(1)}, f32[1152,128]{1,0:T(8,128)S(1)}, f32[1152,128]{1,0:T(8,128)S(1)}) custom-call(bf16[2,384,128]{2,1,0:T(8,128)(2,1)S(1)} %maximum_bitcast_fusion.1.q_ref, bf16[2,384,128]{2,1,0:T(8,128)(2,1)S(1)} %bitcast.76, ...), custom_call_target="tpu_custom_call" | custom-call | flops 1358954496 | bytes 3145728 | tf_op jit(solution)/shard_map/pallas_call | solution.py:175
  219.2 0.8 copy-done.5
  220.6 0.8 pad_maximum_fusion.2
  221.4 1.7 copy.73
  223.2 1.7 copy.75
  224.9 1.0 copy_bitcast_fusion
  225.9 4.0 fusion.19
  230.2 1.3 maximum_maximum_fusion
  231.7 104.9 %all-gather.5.cloned.1.call-done = bf16[30848,256]{1,0:T(8,128)(2,1)} async-done(((bf16[1928,256]{1,0:T(8,128)(2,1)}), bf16[30848,256]{1,0:T(8,128)(2,1)}) %all-gather.5.cloned.1.call-update) | async-done | bytes 15794192 | tf_op jit(solution)/shard_map/all_gather | solution.py:319
  336.6 6.2 %fusion.50 = (bf16[16,384,256]{2,1,0:T(8,128)(2,1)}, bf16[16,384,256]{2,1,0:T(8,128)(2,1)}) fusion(bf16[16,1928,256]{2,1,0:T(8,128)(2,1)} %bitcast.78), kind=kLoop, calls=%fused_computation.108 | loop fusion | bytes 12582912 | tf_op jit(solution)/shard_map/slice | solution.py:327
  342.8 5.7 %convert_reduce_fusion = f32[4,1152,256]{2,1,0:T(8,128)S(1)} fusion(bf16[16,1928,256]{2,1,0:T(8,128)(2,1)} %bitcast.79), kind=kLoop, calls=%fused_computation.3 | loop fusion | flops 8257536 | bytes 14155776 | tf_op jit(solution)/shard_map/reduce_sum | solution.py:335
  348.5 4.3 %copy.78 = bf16[4,384,4,256]{3,2,1,0:T(4,128)(2,1)S(1)} copy(bf16[4,384,4,256]{3,1,2,0:T(8,128)(2,1)} %bitcast.83) | data formatting | bytes 6291456 | tf_op jit(solution)/shard_map/transpose | solution.py:74
  352.8 0.8 copy.90
  354.0 1.8 fusion.53
  356.8 1.8 copy-done.11
  358.6 2.4 copy.76
  361.1 0.8 copy.89
  362.3 2.1 convolution_convert_fusion
  364.4 0.6 convolution_add_fusion.1
  365.3 1.9 fusion.2
  367.2 2.2 pad_maximum_fusion
  369.4 14.8 %psum.37 = f32[2048]{0:T(1024)S(1)} all-reduce(f32[2048]{0:T(1024)S(1)} %pad_maximum_fusion.3), channel_id=1, replica_groups=mesh['row'=4,'col'=8,'seq'=4] {'col'}, use_global_device_ids=true, to_apply=%region_8.9 | all-reduce | flops 2048 | bytes 16384 | tf_op jit(solution)/shard_map/psum | solution.py:368
  384.2 0.6 slice.218
  384.9 10.4 %psum.38 = f32[192]{0:T(256)S(1)} all-reduce(f32[192]{0:T(256)S(1)} %dynamic_slice.27), channel_id=1, replica_groups=mesh['row'=4,'col'=8,'seq'=4] {'seq'}, use_global_device_ids=true, to_apply=%region_9.10 | all-reduce | flops 192 | bytes 1536 | tf_op jit(solution)/shard_map/psum | solution.py:371
  395.3 8.5 %psum.39 = f32[192]{0:T(256)S(1)} all-reduce(f32[192]{0:T(256)S(1)} %psum.38), channel_id=1, replica_groups=mesh['row'=4,'col'=8,'seq'=4] {'row'}, use_global_device_ids=true, to_apply=%region_10.11 | all-reduce | flops 192 | bytes 1536 | tf_op jit(solution)/shard_map/psum | solution.py:371
  403.9 2.7 fusion.31
  406.6 1.6 fusion.28
  408.4 3.2 fusion.7
  411.6 3.3 fusion.48
  415.0 1.1 convert_element_type.93
  416.1 0.9 fusion.25
  (119 shorter events, 5.5 us)
Async XLA Ops:
  7.2 1.6 copy-start
  7.2 5.0 %copy-start.25 = (bf16[192,512]{1,0:T(8,128)(2,1)S(1)}, bf16[192,512]{1,0:T(8,128)(2,1)}, u32[]{:S(2)}) copy-start(bf16[192,512]{1,0:T(8,128)(2,1)} %param.29) | copy-start | bytes 589828
  7.2 5.9 %copy-start.33 = (f32[512]{0:T(512)S(1)}, f32[512]{0:T(512)}, u32[]{:S(2)}) copy-start(f32[512]{0:T(512)} %param.24) | copy-start | bytes 6148
  7.2 5.9 %copy-start.30 = (bf16[512,128]{1,0:T(8,128)(2,1)S(1)}, bf16[512,128]{1,0:T(8,128)(2,1)}, u32[]{:S(2)}) copy-start(bf16[512,128]{1,0:T(8,128)(2,1)} %param.27) | copy-start | bytes 393220
  7.2 5.9 %copy-start.28 = (bf16[512,128]{1,0:T(8,128)(2,1)S(1)}, bf16[512,128]{1,0:T(8,128)(2,1)}, u32[]{:S(2)}) copy-start(bf16[512,128]{1,0:T(8,128)(2,1)} %param.26) | copy-start | bytes 393220
  7.2 36.2 %all-gather.3.cloned.1.call-start = ((), (), s32[]{:S(2)}) async-start(), calls=%async_computation.2 | async-start | bytes 3538944 | tf_op jit(solution)/shard_map/all_gather | solution.py:249
  9.8 33.6 %copy-start.6 = (bf16[1024,512]{1,0:T(8,128)(2,1)S(1)}, bf16[1024,512]{1,0:T(8,128)(2,1)}, u32[]{:S(2)}) copy-start(bf16[1024,512]{1,0:T(8,128)(2,1)} %wo_ref.1) | copy-start | bytes 3145732
  12.2 0.8 copy-start.18
  13.1 162.4 %reduce-scatter.3.cloned.1.call-start = ((), (), s32[]{:S(2)}) async-start(), calls=%async_computation.3 | async-start | bytes 16711680 | tf_op jit(solution)/shard_map/reduce_scatter | solution.py:264
  43.4 1.9 copy-start.2
  69.2 0.7 copy-start.10
  69.2 6.2 %copy-start.3 = (bf16[1536,1024]{1,0:T(8,128)(2,1)S(1)}, bf16[1536,1024]{1,0:T(8,128)(2,1)}, u32[]{:S(2)}) copy-start(bf16[1536,1024]{1,0:T(8,128)(2,1)} %all-gather.3.cloned.1.call-done.lhs_ref) | copy-start | bytes 9437188
  69.2 267.5 %all-gather.5.cloned.1.call-start = ((), (), s32[]{:S(2)}) async-start(), calls=%async_computation.4 | async-start | bytes 16781312 | tf_op jit(solution)/shard_map/all_gather | solution.py:319
  73.1 0.8 copy-start.39
  73.1 0.8 copy-start.35
  100.6 0.6 copy-start.37
  189.7 23.9 %copy-start.16 = (f32[384,64]{1,0:T(8,128)S(1)}, f32[384,64]{1,0:T(8,128)}, u32[]{:S(2)}) copy-start(f32[384,64]{1,0:T(8,128)} %get-tuple-element.84) | copy-start | bytes 294916
  189.7 23.9 %copy-start.17 = (f32[384,64]{1,0:T(8,128)S(1)}, f32[384,64]{1,0:T(8,128)}, u32[]{:S(2)}) copy-start(f32[384,64]{1,0:T(8,128)} %get-tuple-element.85) | copy-start | bytes 294916
  189.7 23.9 %copy-start.22 = (f32[384,2,64]{2,0,1:T(8,128)S(1)}, f32[384,2,64]{2,0,1:T(8,128)}, u32[]{:S(2)}) copy-start(f32[384,2,64]{2,0,1:T(8,128)} %copy.87) | copy-start | bytes 589828
  189.8 23.9 %copy-start.23 = (f32[384,2,64]{2,0,1:T(8,128)S(1)}, f32[384,2,64]{2,0,1:T(8,128)}, u32[]{:S(2)}) copy-start(f32[384,2,64]{2,0,1:T(8,128)} %copy.86) | copy-start | bytes 589828
  189.8 24.1 %copy-start.8 = (bf16[384,2,128]{2,0,1:T(8,128)(2,1)S(1)}, bf16[384,2,128]{2,0,1:T(8,128)(2,1)}, u32[]{:S(2)}) copy-start(bf16[384,2,128]{2,0,1:T(8,128)(2,1)} %copy.69) | copy-start | bytes 589828
  219.2 0.8 copy-start.5
  220.0 0.7 copy-start.9
  220.0 6.0 %copy-start.32 = (f32[1152]{0:T(1024)S(1)}, f32[1152]{0:T(1024)}, u32[]{:S(2)}) copy-start(f32[1152]{0:T(1024)} %add_convert_fusion.3) | copy-start | bytes 13828
  220.0 6.0 %copy-start.40 = (f32[64]{0:T(128)S(1)}, f32[64]{0:T(128)}, u32[]{:S(2)}) copy-start(f32[64]{0:T(128)} %copy-done.39) | copy-start | bytes 772
  220.0 10.1 %copy-start.36 = (bf16[1928]{0:T(1024)(128)(2,1)S(1)}, bf16[1928]{0:T(1024)(128)(2,1)}, u32[]{:S(2)}) copy-start(bf16[1928]{0:T(1024)(128)(2,1)} %pad.17.clone) | copy-start | bytes 11572
  224.9 5.2 %copy-start.27 = (bf16[384,256]{1,0:T(8,128)(2,1)S(1)}, bf16[384,256]{1,0:T(8,128)(2,1)}, u32[]{:S(2)}) copy-start(bf16[384,256]{1,0:T(8,128)(2,1)} %copy.75) | copy-start | bytes 589828
  231.5 183.5 %reduce-scatter.5.cloned.1.call-start = ((), (), s32[]{:S(2)}) async-start(), calls=%async_computation.5 | async-start | bytes 3538944 | tf_op jit(solution)/shard_map/reduce_scatter | solution.py:372
  352.8 1.2 copy-start.24
  353.6 2.3 copy-start.12
  356.5 2.2 copy-start.11
  356.8 8.2 %copy-start.20 = (bf16[1536,256]{1,0:T(8,128)(2,1)}, bf16[1536,256]{1,0:T(8,128)(2,1)S(1)}, u32[]{:S(2)}) copy-start(bf16[1536,256]{1,0:T(8,128)(2,1)S(1)} %convert_element_type.92) | copy-start | bytes 2359300
  361.1 1.2 copy-start.7
  361.9 2.5 copy-start.14
  362.3 2.1 copy-start.29
  364.4 0.9 copy-start.31
  364.4 0.9 copy-start.34
  364.4 0.9 copy-start.38
  403.8 2.8 copy-start.21
  406.6 1.9 copy-start.15
  408.4 3.2 copy-start.4
  408.4 3.2 copy-start.13
  411.6 4.4 %copy-start.19 = (bf16[192,512]{1,0:T(8,128)(2,1)S(1)}, bf16[192,512]{1,0:T(8,128)(2,1)}, u32[]{:S(2)}) copy-start(bf16[192,512]{1,0:T(8,128)(2,1)} %copy-done.18) | copy-start | bytes 589828
  411.6 4.4 %copy-start.26 = (bf16[192,512]{1,0:T(8,128)(2,1)S(1)}, bf16[192,512]{1,0:T(8,128)(2,1)}, u32[]{:S(2)}) copy-start(bf16[192,512]{1,0:T(8,128)(2,1)} %param.29) | copy-start | bytes 589828
  411.6 5.3 %copy-start.1 = (bf16[1024,512]{1,0:T(8,128)(2,1)S(1)}, bf16[1024,512]{1,0:T(8,128)(2,1)}, u32[]{:S(2)}) copy-start(bf16[1024,512]{1,0:T(8,128)(2,1)} %param.23) | copy-start | bytes 3145732
Sparse Core Ops, SparseCore 0:
  13.2 30.1 all-gather.2
  69.3 106.1 reduce-scatter.2
  231.6 105.0 all-gather.4
  369.5 35.6 reduce-scatter.4

commit v10 on v9

--- a/solution.py
+++ b/solution.py
@@ -74,21 +74,29 @@
     return blocks.transpose(0, 2, 1, 3).reshape(n_row * rows, n_seq * w)
 
 
-def project_kernel(lhs_ref, wq_ref, wkv_ref, wo_ref, out_ref):
+def project_kernel(lhs_ref, wq_ref, wkv_ref, wo_ref, out_hbm, buf, sems):
+    part = pl.program_id(0)
+    n_part = pl.num_programs(0)
     feat = wq_ref.shape[0]
     qw = wq_ref.shape[1]
     kw = wkv_ref.shape[1]
-    n_row, _, rows, _ = out_ref.shape
+    n_row, rows, _ = buf.shape
+    copies = []
     for r in range(n_row):
         emb = lhs_ref[r * rows : (r + 1) * rows, :feat]
         og = lhs_ref[r * rows : (r + 1) * rows, feat:]
-        out_ref[r, 0, :, :qw] = jnp.dot(emb, wq_ref[...], preferred_element_type=jnp.float32)
-        out_ref[r, 0, :, qw : qw + kw] = jnp.dot(
-            emb, wkv_ref[...], preferred_element_type=jnp.float32
-        )
-        out_ref[r, 0, :, qw + kw :] = lax.dot_general(
+        buf[r, :, :qw] = jnp.dot(emb, wq_ref[...], preferred_element_type=jnp.float32)
+        buf[r, :, qw : qw + kw] = jnp.dot(emb, wkv_ref[...], preferred_element_type=jnp.float32)
+        buf[r, :, qw + kw :] = lax.dot_general(
             og, wo_ref[...], (((1,), (1,)), ((), ())), preferred_element_type=jnp.float32
         )
+        copy = pltpu.make_async_copy(
+            buf.at[r], out_hbm.at[pl.ds((r * n_part + part) * rows, rows)], sems.at[r]
+        )
+        copy.start()
+        copies.append(copy)
+    for copy in copies:
+        copy.wait()
 
 
 def project_blocks(lhs, wq, wkv, wo, n_row, n_seq, out_w):
@@ -99,7 +107,7 @@
     ow = wo.shape[0] // n_seq
     rows = length // n_row
     flops = 2 * length * feat * (n_seq * (qw + kw + ow))
-    out = pl.pallas_call(
+    return pl.pallas_call(
         project_kernel,
         grid=(n_seq,),
         in_specs=[
@@ -108,8 +116,12 @@
             pl.BlockSpec((feat, kw), lambda s: (0, s % 2)),
             pl.BlockSpec((ow, feat), lambda s: (s, 0)),
         ],
-        out_specs=pl.BlockSpec((n_row, 1, rows, out_w), lambda s: (0, s, 0, 0)),
-        out_shape=jax.ShapeDtypeStruct((n_row, n_seq, rows, out_w), jnp.float32),
+        out_specs=pl.BlockSpec(memory_space=pl.ANY),
+        out_shape=jax.ShapeDtypeStruct((n_row * n_seq * rows, out_w), jnp.float32),
+        scratch_shapes=[
+            pltpu.VMEM((n_row, rows, out_w), jnp.float32),
+            pltpu.SemaphoreType.DMA((n_row,)),
+        ],
         compiler_params=pltpu.CompilerParams(vmem_limit_bytes=48 * 1024 * 1024),
         cost_estimate=pl.CostEstimate(
             flops=flops,
@@ -118,7 +130,6 @@
             + n_row * n_seq * rows * out_w * 4,
         ),
     )(lhs, wq, wkv, wo)
-    return out.reshape(n_row * n_seq * rows, out_w)
 
 
 def attention_kernel(

time: 425 us -> 411 us (0.967)
  local copies, waits for them, and re-layouts: 59.7 us -> 40.2 us
    reshape x1 -> x0, local copies, waits for them, and re-layouts: 15.6 us -> none  [project_blocks(): return out.reshape(n_row * n_seq * rows, out_w)]
    unnamed x86 -> x76, local copies, waits for them, and re-layouts: 12.7 us -> 14.3 us
where the time goes in v10:
time: 411 us; the launch traced here: 409 us
  waiting for transfers between devices  211 us (51%)
  blocking collectives  79.4 us (19%)
  local copies, waits for them, and re-layouts  40.2 us (10%)
  other arithmetic  30.8 us (7%)
  matrix products  17.1 us (4%)
  Pallas kernels  15.6 us (4%)
  between operations  14.5 us (4%)
    all_gather x1, waiting for transfers between devices, per_device(): lax.all_gather(jnp.concatenate([attn_out, grad_query_round, kv_grad_win,...  105 us
    reduce_scatter x1, waiting for transfers between devices, per_device(): lax.psum_scatter(blocks, ('row', 'seq'), scatter_dimension=0, tiled=True)  77.8 us
    all_gather x1, waiting for transfers between devices, per_device(): lax.all_gather(jnp.concatenate([embedded, out_grad], axis=1), 'col', axis...  28.7 us
    all_gather x1, blocking collectives, per_device(): lax.all_gather(kv_half, ('row', 'seq'), axis=0, tiled=True)  23.5 us
    psum x2, blocking collectives, per_device(): total_dot = lax.psum(lax.psum(own_dots, 'seq'), 'row')  18.9 us
    psum x1, blocking collectives, per_device(): col_terms = lax.psum(jnp.concatenate([gain_terms, dot_terms]), 'col')  14.8 us
    unnamed x76, local copies, waits for them, and re-layouts  14.3 us
    psum x1, blocking collectives, per_device(): lax.psum(jnp.sum(emb_all_f * emb_all_f, axis=1), 'seq')  11.1 us
  transfers between devices with their start and end apart: 4, of which 3 were waited for; matrix products, arithmetic and copies ran while one was open for 5% of the time, Pallas kernels for 0%

profile of v10, /device:TPU:0, one launch (start us, length us, event | category | flops | bytes accessed | tf_op | source)
XLA Modules:
  0.0 409.5 jit_solution(4121354042640005861)
XLA Ops:
  7.3 0.8 compare_select_fusion.1
  8.1 0.7 compare_and_fusion
  8.8 2.2 gather_fusion
  11.0 1.0 gather_fusion.1
  12.2 0.8 pad_maximum_fusion.1
  13.2 1.5 multiply_convert_fusion.wq_ref
  14.7 28.7 %all-gather.3.cloned.1.call-done.lhs_ref = bf16[1536,1024]{1,0:T(8,128)(2,1)} async-done(((bf16[192,1024]{1,0:T(8,128)(2,1)}), bf16[1536,1024]{1,0:T(8,128)(2,1)}) %all-gather.3.cloned.1.call-update) | async-done | bytes 3145744 | tf_op jit(solution)/shard_map/all_gather | solution.py:260
  43.3 1.9 copy-done.2
  45.2 10.4 %shard_map.162 = f32[6144,640]{1,0:T(8,128)} custom-call(bf16[1536,1024]{1,0:T(8,128)(2,1)S(1)} %copy-done.2, bf16[512,1024]{1,0:T(8,128)(2,1)S(1)} %multiply_convert_fusion.wq_ref, bf16[512,256]{1,0:T(8,128)(2,1)S(1)} %multiply_convert_fusion.1.wkv_ref, bf16[1024,512]{1,0:T(8,128)(2,1)S(1)} %copy-done.6), custom_call_target="tpu_custom_call" | custom-call | flops 4026531840 | bytes 21233664 | tf_op jit(solution)/shard_map/pallas_call | solution.py:110
  56.4 2.5 gather_fusion.2
  59.0 0.8 reshape_select_fusion
  59.9 1.5 multiply_cosine_fusion.2
  61.7 11.1 %psum.35 = f32[1536]{0:T(1024)S(1)} all-reduce(f32[1536]{0:T(1024)S(1)} %fusion.4), channel_id=1, replica_groups=mesh['row'=4,'col'=8,'seq'=4] {'seq'}, use_global_device_ids=true, to_apply=%region_2.3 | all-reduce | flops 1536 | bytes 12288 | tf_op jit(solution)/shard_map/psum | solution.py:272
  72.9 11.1 %psum.36 = f32[1536]{0:T(1024)S(1)} all-reduce(f32[1536]{0:T(1024)S(1)} %psum.35), channel_id=1, replica_groups=mesh['row'=4,'col'=8,'seq'=4] {'row'}, use_global_device_ids=true, to_apply=%region_3.4 | all-reduce | flops 1536 | bytes 12288 | tf_op jit(solution)/shard_map/psum | solution.py:272
  84.1 77.8 %reduce-scatter.3.cloned.1.call-done = f32[384,640]{1,0:T(8,128)} async-done(((f32[6144,640]{1,0:T(8,128)}), f32[384,640]{1,0:T(8,128)}) %reduce-scatter.3.cloned.1.call-update) | async-done | bytes 983056 | tf_op jit(solution)/shard_map/reduce_scatter | solution.py:275
  161.9 1.0 fusion.62
  163.0 0.8 fusion.39
  163.9 1.0 slice_multiply_fusion.2
  165.0 23.5 %all_gather.10 = bf16[3072,128]{1,0:T(8,128)(2,1)S(1)} all-gather(bf16[192,128]{1,0:T(8,128)(2,1)S(1)} %fusion.43), channel_id=1, replica_groups=mesh['row'=4,'col'=8,'seq'=4] {'row','seq'}, dimensions={0}, use_global_device_ids=true | all-gather | bytes 835584 | tf_op jit(solution)/shard_map/all_gather | solution.py:292
  188.6 0.8 constant_dynamic-slice_fusion.1.k_ref
  189.5 1.9 slice_multiply_fusion.1
  191.3 1.9 copy.57
  193.2 1.8 fusion.52
  195.0 1.8 copy.80
  196.9 1.8 copy.81
  198.7 1.7 slice.284
  200.4 1.7 copy.60
  202.1 1.7 copy.61
  203.9 1.3 subtract_convert_fusion.1
  205.4 1.0 copy-done.9
  206.4 0.9 copy-done.10
  207.3 0.9 copy-done.11
  208.2 0.9 copy-done.13
  209.1 5.2 %shard_map.163 = (bf16[2,384,128]{2,1,0:T(8,128)(2,1)S(1)}, f32[2,384,128]{2,1,0:T(8,128)S(1)}, f32[1152,128]{1,0:T(8,128)S(1)}, f32[1152,128]{1,0:T(8,128)S(1)}) custom-call(bf16[2,384,128]{2,1,0:T(8,128)(2,1)S(1)} %maximum_bitcast_fusion.1.q_ref, bf16[2,384,128]{2,1,0:T(8,128)(2,1)S(1)} %bitcast.79, bf16[1152,128]{1,0:T(8,128)(2,1)S(1)} %copy-done.9, ...), custom_call_target="tpu_custom_call" | custom-call | flops 1358954496 | bytes 3145728 | tf_op jit(solution)/shard_map/pallas_call | solution.py:186
  214.4 0.8 copy-done.5
  215.4 0.6 copy-done.8
  216.5 1.1 convert.48
  217.6 1.0 copy_bitcast_fusion
  218.5 4.0 fusion.19
  222.8 1.3 maximum_maximum_fusion
  224.3 104.9 %all-gather.5.cloned.1.call-done = bf16[30848,256]{1,0:T(8,128)(2,1)} async-done(((bf16[1928,256]{1,0:T(8,128)(2,1)}), bf16[30848,256]{1,0:T(8,128)(2,1)}) %all-gather.5.cloned.1.call-update) | async-done | bytes 15794192 | tf_op jit(solution)/shard_map/all_gather | solution.py:330
  329.2 5.7 %convert_reduce_fusion = f32[4,1152,256]{2,1,0:T(8,128)S(1)} fusion(bf16[16,1928,256]{2,1,0:T(8,128)(2,1)} %bitcast.80), kind=kLoop, calls=%fused_computation.3 | loop fusion | flops 8257536 | bytes 14155776 | tf_op jit(solution)/shard_map/reduce_sum | solution.py:346
  334.9 3.3 fusion.50
  339.1 2.4 copy.72
  341.6 0.8 copy.86
  342.3 0.4 copy-done.25
  342.8 1.8 fusion.53
  344.6 2.4 copy.70
  347.1 0.8 copy.85
  347.9 0.4 copy-done.7
  348.3 2.1 convolution_convert_fusion
  350.4 0.6 convolution_add_fusion.1
  351.3 1.8 fusion.2
  353.1 2.2 pad_maximum_fusion
  355.4 14.8 %psum.37 = f32[2048]{0:T(1024)S(1)} all-reduce(f32[2048]{0:T(1024)S(1)} %pad_maximum_fusion.3), channel_id=1, replica_groups=mesh['row'=4,'col'=8,'seq'=4] {'col'}, use_global_device_ids=true, to_apply=%region_8.9 | all-reduce | flops 2048 | bytes 16384 | tf_op jit(solution)/shard_map/psum | solution.py:379
  370.2 0.6 slice.218
  370.9 10.4 %psum.38 = f32[192]{0:T(256)S(1)} all-reduce(f32[192]{0:T(256)S(1)} %dynamic_slice.27), channel_id=1, replica_groups=mesh['row'=4,'col'=8,'seq'=4] {'seq'}, use_global_device_ids=true, to_apply=%region_9.10 | all-reduce | flops 192 | bytes 1536 | tf_op jit(solution)/shard_map/psum | solution.py:382
  381.3 8.5 %psum.39 = f32[192]{0:T(256)S(1)} all-reduce(f32[192]{0:T(256)S(1)} %psum.38), channel_id=1, replica_groups=mesh['row'=4,'col'=8,'seq'=4] {'row'}, use_global_device_ids=true, to_apply=%region_10.11 | all-reduce | flops 192 | bytes 1536 | tf_op jit(solution)/shard_map/psum | solution.py:382
  389.8 2.7 fusion.28
  392.5 1.6 fusion.31
  394.4 3.2 fusion.7
  397.6 3.3 fusion.48
  401.0 1.1 convert_element_type.93
  402.1 0.9 fusion.25
  (109 shorter events, 4.9 us)
Async XLA Ops:
  7.2 3.8 copy-start
  7.2 5.0 %copy-start.26 = (bf16[192,512]{1,0:T(8,128)(2,1)S(1)}, bf16[192,512]{1,0:T(8,128)(2,1)}, u32[]{:S(2)}) copy-start(bf16[192,512]{1,0:T(8,128)(2,1)} %param.29) | copy-start | bytes 589828
  7.2 5.9 %copy-start.32 = (f32[512]{0:T(512)S(1)}, f32[512]{0:T(512)}, u32[]{:S(2)}) copy-start(f32[512]{0:T(512)} %param.24) | copy-start | bytes 6148
  7.2 5.9 %copy-start.28 = (bf16[512,128]{1,0:T(8,128)(2,1)S(1)}, bf16[512,128]{1,0:T(8,128)(2,1)}, u32[]{:S(2)}) copy-start(bf16[512,128]{1,0:T(8,128)(2,1)} %param.26) | copy-start | bytes 393220
  7.2 5.8 %copy-start.30 = (bf16[512,128]{1,0:T(8,128)(2,1)S(1)}, bf16[512,128]{1,0:T(8,128)(2,1)}, u32[]{:S(2)}) copy-start(bf16[512,128]{1,0:T(8,128)(2,1)} %param.27) | copy-start | bytes 393220
  7.2 36.1 %all-gather.3.cloned.1.call-start = ((), (), s32[]{:S(2)}) async-start(), calls=%async_computation.2 | async-start | bytes 3538944 | tf_op jit(solution)/shard_map/all_gather | solution.py:260
  11.0 32.4 %copy-start.6 = (bf16[1024,512]{1,0:T(8,128)(2,1)S(1)}, bf16[1024,512]{1,0:T(8,128)(2,1)}, u32[]{:S(2)}) copy-start(bf16[1024,512]{1,0:T(8,128)(2,1)} %wo_ref.1) | copy-start | bytes 3145732
  12.1 0.8 copy-start.21
  13.0 149.0 %reduce-scatter.3.cloned.1.call-start = ((), (), s32[]{:S(2)}) async-start(), calls=%async_computation.3 | async-start | bytes 16711680 | tf_op jit(solution)/shard_map/reduce_scatter | solution.py:275
  43.3 1.9 copy-start.2
  55.7 0.7 copy-start.14
  55.7 5.7 %copy-start.3 = (bf16[1536,1024]{1,0:T(8,128)(2,1)S(1)}, bf16[1536,1024]{1,0:T(8,128)(2,1)}, u32[]{:S(2)}) copy-start(bf16[1536,1024]{1,0:T(8,128)(2,1)} %all-gather.3.cloned.1.call-done.lhs_ref) | copy-start | bytes 9437188
  55.7 273.5 %all-gather.5.cloned.1.call-start = ((), (), s32[]{:S(2)}) async-start(), calls=%async_computation.4 | async-start | bytes 16781312 | tf_op jit(solution)/shard_map/all_gather | solution.py:330
  59.0 129.5 %copy-start.35 = (f32[64]{0:T(128)}, f32[64]{0:T(128)S(1)}, u32[]{:S(2)}) copy-start(f32[64]{0:T(128)S(1)} %multiply_power_fusion) | copy-start | bytes 772
  84.0 109.2 %copy-start.33 = (f32[1536]{0:T(1024)}, f32[1536]{0:T(1024)S(1)}, u32[]{:S(2)}) copy-start(f32[1536]{0:T(1024)S(1)} %add_rsqrt_fusion) | copy-start | bytes 18436
  205.2 10.0 %copy-start.19 = (f32[384,64]{1,0:T(8,128)S(1)}, f32[384,64]{1,0:T(8,128)}, u32[]{:S(2)}) copy-start(f32[384,64]{1,0:T(8,128)} %get-tuple-element.84) | copy-start | bytes 294916
  205.2 9.9 %copy-start.20 = (f32[384,64]{1,0:T(8,128)S(1)}, f32[384,64]{1,0:T(8,128)}, u32[]{:S(2)}) copy-start(f32[384,64]{1,0:T(8,128)} %get-tuple-element.85) | copy-start | bytes 294916
  205.4 1.0 copy-start.9
  206.4 0.9 copy-start.10
  207.3 0.9 copy-start.11
  208.2 0.9 copy-start.13
  214.3 0.8 copy-start.5
  215.2 0.8 copy-start.8
  215.2 0.9 copy-start.12
  224.1 176.9 %reduce-scatter.5.cloned.1.call-start = ((), (), s32[]{:S(2)}) async-start(), calls=%async_computation.5 | async-start | bytes 3538944 | tf_op jit(solution)/shard_map/reduce_scatter | solution.py:383
  339.1 11.9 %copy-start.23 = (bf16[1536,256]{1,0:T(8,128)(2,1)}, bf16[1536,256]{1,0:T(8,128)(2,1)S(1)}, u32[]{:S(2)}) copy-start(bf16[1536,256]{1,0:T(8,128)(2,1)S(1)} %convert_element_type.92) | copy-start | bytes 2359300
  341.6 1.2 copy-start.25
  342.3 2.3 copy-start.15
  347.1 1.2 copy-start.7
  347.9 2.5 copy-start.17
  348.3 2.1 copy-start.29
  350.4 0.9 copy-start.31
  350.4 0.9 copy-start.34
  389.8 2.8 copy-start.24
  392.5 1.9 copy-start.18
  394.4 3.2 copy-start.4
  394.4 3.2 copy-start.16
  397.6 4.4 %copy-start.22 = (bf16[192,512]{1,0:T(8,128)(2,1)S(1)}, bf16[192,512]{1,0:T(8,128)(2,1)}, u32[]{:S(2)}) copy-start(bf16[192,512]{1,0:T(8,128)(2,1)} %copy-done.21) | copy-start | bytes 589828
  397.6 4.4 %copy-start.27 = (bf16[192,512]{1,0:T(8,128)(2,1)S(1)}, bf16[192,512]{1,0:T(8,128)(2,1)}, u32[]{:S(2)}) copy-start(bf16[192,512]{1,0:T(8,128)(2,1)} %param.29) | copy-start | bytes 589828
  397.6 5.3 %copy-start.1 = (bf16[1024,512]{1,0:T(8,128)(2,1)S(1)}, bf16[1024,512]{1,0:T(8,128)(2,1)}, u32[]{:S(2)}) copy-start(bf16[1024,512]{1,0:T(8,128)(2,1)} %param.23) | copy-start | bytes 3145732
Sparse Core Ops, SparseCore 0:
  13.1 30.1 all-gather.2
  55.8 106.0 reduce-scatter.2
  224.2 105.0 all-gather.4
  355.5 35.6 reduce-scatter.4

commit v11 on v8

--- a/solution.py
+++ b/solution.py
@@ -98,14 +98,14 @@
     flops = 2 * length * feat * (n_seq * (qw + kw + ow))
     return pl.pallas_call(
         project_kernel,
-        grid=(n_row, n_seq),
+        grid=(n_seq, n_row),
         in_specs=[
-            pl.BlockSpec((rows, lw), lambda r, s: (r, 0)),
-            pl.BlockSpec((feat, qw), lambda r, s: (0, s)),
-            pl.BlockSpec((feat, kw), lambda r, s: (0, s % 2)),
-            pl.BlockSpec((ow, feat), lambda r, s: (s, 0)),
-        ],
-        out_specs=pl.BlockSpec((rows, out_w), lambda r, s: (r * n_seq + s, 0)),
+            pl.BlockSpec((rows, lw), lambda s, r: (r, 0)),
+            pl.BlockSpec((feat, qw), lambda s, r: (0, s)),
+            pl.BlockSpec((feat, kw), lambda s, r: (0, s % 2)),
+            pl.BlockSpec((ow, feat), lambda s, r: (s, 0)),
+        ],
+        out_specs=pl.BlockSpec((rows, out_w), lambda s, r: (r * n_seq + s, 0)),
         out_shape=jax.ShapeDtypeStruct((n_row * n_seq * rows, out_w), jnp.float32),
         cost_estimate=pl.CostEstimate(
             flops=flops,

time: 398 us -> 398 us (level)
  no operation moved by 1% of the time
where the time goes in v11:
time: 398 us; the launch traced here: 397 us
  waiting for transfers between devices  211 us (53%)
  blocking collectives  79.3 us (20%)
  other arithmetic  26.8 us (7%)
  Pallas kernels  24.5 us (6%)
  local copies, waits for them, and re-layouts  21.5 us (5%)
  matrix products  19.2 us (5%)
  between operations  14.4 us (4%)
    all_gather x1, waiting for transfers between devices, per_device(): lax.all_gather(jnp.concatenate([attn_out, grad_query_round, kv_grad_win,...  105 us
    reduce_scatter x1, waiting for transfers between devices, per_device(): lax.psum_scatter(blocks, ('row', 'seq'), scatter_dimension=0, tiled=True)  77.8 us
    all_gather x1, waiting for transfers between devices, per_device(): lax.all_gather(jnp.concatenate([embedded, out_grad], axis=1), 'col', axis...  28.2 us
    all_gather x1, blocking collectives, per_device(): lax.all_gather(kv_half, ('row', 'seq'), axis=0, tiled=True)  23.3 us
    pallas_call x1, Pallas kernels, project_blocks(): pl.pallas_call(project_kernel, grid=(n_seq, n_row), in_specs=[pl.BlockSpe...  19.3 us
    psum x2, blocking collectives, per_device(): total_dot = lax.psum(lax.psum(own_dots, 'seq'), 'row')  18.9 us
    psum x1, blocking collectives, per_device(): col_terms = lax.psum(jnp.concatenate([gain_terms, dot_terms]), 'col')  14.8 us
    psum x1, blocking collectives, per_device(): lax.psum(jnp.sum(emb_all_f * emb_all_f, axis=1), 'seq')  11.1 us
  transfers between devices with their start and end apart: 4, of which 3 were waited for; matrix products, arithmetic and copies ran while one was open for 5% of the time, Pallas kernels for 0%

profile of v11, /device:TPU:0, one launch (start us, length us, event | category | flops | bytes accessed | tf_op | source)
XLA Modules:
  0.0 397.2 jit_solution(14837740268488738457)
XLA Ops:
  7.3 0.9 compare_select_fusion.1
  8.1 0.7 compare_and_fusion
  8.9 2.2 gather_fusion
  11.0 1.0 gather_fusion.1
  12.2 0.8 pad_maximum_fusion.1
  13.1 0.8 multiply_convert_fusion.1.wkv_ref
  13.9 1.2 multiply_convert_fusion.wq_ref
  15.1 28.2 %all-gather.3.cloned.1.call-done.lhs_ref = bf16[1536,1024]{1,0:T(8,128)(2,1)} async-done(((bf16[192,1024]{1,0:T(8,128)(2,1)}), bf16[1536,1024]{1,0:T(8,128)(2,1)}) %all-gather.3.cloned.1.call-update) | async-done | bytes 3145744 | tf_op jit(solution)/shard_map/all_gather | solution.py:244
  43.4 19.3 %shard_map.162 = f32[6144,640]{1,0:T(8,128)} custom-call(bf16[1536,1024]{1,0:T(8,128)(2,1)} %all-gather.3.cloned.1.call-done.lhs_ref, bf16[512,1024]{1,0:T(8,128)(2,1)} %multiply_convert_fusion.wq_ref, bf16[512,256]{1,0:T(8,128)(2,1)} %multiply_convert_fusion.1.wkv_ref, bf16[1024,512]{1,0:T(8,128)(2,1)} %wo_ref.1), custom_call_target="tpu_custom_call" | custom-call | flops 4026531840 | bytes 21233664 | tf_op jit(solution)/shard_map/pallas_call | solution.py:99
  62.8 0.1 fusion.42
  63.0 0.4 copy-done.2
  63.4 2.5 gather_fusion.2
  66.2 0.8 multiply_cosine_fusion.2
  67.0 1.8 fusion.4
  68.8 11.1 %psum.35 = f32[1536]{0:T(1024)S(1)} all-reduce(f32[1536]{0:T(1024)S(1)} %fusion.4), channel_id=1, replica_groups=mesh['row'=4,'col'=8,'seq'=4] {'seq'}, use_global_device_ids=true, to_apply=%region_2.3 | all-reduce | flops 1536 | bytes 12288 | tf_op jit(solution)/shard_map/psum | solution.py:256
  79.9 11.1 %psum.36 = f32[1536]{0:T(1024)S(1)} all-reduce(f32[1536]{0:T(1024)S(1)} %psum.35), channel_id=1, replica_groups=mesh['row'=4,'col'=8,'seq'=4] {'row'}, use_global_device_ids=true, to_apply=%region_3.4 | all-reduce | flops 1536 | bytes 12288 | tf_op jit(solution)/shard_map/psum | solution.py:256
  91.1 77.8 %reduce-scatter.3.cloned.1.call-done = f32[384,640]{1,0:T(8,128)} async-done(((f32[6144,640]{1,0:T(8,128)}), f32[384,640]{1,0:T(8,128)}) %reduce-scatter.3.cloned.1.call-update) | async-done | bytes 983056 | tf_op jit(solution)/shard_map/reduce_scatter | solution.py:259
  168.9 1.0 fusion.62
  170.0 0.8 fusion.39
  170.9 1.0 slice_multiply_fusion.2
  172.0 23.3 %all_gather.10 = bf16[3072,128]{1,0:T(8,128)(2,1)S(1)} all-gather(bf16[192,128]{1,0:T(8,128)(2,1)S(1)} %fusion.43), channel_id=1, replica_groups=mesh['row'=4,'col'=8,'seq'=4] {'row','seq'}, dimensions={0}, use_global_device_ids=true | all-gather | bytes 835584 | tf_op jit(solution)/shard_map/all_gather | solution.py:276
  195.6 1.1 slice_multiply_fusion.1
  196.7 0.2 copy.57
  196.9 0.2 copy.80
  197.1 0.2 copy.81
  197.2 1.0 slice.284
  198.3 0.2 copy.60
  198.4 0.2 copy.61
  198.9 5.2 %shard_map.163 = (bf16[2,384,128]{2,1,0:T(8,128)(2,1)S(1)}, f32[2,384,128]{2,1,0:T(8,128)S(1)}, f32[1152,128]{1,0:T(8,128)S(1)}, f32[1152,128]{1,0:T(8,128)S(1)}) custom-call(bf16[2,384,128]{2,1,0:T(8,128)(2,1)S(1)} %maximum_bitcast_fusion.1.q_ref, bf16[2,384,128]{2,1,0:T(8,128)(2,1)S(1)} %bitcast.79, ...), custom_call_target="tpu_custom_call" | custom-call | flops 1358954496 | bytes 3145728 | tf_op jit(solution)/shard_map/pallas_call | solution.py:170
  204.1 0.2 add_convert_fusion
  204.5 0.2 copy.67
  204.6 0.1 copy.69
  204.9 2.7 fusion.19
  207.6 0.2 maximum_bitcast_fusion
  207.8 1.3 maximum_maximum_fusion
  209.0 0.2 reduce-scatter.5.cloned.1.call-start
  209.3 105.0 %all-gather.5.cloned.1.call-done = bf16[30848,256]{1,0:T(8,128)(2,1)} async-done(((bf16[1928,256]{1,0:T(8,128)(2,1)}), bf16[30848,256]{1,0:T(8,128)(2,1)}) %all-gather.5.cloned.1.call-update) | async-done | bytes 15794192 | tf_op jit(solution)/shard_map/all_gather | solution.py:314
  314.2 5.7 %convert_reduce_fusion = f32[4,1152,256]{2,1,0:T(8,128)S(1)} fusion(bf16[16,1928,256]{2,1,0:T(8,128)(2,1)} %bitcast.80), kind=kLoop, calls=%fused_computation.3 | loop fusion | flops 8257536 | bytes 14155776 | tf_op jit(solution)/shard_map/reduce_sum | solution.py:330
  319.9 3.3 fusion.50
  323.4 0.2 fusion.22
  323.5 0.2 fusion.12
  323.8 0.3 fusion.10
  324.1 2.4 copy.72
  326.6 0.8 copy.86
  327.4 0.4 copy-done.10
  327.8 1.8 fusion.53
  329.7 2.4 copy.70
  332.1 0.8 copy.85
  332.9 0.4 copy-done.11
  333.3 2.0 convolution_convert_fusion
  335.4 0.6 convolution_add_fusion.1
  336.0 1.3 copy-done.3
  337.3 1.9 fusion.2
  339.1 2.1 pad_maximum_fusion
  341.3 14.8 %psum.37 = f32[2048]{0:T(1024)S(1)} all-reduce(f32[2048]{0:T(1024)S(1)} %pad_maximum_fusion.3), channel_id=1, replica_groups=mesh['row'=4,'col'=8,'seq'=4] {'col'}, use_global_device_ids=true, to_apply=%region_8.9 | all-reduce | flops 2048 | bytes 16384 | tf_op jit(solution)/shard_map/psum | solution.py:363
  356.1 0.6 slice.218
  356.8 10.4 %psum.38 = f32[192]{0:T(256)S(1)} all-reduce(f32[192]{0:T(256)S(1)} %dynamic_slice.27), channel_id=1, replica_groups=mesh['row'=4,'col'=8,'seq'=4] {'seq'}, use_global_device_ids=true, to_apply=%region_9.10 | all-reduce | flops 192 | bytes 1536 | tf_op jit(solution)/shard_map/psum | solution.py:366
  367.2 8.5 %psum.39 = f32[192]{0:T(256)S(1)} all-reduce(f32[192]{0:T(256)S(1)} %psum.38), channel_id=1, replica_groups=mesh['row'=4,'col'=8,'seq'=4] {'row'}, use_global_device_ids=true, to_apply=%region_10.11 | all-reduce | flops 192 | bytes 1536 | tf_op jit(solution)/shard_map/psum | solution.py:366
  375.8 3.2 fusion.28
  379.0 3.2 fusion.31
  382.2 3.1 fusion.7
  385.3 3.3 fusion.48
  388.7 1.1 convert_element_type.93
  389.7 0.9 fusion.25
  (79 shorter events, 2.0 us)
Async XLA Ops:
  7.2 3.9 copy-start
  7.2 5.0 %copy-start.12 = (bf16[192,512]{1,0:T(8,128)(2,1)S(1)}, bf16[192,512]{1,0:T(8,128)(2,1)}, u32[]{:S(2)}) copy-start(bf16[192,512]{1,0:T(8,128)(2,1)} %param.29) | copy-start | bytes 589828
  7.2 5.9 %copy-start.16 = (f32[512]{0:T(512)S(1)}, f32[512]{0:T(512)}, u32[]{:S(2)}) copy-start(f32[512]{0:T(512)} %param.24) | copy-start | bytes 6148
  7.2 5.9 %copy-start.13 = (bf16[512,128]{1,0:T(8,128)(2,1)S(1)}, bf16[512,128]{1,0:T(8,128)(2,1)}, u32[]{:S(2)}) copy-start(bf16[512,128]{1,0:T(8,128)(2,1)} %param.26) | copy-start | bytes 393220
  7.2 5.9 %copy-start.14 = (bf16[512,128]{1,0:T(8,128)(2,1)S(1)}, bf16[512,128]{1,0:T(8,128)(2,1)}, u32[]{:S(2)}) copy-start(bf16[512,128]{1,0:T(8,128)(2,1)} %param.27) | copy-start | bytes 393220
  7.2 6.7 %copy-start.9 = (bf16[512,1024]{1,0:T(8,128)(2,1)S(1)}, bf16[512,1024]{1,0:T(8,128)(2,1)}, u32[]{:S(2)}) copy-start(bf16[512,1024]{1,0:T(8,128)(2,1)} %param.25) | copy-start | bytes 3145732
  7.2 36.1 %all-gather.3.cloned.1.call-start = ((), (), s32[]{:S(2)}) async-start(), calls=%async_computation.2 | async-start | bytes 3538944 | tf_op jit(solution)/shard_map/all_gather | solution.py:244
  13.0 155.9 %reduce-scatter.3.cloned.1.call-start = ((), (), s32[]{:S(2)}) async-start(), calls=%async_computation.3 | async-start | bytes 16711680 | tf_op jit(solution)/shard_map/reduce_scatter | solution.py:259
  62.7 0.7 copy-start.2
  62.7 251.5 %all-gather.5.cloned.1.call-start = ((), (), s32[]{:S(2)}) async-start(), calls=%async_computation.4 | async-start | bytes 16781312 | tf_op jit(solution)/shard_map/all_gather | solution.py:314
  66.0 104.9 %copy-start.19 = (f32[64]{0:T(128)}, f32[64]{0:T(128)S(1)}, u32[]{:S(2)}) copy-start(f32[64]{0:T(128)S(1)} %multiply_power_fusion) | copy-start | bytes 772
  91.0 79.9 %copy-start.17 = (f32[1536]{0:T(1024)}, f32[1536]{0:T(1024)S(1)}, u32[]{:S(2)}) copy-start(f32[1536]{0:T(1024)S(1)} %add_rsqrt_fusion) | copy-start | bytes 18436
  204.1 0.8 copy-start.20
  209.0 179.6 %reduce-scatter.5.cloned.1.call-start = ((), (), s32[]{:S(2)}) async-start(), calls=%async_computation.5 | async-start | bytes 3538944 | tf_op jit(solution)/shard_map/reduce_scatter | solution.py:367
  326.6 1.2 copy-start.10
  327.3 2.3 copy-start.5
  332.1 1.2 copy-start.11
  332.9 2.5 copy-start.7
  335.4 1.9 copy-start.3
  335.4 1.9 copy-start.15
  335.4 1.9 copy-start.18
  375.8 6.4 %copy-start.8 = (bf16[192,8,4,256]{3,1,2,0:T(8,128)(2,1)S(1)}, bf16[192,8,4,256]{3,1,2,0:T(8,128)(2,1)}, u32[]{:S(2)}) copy-start(bf16[192,8,4,256]{3,1,2,0:T(8,128)(2,1)} %copy-done.7) | copy-start | bytes 9437188
  379.0 3.2 copy-start.4
  382.2 3.1 copy-start.6
  385.3 5.3 %copy-start.1 = (bf16[1024,512]{1,0:T(8,128)(2,1)S(1)}, bf16[1024,512]{1,0:T(8,128)(2,1)}, u32[]{:S(2)}) copy-start(bf16[1024,512]{1,0:T(8,128)(2,1)} %param.23) | copy-start | bytes 3145732
Sparse Core Ops, SparseCore 0:
  13.1 30.1 all-gather.2
  62.8 106.0 reduce-scatter.2
  209.2 105.0 all-gather.4
  341.4 35.6 reduce-scatter.4
